TPU v7x, 32 devices: a whole 2x2x4 slice. The times are simulated.
32 devices in a mesh: groups: 2 (over y), tile: 16 (over z, x, core).
Axes of the slice: x: 2, y: 2, z: 4, core: 2. Of those that a mesh axis runs over, the one named last changes fastest.
Arguments:
- log_demand: float32 [512, 256], P(('groups', 'tile')), parts along dimension 0, may hold values from -3 to 0
- log_capacity: float32 [32, 256], P(('groups', 'tile')), parts along dimension 0, may hold values from -1 to 1
- warm_potential: float32 [32, 256], P(('groups', 'tile')), parts along dimension 0, may hold values from -4 to 4
- facility_xy: float32 [32, 2, 256], P('groups'), parts along dimension 0, may hold values from 0 to 1472
- pair_block: int32 [512, 16], P(('groups', 'tile')), parts along dimension 0, may hold values from 0 to 15, as said below
- pair_count: int32 [512], P(('groups', 'tile')), parts along dimension 0, may hold values from 1 to 16, as said below
Outputs:
- cell_potential: float32 [512, 256], P(('groups', 'tile')), parts along dimension 0
- facility_potential: float32 [32, 256], P(('groups', 'tile')), parts along dimension 0
There are 2 independent parts, one for each index of `groups`. A program takes and returns all parts, laid end to end along the dimension named above; each array names one. Nothing has to cross between parts.
Inputs may be any that keep to these rules, and one draw needn't show every extreme that they name: `pair_count`: every tile has at least one active pair and some tile has 16. `pair_block`: the 16 slots of a tile name distinct blocks; slot 0 is the block of the tile's own tile row (block b belongs to tile row b); every slot's block b satisfies |b - floor(t / 16)| <= 16 for its tile t; slots at or beyond the tile's pair_count are ignored.
All inputs are finite; a program needn't handle non-finite values.
Results may differ from a plain program's by a relative error of at most 0.0003.
Values sent between devices are 32-bit elements; how exact they have to be, the bound alone decides.
No kernel may reach another device: no remote copies, remote signals or barrier semaphores. Data moves between devices by JAX's collectives and lax.ppermute only.
A program may use at most 64 MiB of HBM per device.

v0:
```python
import jax
import jax.numpy as jnp
from jax import lax
from jax.sharding import PartitionSpec as P

TSIDE = 16
TILE_COLS = 16
KSLOTS = 16
ITERS = 2
REACH = 64
SPAN = 16


LOWEST = -1e30


def from_behind(block, axis, distance):
    devices = range(lax.axis_size(axis))
    route = [(i - distance, i) for i in devices if i - distance in devices]
    return lax.ppermute(block, axis, route)


def cell_coords(tile_index):
    cell_ids = jnp.arange(TSIDE * TSIDE, dtype=jnp.int32)
    column = tile_index % TILE_COLS * TSIDE + cell_ids % TSIDE
    row_cell = tile_index // TILE_COLS * TSIDE + cell_ids // TSIDE
    return (column.astype(jnp.float32) + 0.5, row_cell.astype(jnp.float32) + 0.5)


def pair_cost(coord_x, coord_y, positions):
    delta_x = coord_x[None, :, None] - positions[:, 0, :][:, None, :]
    delta_y = coord_y[None, :, None] - positions[:, 1, :][:, None, :]
    return (delta_x * delta_x + delta_y * delta_y) / float(REACH * REACH)


def tile_pass(tile_index, demand_row, potentials, positions, active):
    coord_x, coord_y = cell_coords(tile_index)
    pair_costs = pair_cost(coord_x, coord_y, positions)
    scores = jnp.where(active[:, None, None], potentials[:, None, :] - pair_costs, LOWEST)
    row_top = jnp.max(scores, axis=(0, 2))
    row_sum = jnp.sum(jnp.exp(scores - row_top[None, :, None]), axis=(0, 2))
    cell_pot = demand_row - (row_top + jnp.log(row_sum))
    column_scores = cell_pot[None, :, None] - pair_costs
    col_top = jnp.max(column_scores, axis=1)
    col_sum = jnp.sum(jnp.exp(column_scores - col_top[:, None, :]), axis=1)
    col_top = jnp.where(active[:, None], col_top, LOWEST)
    col_sum = jnp.where(active[:, None], col_sum, 0.0)
    return (cell_pot, col_top, col_sum)


def merge_parts(top_a, sum_a, top_b, sum_b):
    top_new = jnp.maximum(top_a, top_b)
    return (top_new, sum_a * jnp.exp(top_a - top_new) + sum_b * jnp.exp(top_b - top_new))


def on_device(log_demand, log_capacity, warm_potential, facility_xy, pair_block, pair_count):
    tiles_here = log_demand.shape[0]
    blocks_here = log_capacity.shape[0]
    block_width = log_capacity.shape[1]
    devices_along = lax.axis_size("tile")
    my_index = lax.axis_index("tile")
    reach = min(devices_along - 1, (SPAN + blocks_here - 1) // blocks_here)
    window = 2 * reach + 1
    tile_ids = my_index * tiles_here + jnp.arange(tiles_here, dtype=jnp.int32)
    slot_ids = jnp.arange(KSLOTS, dtype=jnp.int32)
    first_block = (my_index - reach) * blocks_here
    local_block = pair_block - first_block
    facility_pot = warm_potential
    cell_pot = log_demand
    for step_index in range(ITERS):
        slabs = []
        for position in range(window):
            distance = reach - position
            if distance == 0:
                slabs.append(facility_pot)
            else:
                slabs.append(from_behind(facility_pot, "tile", distance))
        window_pot = jnp.concatenate(slabs, axis=0)

        def one_tile(inputs):
            tile_index, demand_row, blocks, nearby, slot_limit = inputs
            active = slot_ids < slot_limit
            return tile_pass(
                tile_index, demand_row, window_pot[nearby], facility_xy[blocks], active
            )

        cell_pot, col_top, col_sum = lax.map(
            one_tile, (tile_ids, log_demand, pair_block, local_block, pair_count)
        )
        flat_ids = local_block.reshape(-1)
        flat_top = col_top.reshape(-1, block_width)
        flat_sum = col_sum.reshape(-1, block_width)
        local_top = (
            jnp.full((window * blocks_here, block_width), LOWEST, jnp.float32)
            .at[flat_ids]
            .max(flat_top)
        )
        local_sum = (
            jnp.zeros((window * blocks_here, block_width), jnp.float32)
            .at[flat_ids]
            .add(flat_sum * jnp.exp(flat_top - local_top[flat_ids]))
        )

        def slab_of(position):
            return (
                local_top[position * blocks_here : (position + 1) * blocks_here],
                local_sum[position * blocks_here : (position + 1) * blocks_here],
            )

        own_top, block_sum = slab_of(reach)
        for distance in range(-reach, reach + 1):
            if distance != 0:
                send_top, send_sum = slab_of(reach + distance)
                got_top, got_sum = from_behind((send_top, send_sum), "tile", distance)
                source = my_index - distance
                valid = (source >= 0) & (source < devices_along)
                got_top = jnp.where(valid, got_top, LOWEST)
                got_sum = jnp.where(valid, got_sum, 0.0)
                own_top, block_sum = merge_parts(own_top, block_sum, got_top, got_sum)
        facility_pot = log_capacity - (own_top + jnp.log(block_sum))
    return (cell_pot, facility_pot)


def solution(mesh):
    placed = (
        P(("groups", "tile"), None),
        P(("groups", "tile"), None),
        P(("groups", "tile"), None),
        P("groups", None, None),
        P(("groups", "tile"), None),
        P(("groups", "tile")),
    )
    return jax.shard_map(
        on_device,
        mesh=mesh,
        in_specs=placed,
        out_specs=(P(("groups", "tile"), None), P(("groups", "tile"), None)),
        check_vma=False,
    )
```

profile of v0, /device:TPU:0, one launch (start us, length us, event | category | flops | bytes accessed | tf_op | source)
XLA Modules:
  0.0 832.8 jit_solution(4137859479045331866)
XLA Ops:
  0.6 7.3 collective-permute-start
  15.1 4.0 collective-permute-start.13
  27.2 11.6 %collective-permute-start.2 = (f32[1,256]{1,0:T(1,128)}, f32[1,256]{1,0:T(1,128)S(1)}, u32[]{:S(2)}, u32[]{:S(2)}) collective-permute-start(f32[1,256]{1,0:T(1,128)} %param.12), channel_id=1, source_target_pairs={{0,13},{1,14},{2,15},{16,29},{17,30},{18,31}} | collective-permute-start | bytes 3080 | tf_op jit(solution)/shard_map/ppermute | solution.py:20
  54.3 3.6 collective-permute-start.3
  63.2 6.2 collective-permute-start.8
  74.0 214.7 %while.34 = (s32[]{:T(128)}, f32[16,16,256]{2,1,0:T(8,128)S(1)}, f32[16,16,256]{2,1,0:T(8,128)S(1)}, s32[16]{0:T(128)S(1)}, f32[16,256]{1,0:T(8,128)}, /*index=5...) while((s32[]{:T(128)}, f32[16,16,256]{2,1,0:T(8,128)S(1)}, ...), condition=%wide.region_5.6_spmd.clone, body=%wide.region_0.5_spmd.clone.sunk | while | flops 37755528 | bytes 539080 | solution.py:87
  302.2 4.8 collective-permute-start.76
  307.0 5.6 collective-permute-start.77
  312.6 3.3 collective-permute-start.78
  360.6 3.7 collective-permute-start.46
  364.3 5.4 collective-permute-start.47
  369.7 5.3 collective-permute-start.48
  414.4 4.1 collective-permute-start.100
  418.5 3.9 collective-permute-start.101
  422.4 3.8 collective-permute-start.102
  456.7 8.0 collective-permute-start.90
  474.0 3.2 collective-permute-start.98
  480.8 226.6 %while.35 = (s32[]{:T(128)}, f32[16,256]{1,0:T(8,128)S(1)}, f32[16,16,256]{2,1,0:T(8,128)S(1)}, f32[16,16,256]{2,1,0:T(8,128)S(1)}, f32[16,256]{1,0:T(8,128)}, /...) while((s32[]{:T(128)}, f32[16,256]{1,0:T(8,128)S(1)}, ...), condition=%wide.region_13.14_spmd.clone, body=%wide.region_8.13_spmd.clone.sunk | while | flops 37755784 | bytes 545240 | solution.py:87
  720.7 4.8 collective-permute-start.166
  725.5 5.6 collective-permute-start.167
  731.1 3.3 collective-permute-start.168
  778.5 3.7 collective-permute-start.136
  782.2 5.4 collective-permute-start.137
  787.6 5.3 collective-permute-start.138
  (1016 shorter events, 631.2 us)
Async XLA Ops:
  21.9 16.8 %collective-permute-start.16 = (f32[1,256]{1,0:T(1,128)}, f32[1,256]{1,0:T(1,128)S(1)}, u32[]{:S(2)}, u32[]{:S(2)}) collective-permute-start(f32[1,256]{1,0:T(1,128)} %param.12), channel_id=1, source_target_pairs={{2,0},{3,1},{4,2},{5,3},{6,4},{7,5},{8,6},{9,7},{10,8},{11,9},{12,... | collective-permute-start | bytes 3080 | tf_op jit(solution)/shard_map/ppermute | solution.py:20
  23.2 16.8 %collective-permute-start.17 = (f32[1,256]{1,0:T(1,128)}, f32[1,256]{1,0:T(1,128)S(1)}, u32[]{:S(2)}, u32[]{:S(2)}) collective-permute-start(f32[1,256]{1,0:T(1,128)} %param.12), channel_id=1, source_target_pairs={{3,0},{4,1},{5,2},{6,3},{7,4},{8,5},{9,6},{10,7},{11,8},{12,9},{13... | collective-permute-start | bytes 3080 | tf_op jit(solution)/shard_map/ppermute | solution.py:20
  24.6 16.8 %collective-permute-start.18 = (f32[1,256]{1,0:T(1,128)}, f32[1,256]{1,0:T(1,128)S(1)}, u32[]{:S(2)}, u32[]{:S(2)}) collective-permute-start(f32[1,256]{1,0:T(1,128)} %param.12), channel_id=1, source_target_pairs={{4,0},{5,1},{6,2},{7,3},{8,4},{9,5},{10,6},{11,7},{12,8},{13,9},{1... | collective-permute-start | bytes 3080 | tf_op jit(solution)/shard_map/ppermute | solution.py:20
  25.9 16.8 %collective-permute-start.19 = (f32[1,256]{1,0:T(1,128)}, f32[1,256]{1,0:T(1,128)S(1)}, u32[]{:S(2)}, u32[]{:S(2)}) collective-permute-start(f32[1,256]{1,0:T(1,128)} %param.12), channel_id=1, source_target_pairs={{5,0},{6,1},{7,2},{8,3},{9,4},{10,5},{11,6},{12,7},{13,8},{14,9},{... | collective-permute-start | bytes 3080 | tf_op jit(solution)/shard_map/ppermute | solution.py:20
  27.2 16.8 %collective-permute-start.2 = (f32[1,256]{1,0:T(1,128)}, f32[1,256]{1,0:T(1,128)S(1)}, u32[]{:S(2)}, u32[]{:S(2)}) collective-permute-start(f32[1,256]{1,0:T(1,128)} %param.12), channel_id=1, source_target_pairs={{0,13},{1,14},{2,15},{16,29},{17,30},{18,31}} | collective-permute-start | bytes 3080 | tf_op jit(solution)/shard_map/ppermute | solution.py:20
  296.5 16.1 %collective-permute-start.73 = (f32[1,256]{1,0:T(1,128)S(1)}, f32[1,256]{1,0:T(1,128)S(1)}, u32[]{:S(2)}, u32[]{:S(2)}) collective-permute-start(f32[1,256]{1,0:T(1,128)S(1)} %get-tuple-element.585), channel_id=1, source_target_pairs={{2,0},{3,1},{4,2},{5,3},{6,4},{7,5},{8,6},{9,7},{10,8},{11,9},{12,... | collective-permute-start | bytes 3080 | tf_op jit(solution)/shard_map/ppermute | solution.py:20
  297.8 18.1 %collective-permute-start.74 = (f32[1,256]{1,0:T(1,128)S(1)}, f32[1,256]{1,0:T(1,128)S(1)}, u32[]{:S(2)}, u32[]{:S(2)}) collective-permute-start(f32[1,256]{1,0:T(1,128)S(1)} %get-tuple-element.584), channel_id=1, source_target_pairs={{1,0},{2,1},{3,2},{4,3},{5,4},{6,5},{7,6},{8,7},{9,8},{10,9},{11,1... | collective-permute-start | bytes 3080 | tf_op jit(solution)/shard_map/ppermute | solution.py:20
  299.1 19.9 %collective-permute-start.75 = (f32[1,256]{1,0:T(1,128)S(1)}, f32[1,256]{1,0:T(1,128)S(1)}, u32[]{:S(2)}, u32[]{:S(2)}) collective-permute-start(f32[1,256]{1,0:T(1,128)S(1)} %get-tuple-element.583), channel_id=1, source_target_pairs={{0,1},{1,2},{2,3},{3,4},{4,5},{5,6},{6,7},{7,8},{8,9},{9,10},{10,1... | collective-permute-start | bytes 3080 | tf_op jit(solution)/shard_map/ppermute | solution.py:20
  302.2 20.0 %collective-permute-start.76 = (f32[1,256]{1,0:T(1,128)S(1)}, f32[1,256]{1,0:T(1,128)S(1)}, u32[]{:S(2)}, u32[]{:S(2)}) collective-permute-start(f32[1,256]{1,0:T(1,128)S(1)} %get-tuple-element.582), channel_id=1, source_target_pairs={{0,2},{1,3},{2,4},{3,5},{4,6},{5,7},{6,8},{7,9},{8,10},{9,11},{10,... | collective-permute-start | bytes 3080 | tf_op jit(solution)/shard_map/ppermute | solution.py:20
  307.0 16.5 %collective-permute-start.77 = (f32[1,256]{1,0:T(1,128)S(1)}, f32[1,256]{1,0:T(1,128)S(1)}, u32[]{:S(2)}, u32[]{:S(2)}) collective-permute-start(f32[1,256]{1,0:T(1,128)S(1)} %get-tuple-element.581), channel_id=1, source_target_pairs={{0,3},{1,4},{2,5},{3,6},{4,7},{5,8},{6,9},{7,10},{8,11},{9,12},{10... | collective-permute-start | bytes 3080 | tf_op jit(solution)/shard_map/ppermute | solution.py:20
  353.6 16.1 %collective-permute-start.43 = (f32[1,256]{1,0:T(1,128)S(1)}, f32[1,256]{1,0:T(1,128)S(1)}, u32[]{:S(2)}, u32[]{:S(2)}) collective-permute-start(f32[1,256]{1,0:T(1,128)S(1)} %get-tuple-element.555), channel_id=1, source_target_pairs={{2,0},{3,1},{4,2},{5,3},{6,4},{7,5},{8,6},{9,7},{10,8},{11,9},{12,... | collective-permute-start | bytes 3080 | tf_op jit(solution)/shard_map/ppermute | solution.py:20
  354.9 20.1 %collective-permute-start.44 = (f32[1,256]{1,0:T(1,128)S(1)}, f32[1,256]{1,0:T(1,128)S(1)}, u32[]{:S(2)}, u32[]{:S(2)}) collective-permute-start(f32[1,256]{1,0:T(1,128)S(1)} %get-tuple-element.554), channel_id=1, source_target_pairs={{1,0},{2,1},{3,2},{4,3},{5,4},{6,5},{7,6},{8,7},{9,8},{10,9},{11,1... | collective-permute-start | bytes 3080 | tf_op jit(solution)/shard_map/ppermute | solution.py:20
  356.2 21.9 %collective-permute-start.45 = (f32[1,256]{1,0:T(1,128)S(1)}, f32[1,256]{1,0:T(1,128)S(1)}, u32[]{:S(2)}, u32[]{:S(2)}) collective-permute-start(f32[1,256]{1,0:T(1,128)S(1)} %get-tuple-element.553), channel_id=1, source_target_pairs={{0,1},{1,2},{2,3},{3,4},{4,5},{5,6},{6,7},{7,8},{8,9},{9,10},{10,1... | collective-permute-start | bytes 3080 | tf_op jit(solution)/shard_map/ppermute | solution.py:20
  360.6 20.6 %collective-permute-start.46 = (f32[1,256]{1,0:T(1,128)S(1)}, f32[1,256]{1,0:T(1,128)S(1)}, u32[]{:S(2)}, u32[]{:S(2)}) collective-permute-start(f32[1,256]{1,0:T(1,128)S(1)} %get-tuple-element.552), channel_id=1, source_target_pairs={{0,2},{1,3},{2,4},{3,5},{4,6},{5,7},{6,8},{7,9},{8,10},{9,11},{10,... | collective-permute-start | bytes 3080 | tf_op jit(solution)/shard_map/ppermute | solution.py:20
  364.3 18.3 %collective-permute-start.47 = (f32[1,256]{1,0:T(1,128)S(1)}, f32[1,256]{1,0:T(1,128)S(1)}, u32[]{:S(2)}, u32[]{:S(2)}) collective-permute-start(f32[1,256]{1,0:T(1,128)S(1)} %get-tuple-element.551), channel_id=1, source_target_pairs={{0,3},{1,4},{2,5},{3,6},{4,7},{5,8},{6,9},{7,10},{8,11},{9,12},{10... | collective-permute-start | bytes 3080 | tf_op jit(solution)/shard_map/ppermute | solution.py:20
  716.3 18.1 %collective-permute-start.164 = (f32[1,256]{1,0:T(1,128)S(1)}, f32[1,256]{1,0:T(1,128)S(1)}, u32[]{:S(2)}, u32[]{:S(2)}) collective-permute-start(f32[1,256]{1,0:T(1,128)S(1)} %get-tuple-element.524), channel_id=1, source_target_pairs={{1,0},{2,1},{3,2},{4,3},{5,4},{6,5},{7,6},{8,7},{9,8},{10,9},{11,1... | collective-permute-start | bytes 3080 | tf_op jit(solution)/shard_map/ppermute | solution.py:20
  717.6 19.6 %collective-permute-start.165 = (f32[1,256]{1,0:T(1,128)S(1)}, f32[1,256]{1,0:T(1,128)S(1)}, u32[]{:S(2)}, u32[]{:S(2)}) collective-permute-start(f32[1,256]{1,0:T(1,128)S(1)} %get-tuple-element.523), channel_id=1, source_target_pairs={{0,1},{1,2},{2,3},{3,4},{4,5},{5,6},{6,7},{7,8},{8,9},{9,10},{10,1... | collective-permute-start | bytes 3080 | tf_op jit(solution)/shard_map/ppermute | solution.py:20
  720.7 19.7 %collective-permute-start.166 = (f32[1,256]{1,0:T(1,128)S(1)}, f32[1,256]{1,0:T(1,128)S(1)}, u32[]{:S(2)}, u32[]{:S(2)}) collective-permute-start(f32[1,256]{1,0:T(1,128)S(1)} %get-tuple-element.522), channel_id=1, source_target_pairs={{0,2},{1,3},{2,4},{3,5},{4,6},{5,7},{6,8},{7,9},{8,10},{9,11},{10,... | collective-permute-start | bytes 3080 | tf_op jit(solution)/shard_map/ppermute | solution.py:20
  725.5 16.2 %collective-permute-start.167 = (f32[1,256]{1,0:T(1,128)S(1)}, f32[1,256]{1,0:T(1,128)S(1)}, u32[]{:S(2)}, u32[]{:S(2)}) collective-permute-start(f32[1,256]{1,0:T(1,128)S(1)} %get-tuple-element.521), channel_id=1, source_target_pairs={{0,3},{1,4},{2,5},{3,6},{4,7},{5,8},{6,9},{7,10},{8,11},{9,12},{10... | collective-permute-start | bytes 3080 | tf_op jit(solution)/shard_map/ppermute | solution.py:20
  771.5 16.1 %collective-permute-start.133 = (f32[1,256]{1,0:T(1,128)S(1)}, f32[1,256]{1,0:T(1,128)S(1)}, u32[]{:S(2)}, u32[]{:S(2)}) collective-permute-start(f32[1,256]{1,0:T(1,128)S(1)} %get-tuple-element.495), channel_id=1, source_target_pairs={{2,0},{3,1},{4,2},{5,3},{6,4},{7,5},{8,6},{9,7},{10,8},{11,9},{12,... | collective-permute-start | bytes 3080 | tf_op jit(solution)/shard_map/ppermute | solution.py:20
  772.8 20.1 %collective-permute-start.134 = (f32[1,256]{1,0:T(1,128)S(1)}, f32[1,256]{1,0:T(1,128)S(1)}, u32[]{:S(2)}, u32[]{:S(2)}) collective-permute-start(f32[1,256]{1,0:T(1,128)S(1)} %get-tuple-element.494), channel_id=1, source_target_pairs={{1,0},{2,1},{3,2},{4,3},{5,4},{6,5},{7,6},{8,7},{9,8},{10,9},{11,1... | collective-permute-start | bytes 3080 | tf_op jit(solution)/shard_map/ppermute | solution.py:20
  774.1 21.9 %collective-permute-start.135 = (f32[1,256]{1,0:T(1,128)S(1)}, f32[1,256]{1,0:T(1,128)S(1)}, u32[]{:S(2)}, u32[]{:S(2)}) collective-permute-start(f32[1,256]{1,0:T(1,128)S(1)} %get-tuple-element.493), channel_id=1, source_target_pairs={{0,1},{1,2},{2,3},{3,4},{4,5},{5,6},{6,7},{7,8},{8,9},{9,10},{10,1... | collective-permute-start | bytes 3080 | tf_op jit(solution)/shard_map/ppermute | solution.py:20
  778.5 20.6 %collective-permute-start.136 = (f32[1,256]{1,0:T(1,128)S(1)}, f32[1,256]{1,0:T(1,128)S(1)}, u32[]{:S(2)}, u32[]{:S(2)}) collective-permute-start(f32[1,256]{1,0:T(1,128)S(1)} %get-tuple-element.492), channel_id=1, source_target_pairs={{0,2},{1,3},{2,4},{3,5},{4,6},{5,7},{6,8},{7,9},{8,10},{9,11},{10,... | collective-permute-start | bytes 3080 | tf_op jit(solution)/shard_map/ppermute | solution.py:20
  782.2 18.3 %collective-permute-start.137 = (f32[1,256]{1,0:T(1,128)S(1)}, f32[1,256]{1,0:T(1,128)S(1)}, u32[]{:S(2)}, u32[]{:S(2)}) collective-permute-start(f32[1,256]{1,0:T(1,128)S(1)} %get-tuple-element.491), channel_id=1, source_target_pairs={{0,3},{1,4},{2,5},{3,6},{4,7},{5,8},{6,9},{7,10},{8,11},{9,12},{10... | collective-permute-start | bytes 3080 | tf_op jit(solution)/shard_map/ppermute | solution.py:20
  (160 other events, 1439.9 us)
where the time goes:
time: 842 us; the launch traced here: 833 us
  starting transfers between devices  344 us (41%)
  other arithmetic  266 us (32%)
  local copies, waits for them, and re-layouts  103 us (12%)
  loops' own time  86.1 us (10%)
  waiting for transfers between devices  29.8 us (4%)
    ppermute x180, starting transfers between devices, from_behind(): return lax.ppermute(block, axis, route)  344 us
    another operation x2, loops' own time, on_device(): lax.map(one_tile, (tile_ids, log_demand, pair_block, local_block, pair_co...  86.1 us
    dynamic_slice x96, local copies, waits for them, and re-layouts, on_device(): lax.map(one_tile, (tile_ids, log_demand, pair_block, local_block, pair_co...  60.2 us
    reduce_sum x32, other arithmetic, tile_pass(): row_sum = jnp.sum(jnp.exp(scores - row_top[None, :, None]), axis=(0, 2))  59.7 us
    reduce_sum x32, other arithmetic, tile_pass(): col_sum = jnp.sum(jnp.exp(column_scores - col_top[:, None, :]), axis=1)  52.5 us
    reduce_max x32, other arithmetic, tile_pass(): row_top = jnp.max(scores, axis=(0, 2))  46.9 us
    reduce_max x32, other arithmetic, tile_pass(): col_top = jnp.max(column_scores, axis=1)  39.1 us
    ppermute x180, waiting for transfers between devices, from_behind(): return lax.ppermute(block, axis, route)  29.8 us
  transfers between devices with their start and end apart: 180, of which 23 were waited for; matrix products, arithmetic and copies ran while one was open for 0% of the time, Pallas kernels for 0%

commit v1 on v0

--- a/solution.py
+++ b/solution.py
@@ -1,6 +1,8 @@
 import jax
 import jax.numpy as jnp
 from jax import lax
+from jax.experimental import pallas as pl
+from jax.experimental.pallas import tpu as pltpu
 from jax.sharding import PartitionSpec as P
 
 TSIDE = 16
@@ -12,6 +14,221 @@
 
 
 LOWEST = -1e30
+
+HALF = TSIDE * TILE_COLS // 2
+COLS_HALF = TILE_COLS // 2
+SCALE = 1.0 / float(REACH * REACH)
+MIDDLE = 736.0
+ROW_POT = TSIDE
+ROW_CAP = TSIDE + 2
+ROW_MASK = TSIDE + 4
+ROWS = TSIDE + 8
+
+
+def dot_nt(a, b):
+    return lax.dot_general(a, b, (((1,), (1,)), ((), ())), preferred_element_type=jnp.float32)
+
+
+def dot_nn(a, b):
+    return lax.dot_general(a, b, (((1,), (0,)), ((), ())), preferred_element_type=jnp.float32)
+
+
+def split(values):
+    high = values.astype(jnp.bfloat16)
+    low = (values - high.astype(jnp.float32)).astype(jnp.bfloat16)
+    return high, low
+
+
+def center_cost(xy_ref, block, core, rows):
+    fx = xy_ref[block, 0:1, :]
+    fy = xy_ref[block, 1:2, :]
+    x_mid = (core * HALF).astype(jnp.float32) + 0.5 * HALF
+    y_mid = (lax.broadcasted_iota(jnp.int32, (rows, 1), 0) * TSIDE).astype(jnp.float32) + 0.5 * TSIDE
+    dx = x_mid - fx
+    dy = y_mid - fy
+    return (dx * dx + dy * dy) * SCALE
+
+
+def y_factor(xy_ref, block):
+    offset = lax.broadcasted_iota(jnp.int32, (TSIDE, 1), 0).astype(jnp.float32) - 0.5 * (TSIDE - 1)
+    return jnp.exp(offset * ((xy_ref[block, 1:2, :] - MIDDLE) * (2.0 * SCALE)))
+
+
+def x_factor(xy_ref, block):
+    offset = lax.broadcasted_iota(jnp.int32, (HALF, 1), 0).astype(jnp.float32) - 0.5 * (HALF - 1)
+    return jnp.exp(offset * ((xy_ref[block, 0:1, :] - MIDDLE) * (2.0 * SCALE)))
+
+
+def build_mask(recv_ref, mask_ref, rows, blocks):
+    marks = recv_ref[:, ROW_MASK, :]
+    lane_block = lax.broadcasted_iota(jnp.int32, (blocks, rows, HALF), 2) // COLS_HALF
+    own_block = lax.broadcasted_iota(jnp.int32, (blocks, rows, HALF), 0)
+    picked = jnp.where(lane_block == own_block, marks[None], 0.0)
+    picked = picked.reshape(blocks * rows, HALF).astype(jnp.bfloat16)
+    source = lax.broadcasted_iota(jnp.int32, (HALF, HALF), 0) % COLS_HALF
+    target = lax.broadcasted_iota(jnp.int32, (HALF, HALF), 1) // TSIDE
+    spread = jnp.where(source == target, 1.0, 0.0).astype(jnp.bfloat16)
+    mask_ref[...] = dot_nn(picked, spread).reshape(blocks, rows, HALF)
+
+
+def row_pass(recv_ref, xy_ref, pot_of, mask_ref, top_ref, xf_ref, acc_ref, core, rows, blocks):
+    def tops(block, best):
+        scores = pot_of(block) - center_cost(xy_ref, block, core, rows)
+        top = jnp.broadcast_to(jnp.max(scores, axis=1, keepdims=True), (rows, HALF))
+        top_ref[block] = top
+        return jnp.maximum(best, jnp.where(mask_ref[block] > 0.0, top, LOWEST))
+
+    best = lax.fori_loop(0, blocks, tops, jnp.full((rows, HALF), LOWEST, jnp.float32))
+    acc_ref[...] = jnp.zeros_like(acc_ref)
+
+    def sums(block, carry):
+        high, low = split(x_factor(xy_ref, block))
+        xf_ref[block, :HALF, :] = high
+        xf_ref[block, HALF:, :] = low
+        top = top_ref[block]
+        scores = pot_of(block) - center_cost(xy_ref, block, core, rows)
+        weight = jnp.exp(scores - top[:, 0:1])
+        lhs = weight[:, None, :] * y_factor(xy_ref, block)[None]
+        a_high, a_low = split(lhs.reshape(rows * TSIDE, lhs.shape[-1]))
+        both = dot_nt(a_high, xf_ref[block])
+        third = dot_nt(a_low, xf_ref[block, :HALF, :])
+        part = both[:, :HALF] + both[:, HALF:] + third
+        scale = jnp.where(mask_ref[block] > 0.0, jnp.exp(jnp.minimum(top - best, 0.0)), 0.0)
+        acc_ref[...] += part.reshape(rows, TSIDE, HALF) * scale[:, None, :]
+        return carry
+
+    lax.fori_loop(0, blocks, sums, 0)
+    demand = recv_ref[:, :TSIDE, :]
+    return demand - best[:, None, :] - jnp.log(acc_ref[...])
+
+
+def column_part(xy_ref, mask_ref, xf_ref, level, base, block, core, rows):
+    active = mask_ref[block] > 0.0
+    top = jnp.max(jnp.where(active, level, LOWEST), axis=1, keepdims=True)
+    scale = jnp.where(active, jnp.exp(jnp.minimum(level - top, 0.0)), 0.0)
+    weights = (base * scale[:, None, :]).reshape(rows * TSIDE, HALF)
+    w_high, w_low = split(weights)
+    mixed = dot_nn(jnp.concatenate([w_high, w_high], axis=1), xf_ref[block])
+    mixed = mixed + dot_nn(w_low, xf_ref[block, :HALF, :])
+    width = mixed.shape[-1]
+    sums = jnp.sum(mixed.reshape(rows, TSIDE, width) * y_factor(xy_ref, block)[None], axis=1)
+    tops = top - center_cost(xy_ref, block, core, rows)
+    best = jnp.max(tops, axis=0, keepdims=True)
+    total = jnp.sum(sums * jnp.exp(tops - best), axis=0, keepdims=True)
+    return best + jnp.log(total)
+
+
+def first_kernel(rows, blocks, recv_ref, xy_ref, part_ref, mask_ref, top_ref, xf_ref, acc_ref):
+    core = lax.axis_index("tile") % 2
+    build_mask(recv_ref, mask_ref, rows, blocks)
+
+    def pot_of(block):
+        return jnp.concatenate(
+            [recv_ref[block, ROW_POT : ROW_POT + 1, :], recv_ref[block, ROW_POT + 1 : ROW_POT + 2, :]], axis=1
+        )
+
+    shifted = row_pass(recv_ref, xy_ref, pot_of, mask_ref, top_ref, xf_ref, acc_ref, core, rows, blocks)
+    level = jnp.max(shifted, axis=1)
+    acc_ref[...] = jnp.exp(shifted - level[:, None, :])
+
+    def columns(block, carry):
+        part_ref[pl.ds(block, 1), :] = column_part(
+            xy_ref, mask_ref, xf_ref, level, acc_ref[...], block, core, rows
+        )
+        return carry
+
+    lax.fori_loop(0, blocks, columns, 0)
+
+
+def log_add(a, b):
+    top = jnp.maximum(a, b)
+    return top + jnp.log(jnp.exp(a - top) + jnp.exp(b - top))
+
+
+def second_kernel(
+    rows, blocks, recv_ref, xy_ref, mine_ref, other_ref, keep_ref, send_ref, pot_ref, mask_ref, top_ref, xf_ref, acc_ref
+):
+    me = lax.axis_index("tile")
+    core = me % 2
+    build_mask(recv_ref, mask_ref, rows, blocks)
+    capacity = jnp.concatenate([recv_ref[:, ROW_CAP, :], recv_ref[:, ROW_CAP + 1, :]], axis=1)
+    pot_ref[...] = capacity - log_add(mine_ref[...], other_ref[...])
+
+    def pot_of(block):
+        return pot_ref[pl.ds(block, 1), :]
+
+    shifted = row_pass(recv_ref, xy_ref, pot_of, mask_ref, top_ref, xf_ref, acc_ref, core, rows, blocks)
+    level = jnp.max(shifted, axis=1)
+    acc_ref[...] = shifted
+    x_mid = (core * HALF).astype(jnp.float32) + 0.5 * HALF
+    dx = lax.broadcasted_iota(jnp.int32, (1, HALF), 1).astype(jnp.float32) - 0.5 * (HALF - 1)
+    dy = lax.broadcasted_iota(jnp.int32, (TSIDE, 1), 0).astype(jnp.float32) - 0.5 * (TSIDE - 1)
+    for row, out_ref in ((me, keep_ref), (me + 1 - 2 * core, send_ref)):
+        y_mid = (row * TSIDE).astype(jnp.float32) + 0.5 * TSIDE
+        lift = (dx * (dx + 2.0 * (x_mid - MIDDLE)) + dy * (dy + 2.0 * (y_mid - MIDDLE))) * SCALE
+        out_ref[:TSIDE, :] = acc_ref[row] + lift
+        part = column_part(
+            xy_ref, mask_ref, xf_ref, level, jnp.exp(shifted - level[:, None, :]), row, core, rows
+        )
+        out_ref[ROW_POT : ROW_POT + 1, :] = part[:, :HALF]
+        out_ref[ROW_POT + 1 : ROW_POT + 2, :] = part[:, HALF:]
+        out_ref[ROW_POT + 2 :, :] = jnp.zeros((ROWS - ROW_POT - 2, HALF), jnp.float32)
+
+
+def on_device_all_rows(log_demand, log_capacity, warm_potential, facility_xy, pair_block, pair_count):
+    devices = lax.axis_size("tile")
+    me = lax.axis_index("tile")
+    rows = devices
+    blocks = facility_xy.shape[0]
+    width = log_capacity.shape[1]
+    demand = log_demand.reshape(TILE_COLS, TSIDE, TSIDE).transpose(1, 0, 2).reshape(TSIDE, 2, HALF)
+    active = jnp.arange(KSLOTS, dtype=jnp.int32)[None, :] < pair_count[:, None]
+    block_ids = jnp.arange(blocks, dtype=jnp.int32)
+    hits = (pair_block[None] == block_ids[:, None, None]) & active[None]
+    marks = jnp.max(hits.astype(jnp.float32), axis=2)
+    marks = marks.reshape(blocks, 2, COLS_HALF).transpose(1, 0, 2).reshape(2, 1, HALF)
+    small = jnp.concatenate([warm_potential.reshape(2, HALF), log_capacity.reshape(2, HALF)], axis=0)
+    small = jnp.broadcast_to(small[None], (2, 4, HALF))
+    message = jnp.concatenate(
+        [demand.transpose(1, 0, 2), small, marks, jnp.zeros((2, ROWS - ROW_MASK - 1, HALF), jnp.float32)], axis=1
+    )
+    message = jnp.broadcast_to(message[None], (devices // 2, 2, ROWS, HALF)).reshape(devices, ROWS, HALF)
+    recv = lax.all_to_all(message, "tile", 0, 0, tiled=True)
+    scratch = [
+        pltpu.VMEM((blocks, rows, HALF), jnp.float32),
+        pltpu.VMEM((blocks, rows, HALF), jnp.float32),
+        pltpu.VMEM((blocks, 2 * HALF, width), jnp.bfloat16),
+        pltpu.VMEM((rows, TSIDE, HALF), jnp.float32),
+    ]
+    params = pltpu.CompilerParams(vmem_limit_bytes=48 * 1024 * 1024)
+    part = pl.pallas_call(
+        lambda *refs: first_kernel(rows, blocks, *refs),
+        out_shape=jax.ShapeDtypeStruct((blocks, width), jnp.float32),
+        scratch_shapes=scratch,
+        compiler_params=params,
+        name="first_iteration",
+    )(recv, facility_xy)
+    swap = [(i, i ^ 1) for i in range(devices)]
+    other = lax.ppermute(part, "tile", swap)
+    keep, send = pl.pallas_call(
+        lambda *refs: second_kernel(rows, blocks, *refs),
+        out_shape=(
+            jax.ShapeDtypeStruct((ROWS, HALF), jnp.float32),
+            jax.ShapeDtypeStruct((ROWS, HALF), jnp.float32),
+        ),
+        scratch_shapes=[pltpu.VMEM((blocks, width), jnp.float32)] + scratch,
+        compiler_params=params,
+        name="second_iteration",
+    )(recv, facility_xy, part, other)
+    got = lax.ppermute(send, "tile", swap)
+    is_left = me % 2 == 0
+    left = jnp.where(is_left, keep, got)
+    right = jnp.where(is_left, got, keep)
+    cells = jnp.concatenate([left[:TSIDE], right[:TSIDE]], axis=1)
+    cell_pot = cells.reshape(TSIDE, TILE_COLS, TSIDE).transpose(1, 0, 2).reshape(TILE_COLS, TSIDE * TSIDE)
+    total = log_add(keep[ROW_POT : ROW_POT + 2], got[ROW_POT : ROW_POT + 2])
+    facility_pot = log_capacity - total.reshape(1, width)
+    return (cell_pot, facility_pot)
 
 
 def from_behind(block, axis, distance):
@@ -130,10 +347,19 @@
         P(("groups", "tile"), None),
         P(("groups", "tile")),
     )
-    return jax.shard_map(
-        on_device,
-        mesh=mesh,
-        in_specs=placed,
-        out_specs=(P(("groups", "tile"), None), P(("groups", "tile"), None)),
-        check_vma=False,
-    )
+    devices = mesh.shape["tile"]
+    small = devices % 2 == 0 and devices * COLS_HALF == HALF
+
+    def program(log_demand, log_capacity, warm_potential, facility_xy, pair_block, pair_count):
+        one_row = log_demand.shape[0] == mesh.size * TILE_COLS and log_capacity.shape[0] == mesh.size
+        fits = small and one_row and log_capacity.shape[1] == 2 * HALF
+        body = on_device_all_rows if fits else on_device
+        return jax.shard_map(
+            body,
+            mesh=mesh,
+            in_specs=placed,
+            out_specs=(P(("groups", "tile"), None), P(("groups", "tile"), None)),
+            check_vma=False,
+        )(log_demand, log_capacity, warm_potential, facility_xy, pair_block, pair_count)
+
+    return program

time: 842 us -> 43.3 us (0.05); the launches traced: 833 us -> 42.9 us
  starting transfers between devices: 344 us -> 0.3 us
  other arithmetic: 266 us -> 2.22 us
  local copies, waits for them, and re-layouts: 103 us -> 2.66 us
  loops' own time: 86.1 us -> 0 us
  waiting for transfers between devices: 29.8 us -> 2.18 us
  Pallas kernels: 0 us -> 18.6 us
  blocking collectives: 0 us -> 16.2 us
    ppermute x180 -> x2, starting transfers between devices: 344 us -> 0.3 us  [the longest x1 0.23 us: on_device_all_rows(): got = lax.ppermute(send, 'tile', swap)]
    reduce_sum x64 -> x0, other arithmetic: 112 us -> none  [the longest x32 59.7 us: tile_pass(): row_sum = jnp.sum(jnp.exp(scores - row_top[None, :, None]), axis=(0, 2))]
    another operation x2 -> x0, loops' own time: 86.1 us -> none  [on_device(): lax.map(one_tile, (tile_ids, log_demand, pair_block, local_block, pair_co...]
    reduce_max x64 -> x1, other arithmetic: 86.1 us -> 0.8 us  [on_device_all_rows(): marks = jnp.max(hits.astype(jnp.float32), axis=2)]
    dynamic_slice x96 -> x0, local copies, waits for them, and re-layouts: 60.2 us -> none  [on_device(): lax.map(one_tile, (tile_ids, log_demand, pair_block, local_block, pair_co...]
    gather x66 -> x0, local copies, waits for them, and re-layouts: 39.3 us -> none  [the longest x32 19 us: one_tile(): facility_xy[blocks]]
    ppermute x180 -> x2, waiting for transfers between devices: 29.8 us -> 2.18 us  [the longest x1 1.17 us: on_device_all_rows(): other = lax.ppermute(part, 'tile', swap)]
    select_n x33 -> x1, other arithmetic: 22.4 us -> 0.01 us  [on_device_all_rows(): left = jnp.where(is_left, keep, got)]
  transfers between devices with their start and end apart: 180 -> 2, of which waited for: 23 -> 2; matrix products, arithmetic and copies ran while one was open for 0% -> 0% of each run, Pallas kernels for 0% -> 0%
where the time goes in v1:
time: 43.3 us; the launch traced here: 42.9 us
  Pallas kernels  18.6 us (43%)
  blocking collectives  16.2 us (37%)
  local copies, waits for them, and re-layouts  2.66 us (6%)
  other arithmetic  2.22 us (5%)
  waiting for transfers between devices  2.18 us (5%)
  between operations  0.76 us (2%)
    all_to_all x1, blocking collectives, on_device_all_rows(): recv = lax.all_to_all(message, 'tile', 0, 0, tiled=True)  16.2 us
    pallas_call x1, Pallas kernels, on_device_all_rows(): pl.pallas_call(lambda *refs: first_kernel(rows, blocks, *refs), out_shape...  11.8 us
    pallas_call x1, Pallas kernels, on_device_all_rows(): pl.pallas_call(lambda *refs: second_kernel(rows, blocks, *refs), out_shap...  6.83 us
    unnamed x8, local copies, waits for them, and re-layouts  1.23 us
    ppermute x1, waiting for transfers between devices, on_device_all_rows(): other = lax.ppermute(part, 'tile', swap)  1.17 us
    ppermute x1, waiting for transfers between devices, on_device_all_rows(): got = lax.ppermute(send, 'tile', swap)  1.01 us
  transfers between devices with their start and end apart: 2, of which 2 were waited for; matrix products, arithmetic and copies ran while one was open for 0% of the time, Pallas kernels for 0%

profile of v1, /device:TPU:0, one launch (start us, length us, event | category | flops | bytes accessed | tf_op | source)
XLA Modules:
  0.0 42.9 jit_solution(7265177423467879411)
XLA Ops:
  0.6 0.7 %iota_compare_fusion.1 = pred[16,16]{1,0:T(8,128)(4,1)S(1)} fusion(s32[16]{0:T(128)} %param.11), kind=kLoop, calls=%fused_computation.6 | loop fusion | flops 256 | bytes 320 | tf_op jit(solution)/shard_map/lt | solution.py:185
  1.4 0.8 %convert_reduce_fusion = f32[16,16]{1,0:T(8,128)S(1)} fusion(s32[16,16]{1,0:T(8,128)} %param.10, pred[16,16]{1,0:T(8,128)(4,1)S(1)} %iota_compare_fusion.1), kind=kLoop, calls=%fused_computation.1 | loop fusion | flops 16128 | bytes 2304 | tf_op jit(solution)/shard_map/reduce_max | solution.py:188
  2.2 0.1 copy.14
  2.2 0.1 copy.15
  2.3 0.1 reshape.60
  2.4 0.5 %copy-done.1 = f32[16,256]{1,0:T(8,128)S(1)} copy-done((f32[16,256]{1,0:T(8,128)S(1)}, f32[16,256]{1,0:T(8,128)}, u32[]{:S(2)}) %copy-start.1) | copy-done | bytes 16408
  3.0 0.1 reshape.55
  3.1 0.0 copy-start.3
  3.1 0.1 reshape.56
  3.2 0.0 copy-start.2
  3.2 0.5 %copy-done.3 = f32[1,256]{1,0:T(1,128)S(1)} copy-done((f32[1,256]{1,0:T(1,128)S(1)}, f32[1,256]{1,0:T(1,128)}, u32[]{:S(2)}) %copy-start.3) | copy-done | bytes 1048
  3.8 0.1 copy-done.2
  3.9 0.1 pad.5.clone
  4.0 0.1 maximum_maximum_fusion
  4.1 16.2 %all_to_all.5.refs_0_ = f32[16,24,128]{2,1,0:T(8,128)S(1)} all-to-all(f32[16,24,128]{2,1,0:T(8,128)S(1)} %bitcast.12), channel_id=1, replica_groups=mesh['groups'=2,'tile'=16] {'tile'}, dimensions={0} | all-to-all | bytes 393216 | tf_op jit(solution)/shard_map/all_to_all | solution.py:196
  20.3 11.8 %first_iteration.1.refs_2_ = f32[16,256]{1,0:T(8,128)S(1)} custom-call(f32[16,24,128]{2,1,0:T(8,128)S(1)} %all_to_all.5.refs_0_, f32[16,2,256]{2,1,0:T(2,128)S(1)} %copy-done), custom_call_target="tpu_custom_call" | custom-call | tf_op jit(solution)/shard_map/first_iteration/pallas_call | solution.py:204
  32.1 0.1 collective-permute-start
  32.2 1.2 %collective-permute-done.refs_3_ = f32[16,256]{1,0:T(8,128)S(1)} collective-permute-done((f32[16,256]{1,0:T(8,128)S(1)}, f32[16,256]{1,0:T(8,128)S(1)}, u32[]{:S(2)}, u32[]{:S(2)}) %collective-permute-start) | collective-permute-done | bytes 16416 | tf_op jit(solution)/shard_map/ppermute | solution.py:212
  33.4 6.8 %second_iteration.1 = (f32[24,128]{1,0:T(8,128)S(1)}, f32[24,128]{1,0:T(8,128)S(1)}) custom-call(f32[16,24,128]{2,1,0:T(8,128)S(1)} %all_to_all.5.refs_0_, f32[16,2,256]{2,1,0:T(2,128)S(1)} %copy-done, f32[16,256]{1,0:T(8,128)S(1)} %first_iteration.1.refs_2_, f32[16,256]{1,0:T(8,128)S(1)} %collective-permute-done.refs_3_), custom_call_target="tpu_custom_call" | custom-call | tf_op jit(solution)/shard_map/second_iteration/pallas_call | solution.py:213
  40.2 0.2 collective-permute-start.1
  40.4 1.0 %collective-permute-done.1 = f32[24,128]{1,0:T(8,128)S(1)} collective-permute-done((f32[24,128]{1,0:T(8,128)S(1)}, f32[24,128]{1,0:T(8,128)S(1)}, u32[]{:S(2)}, u32[]{:S(2)}) %collective-permute-start.1) | collective-permute-done | bytes 12320 | tf_op jit(solution)/shard_map/ppermute | solution.py:223
  41.5 0.1 reshape.62
  41.6 0.7 %reshape.63 = f32[16,256]{1,0:T(8,128)} reshape(f32[16,16,16]{2,1,0:T(8,128)S(1)} %copy.17) | data formatting | bytes 32768 | tf_op jit(solution)/shard_map/reshape | solution.py:228
  42.3 0.6 %sub.11 = f32[1,256]{1,0:T(1,128)} subtract(f32[1,256]{1,0:T(1,128)S(1)} %copy-done.2, f32[1,256]{1,0:T(1,128)S(1)} %bitcast.17) | non-fusion elementwise | flops 256 | bytes 3072 | tf_op jit(solution)/shard_map/sub | solution.py:230
  (13 shorter events, 0.1 us)
Async XLA Ops:
  2.2 0.7 %copy-start.1 = (f32[16,256]{1,0:T(8,128)S(1)}, f32[16,256]{1,0:T(8,128)}, u32[]{:S(2)}) copy-start(f32[16,256]{1,0:T(8,128)} %param.6) | copy-start | bytes 49156
  3.1 0.7 %copy-start.3 = (f32[1,256]{1,0:T(1,128)S(1)}, f32[1,256]{1,0:T(1,128)}, u32[]{:S(2)}) copy-start(f32[1,256]{1,0:T(1,128)} %param.8) | copy-start | bytes 3076
  3.2 0.7 %copy-start.2 = (f32[1,256]{1,0:T(1,128)S(1)}, f32[1,256]{1,0:T(1,128)}, u32[]{:S(2)}) copy-start(f32[1,256]{1,0:T(1,128)} %param.7) | copy-start | bytes 3076
  4.1 16.2 %copy-start = (f32[16,2,256]{2,1,0:T(2,128)S(1)}, f32[16,2,256]{2,1,0:T(2,128)}, u32[]{:S(2)}) copy-start(f32[16,2,256]{2,1,0:T(2,128)} %refs_1_.3) | copy-start | bytes 98308
  32.1 1.2 %collective-permute-start = (f32[16,256]{1,0:T(8,128)S(1)}, f32[16,256]{1,0:T(8,128)S(1)}, u32[]{:S(2)}, u32[]{:S(2)}) collective-permute-start(f32[16,256]{1,0:T(8,128)S(1)} %first_iteration.1.refs_2_), channel_id=1, source_target_pairs={{0,1},{1,0},{2,3},{3,2},{4,5},{5,4},{6,7},{7,6},{8,9},{9,8},{10,11... | collective-permute-start | bytes 49160 | tf_op jit(solution)/shard_map/ppermute | solution.py:212
  40.2 1.2 %collective-permute-start.1 = (f32[24,128]{1,0:T(8,128)S(1)}, f32[24,128]{1,0:T(8,128)S(1)}, u32[]{:S(2)}, u32[]{:S(2)}) collective-permute-start(f32[24,128]{1,0:T(8,128)S(1)} %get-tuple-element.5), channel_id=1, source_target_pairs={{0,1},{1,0},{2,3},{3,2},{4,5},{5,4},{6,7},{7,6},{8,9},{9,8},{10,11... | collective-permute-start | bytes 36872 | tf_op jit(solution)/shard_map/ppermute | solution.py:223

commit v2 on v1

--- a/solution.py
+++ b/solution.py
@@ -78,7 +78,7 @@
         top_ref[block] = top
         return jnp.maximum(best, jnp.where(mask_ref[block] > 0.0, top, LOWEST))
 
-    best = lax.fori_loop(0, blocks, tops, jnp.full((rows, HALF), LOWEST, jnp.float32))
+    best = lax.fori_loop(0, blocks, tops, jnp.full((rows, HALF), LOWEST, jnp.float32), unroll=True)
     acc_ref[...] = jnp.zeros_like(acc_ref)
 
     def sums(block, carry):
@@ -97,7 +97,7 @@
         acc_ref[...] += part.reshape(rows, TSIDE, HALF) * scale[:, None, :]
         return carry
 
-    lax.fori_loop(0, blocks, sums, 0)
+    lax.fori_loop(0, blocks, sums, 0, unroll=True)
     demand = recv_ref[:, :TSIDE, :]
     return demand - best[:, None, :] - jnp.log(acc_ref[...])
 
@@ -137,7 +137,7 @@
         )
         return carry
 
-    lax.fori_loop(0, blocks, columns, 0)
+    lax.fori_loop(0, blocks, columns, 0, unroll=True)
 
 
 def log_add(a, b):

time: 43.3 us -> 30.6 us (0.71)
  Pallas kernels: 18.6 us -> 5.99 us
    pallas_call x1, Pallas kernels: 11.8 us -> 3.48 us  [on_device_all_rows(): pl.pallas_call(lambda *refs: first_kernel(rows, blocks, *refs), out_shape...]
    pallas_call x1, Pallas kernels: 6.83 us -> 2.51 us  [on_device_all_rows(): pl.pallas_call(lambda *refs: second_kernel(rows, blocks, *refs), out_shap...]
where the time goes in v2:
time: 30.6 us; the launch traced here: 30.3 us
  blocking collectives  16.2 us (53%)
  Pallas kernels  5.99 us (20%)
  local copies, waits for them, and re-layouts  2.66 us (9%)
  other arithmetic  2.22 us (7%)
  waiting for transfers between devices  2.18 us (7%)
  between operations  0.76 us (2%)
    all_to_all x1, blocking collectives, on_device_all_rows(): recv = lax.all_to_all(message, 'tile', 0, 0, tiled=True)  16.2 us
    pallas_call x1, Pallas kernels, on_device_all_rows(): pl.pallas_call(lambda *refs: first_kernel(rows, blocks, *refs), out_shape...  3.48 us
    pallas_call x1, Pallas kernels, on_device_all_rows(): pl.pallas_call(lambda *refs: second_kernel(rows, blocks, *refs), out_shap...  2.51 us
    unnamed x8, local copies, waits for them, and re-layouts  1.23 us
    ppermute x1, waiting for transfers between devices, on_device_all_rows(): other = lax.ppermute(part, 'tile', swap)  1.17 us
    ppermute x1, waiting for transfers between devices, on_device_all_rows(): got = lax.ppermute(send, 'tile', swap)  1.01 us
    reshape x2, local copies, waits for them, and re-layouts, on_device_all_rows(): cells.reshape(TSIDE, TILE_COLS, TSIDE).transpose(1, 0, 2)  0.81 us
    reduce_max x1, other arithmetic, on_device_all_rows(): marks = jnp.max(hits.astype(jnp.float32), axis=2)  0.8 us
  transfers between devices with their start and end apart: 2, of which 2 were waited for; matrix products, arithmetic and copies ran while one was open for 0% of the time, Pallas kernels for 0%

profile of v2, /device:TPU:0, one launch (start us, length us, event | category | flops | bytes accessed | tf_op | source)
XLA Modules:
  0.0 30.3 jit_solution(10317270202935895472)
XLA Ops:
  0.6 0.7 %iota_compare_fusion.1 = pred[16,16]{1,0:T(8,128)(4,1)S(1)} fusion(s32[16]{0:T(128)} %param.11), kind=kLoop, calls=%fused_computation.6 | loop fusion | flops 256 | bytes 320 | tf_op jit(solution)/shard_map/lt | solution.py:185
  1.4 0.8 %convert_reduce_fusion = f32[16,16]{1,0:T(8,128)S(1)} fusion(s32[16,16]{1,0:T(8,128)} %param.10, pred[16,16]{1,0:T(8,128)(4,1)S(1)} %iota_compare_fusion.1), kind=kLoop, calls=%fused_computation.1 | loop fusion | flops 16128 | bytes 2304 | tf_op jit(solution)/shard_map/reduce_max | solution.py:188
  2.2 0.1 copy.14
  2.2 0.1 copy.15
  2.3 0.1 reshape.60
  2.4 0.5 %copy-done.1 = f32[16,256]{1,0:T(8,128)S(1)} copy-done((f32[16,256]{1,0:T(8,128)S(1)}, f32[16,256]{1,0:T(8,128)}, u32[]{:S(2)}) %copy-start.1) | copy-done | bytes 16408
  3.0 0.1 reshape.55
  3.1 0.0 copy-start.3
  3.1 0.1 reshape.56
  3.2 0.0 copy-start.2
  3.2 0.5 %copy-done.3 = f32[1,256]{1,0:T(1,128)S(1)} copy-done((f32[1,256]{1,0:T(1,128)S(1)}, f32[1,256]{1,0:T(1,128)}, u32[]{:S(2)}) %copy-start.3) | copy-done | bytes 1048
  3.8 0.1 copy-done.2
  3.9 0.1 pad.5.clone
  4.0 0.1 maximum_maximum_fusion
  4.1 16.2 %all_to_all.5.refs_0_ = f32[16,24,128]{2,1,0:T(8,128)S(1)} all-to-all(f32[16,24,128]{2,1,0:T(8,128)S(1)} %bitcast.12), channel_id=1, replica_groups=mesh['groups'=2,'tile'=16] {'tile'}, dimensions={0} | all-to-all | bytes 393216 | tf_op jit(solution)/shard_map/all_to_all | solution.py:196
  20.3 3.5 %first_iteration.1.refs_2_ = f32[16,256]{1,0:T(8,128)S(1)} custom-call(f32[16,24,128]{2,1,0:T(8,128)S(1)} %all_to_all.5.refs_0_, f32[16,2,256]{2,1,0:T(2,128)S(1)} %copy-done), custom_call_target="tpu_custom_call" | custom-call | tf_op jit(solution)/shard_map/first_iteration/pallas_call | solution.py:204
  23.8 0.1 collective-permute-start
  23.9 1.2 %collective-permute-done.refs_3_ = f32[16,256]{1,0:T(8,128)S(1)} collective-permute-done((f32[16,256]{1,0:T(8,128)S(1)}, f32[16,256]{1,0:T(8,128)S(1)}, u32[]{:S(2)}, u32[]{:S(2)}) %collective-permute-start) | collective-permute-done | bytes 16416 | tf_op jit(solution)/shard_map/ppermute | solution.py:212
  25.0 2.5 %second_iteration.1 = (f32[24,128]{1,0:T(8,128)S(1)}, f32[24,128]{1,0:T(8,128)S(1)}) custom-call(f32[16,24,128]{2,1,0:T(8,128)S(1)} %all_to_all.5.refs_0_, f32[16,2,256]{2,1,0:T(2,128)S(1)} %copy-done, f32[16,256]{1,0:T(8,128)S(1)} %first_iteration.1.refs_2_, f32[16,256]{1,0:T(8,128)S(1)} %collective-permute-done.refs_3_), custom_call_target="tpu_custom_call" | custom-call | tf_op jit(solution)/shard_map/second_iteration/pallas_call | solution.py:213
  27.6 0.2 collective-permute-start.1
  27.8 1.0 %collective-permute-done.1 = f32[24,128]{1,0:T(8,128)S(1)} collective-permute-done((f32[24,128]{1,0:T(8,128)S(1)}, f32[24,128]{1,0:T(8,128)S(1)}, u32[]{:S(2)}, u32[]{:S(2)}) %collective-permute-start.1) | collective-permute-done | bytes 12320 | tf_op jit(solution)/shard_map/ppermute | solution.py:223
  28.8 0.1 reshape.62
  29.0 0.7 %reshape.63 = f32[16,256]{1,0:T(8,128)} reshape(f32[16,16,16]{2,1,0:T(8,128)S(1)} %copy.17) | data formatting | bytes 32768 | tf_op jit(solution)/shard_map/reshape | solution.py:228
  29.7 0.6 %sub.11 = f32[1,256]{1,0:T(1,128)} subtract(f32[1,256]{1,0:T(1,128)S(1)} %copy-done.2, f32[1,256]{1,0:T(1,128)S(1)} %bitcast.17) | non-fusion elementwise | flops 256 | bytes 3072 | tf_op jit(solution)/shard_map/sub | solution.py:230
  (13 shorter events, 0.1 us)
Async XLA Ops:
  2.2 0.7 %copy-start.1 = (f32[16,256]{1,0:T(8,128)S(1)}, f32[16,256]{1,0:T(8,128)}, u32[]{:S(2)}) copy-start(f32[16,256]{1,0:T(8,128)} %param.6) | copy-start | bytes 49156
  3.1 0.7 %copy-start.3 = (f32[1,256]{1,0:T(1,128)S(1)}, f32[1,256]{1,0:T(1,128)}, u32[]{:S(2)}) copy-start(f32[1,256]{1,0:T(1,128)} %param.8) | copy-start | bytes 3076
  3.2 0.7 %copy-start.2 = (f32[1,256]{1,0:T(1,128)S(1)}, f32[1,256]{1,0:T(1,128)}, u32[]{:S(2)}) copy-start(f32[1,256]{1,0:T(1,128)} %param.7) | copy-start | bytes 3076
  4.1 16.2 %copy-start = (f32[16,2,256]{2,1,0:T(2,128)S(1)}, f32[16,2,256]{2,1,0:T(2,128)}, u32[]{:S(2)}) copy-start(f32[16,2,256]{2,1,0:T(2,128)} %refs_1_.3) | copy-start | bytes 98308
  23.8 1.2 %collective-permute-start = (f32[16,256]{1,0:T(8,128)S(1)}, f32[16,256]{1,0:T(8,128)S(1)}, u32[]{:S(2)}, u32[]{:S(2)}) collective-permute-start(f32[16,256]{1,0:T(8,128)S(1)} %first_iteration.1.refs_2_), channel_id=1, source_target_pairs={{0,1},{1,0},{2,3},{3,2},{4,5},{5,4},{6,7},{7,6},{8,9},{9,8},{10,11... | collective-permute-start | bytes 49160 | tf_op jit(solution)/shard_map/ppermute | solution.py:212
  27.6 1.2 %collective-permute-start.1 = (f32[24,128]{1,0:T(8,128)S(1)}, f32[24,128]{1,0:T(8,128)S(1)}, u32[]{:S(2)}, u32[]{:S(2)}) collective-permute-start(f32[24,128]{1,0:T(8,128)S(1)} %get-tuple-element.5), channel_id=1, source_target_pairs={{0,1},{1,0},{2,3},{3,2},{4,5},{5,4},{6,7},{7,6},{8,9},{9,8},{10,11... | collective-permute-start | bytes 36872 | tf_op jit(solution)/shard_map/ppermute | solution.py:223

commit v3 on v2

--- a/solution.py
+++ b/solution.py
@@ -118,6 +118,75 @@
     return best + jnp.log(total)
 
 
+def log_add(a, b):
+    top = jnp.maximum(a, b)
+    return top + jnp.log(jnp.exp(a - top) + jnp.exp(b - top))
+
+
+def swap_minor(values):
+    lane_group = lax.broadcasted_iota(jnp.int32, (TSIDE, HALF), 1) // TSIDE
+    diagonal = lane_group[:COLS_HALF] == lax.broadcasted_iota(jnp.int32, (COLS_HALF, HALF), 0)
+    result = []
+    for b in range(TSIDE):
+        start = b // COLS_HALF * HALF
+        piece = jnp.where(lane_group == b % COLS_HALF, values[:, start : start + HALF], 0.0)
+        for shift in (TSIDE, 2 * TSIDE, 4 * TSIDE):
+            piece = piece + pltpu.roll(piece, shift, 1)
+        halves = [
+            jnp.sum(jnp.where(diagonal, piece[start : start + COLS_HALF], 0.0), axis=0, keepdims=True)
+            for start in (0, COLS_HALF)
+        ]
+        result.append(halves)
+    return result
+
+
+def pack_kernel(devices, *refs):
+    sources, message_ref, targets, sems = refs[:5], refs[5], refs[6:11], refs[11]
+    copies = [
+        pltpu.make_async_copy(source, target, sems.at[i])
+        for i, (source, target) in enumerate(zip(sources, targets, strict=True))
+    ]
+    for copy in copies:
+        copy.start()
+    for copy in copies:
+        copy.wait()
+    demand_ref, cap_ref, pot_ref, pair_ref, count_ref = targets
+    tiles = 2 * COLS_HALF
+    tile_of = lax.broadcasted_iota(jnp.int32, (tiles, tiles), 0)
+    lane_of = lax.broadcasted_iota(jnp.int32, (tiles, tiles), 1)
+    counts = jnp.sum(jnp.where(tile_of == lane_of, count_ref[...], 0), axis=1, keepdims=True)
+    pairs = jnp.where(lax.broadcasted_iota(jnp.int32, (tiles, KSLOTS), 1) < counts, pair_ref[...], -1)
+    lanes = lax.broadcasted_iota(jnp.int32, (tiles, HALF), 1)
+    found = lanes < 0
+    for slot in range(KSLOTS):
+        found = found | (pairs[:, slot : slot + 1] == lanes // COLS_HALF)
+    own = lax.broadcasted_iota(jnp.int32, (tiles, HALF), 0) % COLS_HALF == lanes % COLS_HALF
+    marks = jnp.where(found & own, 1.0, 0.0)
+    grid_rows = swap_minor(demand_ref[...])
+    tails = jnp.zeros((ROWS - ROW_MASK - 1, HALF), jnp.float32)
+    for half in (0, 1):
+        mark = jnp.sum(marks[half * COLS_HALF : (half + 1) * COLS_HALF], axis=0, keepdims=True)
+        pieces = [row[half] for row in grid_rows]
+        pieces += [pot_ref[:, :HALF], pot_ref[:, HALF:], cap_ref[:, :HALF], cap_ref[:, HALF:], mark, tails]
+        block = jnp.concatenate(pieces, axis=0)
+        for device in range(half, devices, 2):
+            message_ref[device] = block
+
+
+def unpack_kernel(keep_ref, got_ref, cell_ref, fac_ref):
+    is_left = lax.axis_index("tile") % 2 == 0
+    keep = keep_ref[:TSIDE, :]
+    got = got_ref[:TSIDE, :]
+    grid = jnp.concatenate([jnp.where(is_left, keep, got), jnp.where(is_left, got, keep)], axis=1)
+    for row, halves in enumerate(swap_minor(grid)):
+        cell_ref[row : row + 1, :HALF] = halves[0]
+        cell_ref[row : row + 1, HALF:] = halves[1]
+    total = log_add(keep_ref[ROW_POT : ROW_POT + 2, :], got_ref[ROW_POT : ROW_POT + 2, :])
+    fac = keep_ref[ROW_CAP : ROW_CAP + 2, :] - total
+    fac_ref[:, :HALF] = fac[0:1]
+    fac_ref[:, HALF:] = fac[1:2]
+
+
 def first_kernel(rows, blocks, recv_ref, xy_ref, part_ref, mask_ref, top_ref, xf_ref, acc_ref):
     core = lax.axis_index("tile") % 2
     build_mask(recv_ref, mask_ref, rows, blocks)
@@ -138,11 +207,6 @@
         return carry
 
     lax.fori_loop(0, blocks, columns, 0, unroll=True)
-
-
-def log_add(a, b):
-    top = jnp.maximum(a, b)
-    return top + jnp.log(jnp.exp(a - top) + jnp.exp(b - top))
 
 
 def second_kernel(
@@ -172,27 +236,26 @@
         )
         out_ref[ROW_POT : ROW_POT + 1, :] = part[:, :HALF]
         out_ref[ROW_POT + 1 : ROW_POT + 2, :] = part[:, HALF:]
-        out_ref[ROW_POT + 2 :, :] = jnp.zeros((ROWS - ROW_POT - 2, HALF), jnp.float32)
+        out_ref[ROW_CAP:, :] = recv_ref[row, ROW_CAP:, :]
 
 
 def on_device_all_rows(log_demand, log_capacity, warm_potential, facility_xy, pair_block, pair_count):
     devices = lax.axis_size("tile")
-    me = lax.axis_index("tile")
     rows = devices
     blocks = facility_xy.shape[0]
     width = log_capacity.shape[1]
-    demand = log_demand.reshape(TILE_COLS, TSIDE, TSIDE).transpose(1, 0, 2).reshape(TSIDE, 2, HALF)
-    active = jnp.arange(KSLOTS, dtype=jnp.int32)[None, :] < pair_count[:, None]
-    block_ids = jnp.arange(blocks, dtype=jnp.int32)
-    hits = (pair_block[None] == block_ids[:, None, None]) & active[None]
-    marks = jnp.max(hits.astype(jnp.float32), axis=2)
-    marks = marks.reshape(blocks, 2, COLS_HALF).transpose(1, 0, 2).reshape(2, 1, HALF)
-    small = jnp.concatenate([warm_potential.reshape(2, HALF), log_capacity.reshape(2, HALF)], axis=0)
-    small = jnp.broadcast_to(small[None], (2, 4, HALF))
-    message = jnp.concatenate(
-        [demand.transpose(1, 0, 2), small, marks, jnp.zeros((2, ROWS - ROW_MASK - 1, HALF), jnp.float32)], axis=1
-    )
-    message = jnp.broadcast_to(message[None], (devices // 2, 2, ROWS, HALF)).reshape(devices, ROWS, HALF)
+    light = pltpu.CompilerParams(vmem_limit_bytes=4 * 1024 * 1024)
+    local = (log_demand, log_capacity, warm_potential, pair_block, pair_count.reshape(1, -1))
+    local = [pltpu.with_memory_space_constraint(x, pltpu.HBM) for x in local]
+    message = pl.pallas_call(
+        lambda *refs: pack_kernel(devices, *refs),
+        in_specs=[pl.BlockSpec(memory_space=pltpu.HBM)] * len(local),
+        out_shape=jax.ShapeDtypeStruct((devices, ROWS, HALF), jnp.float32),
+        scratch_shapes=[pltpu.VMEM(x.shape, x.dtype) for x in local]
+        + [pltpu.SemaphoreType.DMA((len(local),))],
+        compiler_params=light,
+        name="pack",
+    )(*local)
     recv = lax.all_to_all(message, "tile", 0, 0, tiled=True)
     scratch = [
         pltpu.VMEM((blocks, rows, HALF), jnp.float32),
@@ -200,7 +263,7 @@
         pltpu.VMEM((blocks, 2 * HALF, width), jnp.bfloat16),
         pltpu.VMEM((rows, TSIDE, HALF), jnp.float32),
     ]
-    params = pltpu.CompilerParams(vmem_limit_bytes=48 * 1024 * 1024)
+    params = pltpu.CompilerParams(vmem_limit_bytes=32 * 1024 * 1024)
     part = pl.pallas_call(
         lambda *refs: first_kernel(rows, blocks, *refs),
         out_shape=jax.ShapeDtypeStruct((blocks, width), jnp.float32),
@@ -221,13 +284,15 @@
         name="second_iteration",
     )(recv, facility_xy, part, other)
     got = lax.ppermute(send, "tile", swap)
-    is_left = me % 2 == 0
-    left = jnp.where(is_left, keep, got)
-    right = jnp.where(is_left, got, keep)
-    cells = jnp.concatenate([left[:TSIDE], right[:TSIDE]], axis=1)
-    cell_pot = cells.reshape(TSIDE, TILE_COLS, TSIDE).transpose(1, 0, 2).reshape(TILE_COLS, TSIDE * TSIDE)
-    total = log_add(keep[ROW_POT : ROW_POT + 2], got[ROW_POT : ROW_POT + 2])
-    facility_pot = log_capacity - total.reshape(1, width)
+    cell_pot, facility_pot = pl.pallas_call(
+        unpack_kernel,
+        out_shape=(
+            jax.ShapeDtypeStruct(log_demand.shape, jnp.float32),
+            jax.ShapeDtypeStruct(log_capacity.shape, jnp.float32),
+        ),
+        compiler_params=light,
+        name="unpack",
+    )(keep, got)
     return (cell_pot, facility_pot)
 
 

time: 30.6 us -> 27.6 us (0.902)
  local copies, waits for them, and re-layouts: 2.66 us -> 0.01 us
  other arithmetic: 2.22 us -> 0 us
  Pallas kernels: 5.99 us -> 7.99 us
    pallas_call x0 -> x2, Pallas kernels: none -> 2 us  [the longest x1 1.14 us: on_device_all_rows(): pl.pallas_call(lambda *refs: pack_kernel(devices, *refs), in_specs=[pl.Bl...]
    unnamed x8 -> x2, local copies, waits for them, and re-layouts: 1.23 us -> 0.01 us
    reshape x6 -> x0, local copies, waits for them, and re-layouts: 1.14 us -> none  [the longest x2 0.81 us: on_device_all_rows(): cells.reshape(TSIDE, TILE_COLS, TSIDE).transpose(1, 0, 2)]
    reduce_max x1 -> x0, other arithmetic: 0.8 us -> none  [on_device_all_rows(): marks = jnp.max(hits.astype(jnp.float32), axis=2)]
    lt x1 -> x0, other arithmetic: 0.73 us -> none  [on_device_all_rows(): active = jnp.arange(KSLOTS, dtype=jnp.int32)[None, :] < pair_count[:, None]]
    sub x1 -> x0, other arithmetic: 0.58 us -> none  [on_device_all_rows(): facility_pot = log_capacity - total.reshape(1, width)]
where the time goes in v3:
time: 27.6 us; the launch traced here: 27.3 us
  blocking collectives  16.2 us (59%)
  Pallas kernels  7.99 us (29%)
  waiting for transfers between devices  2.18 us (8%)
  between operations  0.67 us (2%)
  starting transfers between devices  0.3 us (1%)
    all_to_all x1, blocking collectives, on_device_all_rows(): recv = lax.all_to_all(message, 'tile', 0, 0, tiled=True)  16.2 us
    pallas_call x1, Pallas kernels, on_device_all_rows(): pl.pallas_call(lambda *refs: first_kernel(rows, blocks, *refs), out_shape...  3.48 us
    pallas_call x1, Pallas kernels, on_device_all_rows(): pl.pallas_call(lambda *refs: second_kernel(rows, blocks, *refs), out_shap...  2.51 us
    ppermute x1, waiting for transfers between devices, on_device_all_rows(): other = lax.ppermute(part, 'tile', swap)  1.17 us
    pallas_call x1, Pallas kernels, on_device_all_rows(): pl.pallas_call(lambda *refs: pack_kernel(devices, *refs), in_specs=[pl.Bl...  1.14 us
    ppermute x1, waiting for transfers between devices, on_device_all_rows(): got = lax.ppermute(send, 'tile', swap)  1.01 us
    pallas_call x1, Pallas kernels, on_device_all_rows(): pl.pallas_call(unpack_kernel, out_shape=(jax.ShapeDtypeStruct(log_demand....  0.86 us
  transfers between devices with their start and end apart: 2, of which 2 were waited for; matrix products, arithmetic and copies ran while one was open for 0% of the time, Pallas kernels for 0%

profile of v3, /device:TPU:0, one launch (start us, length us, event | category | flops | bytes accessed | tf_op | source)
XLA Modules:
  0.0 27.3 jit_solution(5964245962240229890)
XLA Ops:
  0.6 1.1 %pack.1 = f32[16,24,128]{2,1,0:T(8,128)S(1)} custom-call(f32[16,256]{1,0:T(8,128)} %refs_0_.1, f32[1,256]{1,0:T(1,128)} %refs_1_.3, f32[1,256]{1,0:T(1,128)} %refs_2_.1, s32[16,16]{1,0:T(8,128)} %refs_3_.1, s32[1,16]{1,0:T(1,128)} %bitcast.1), custom_call_target="tpu_custom_call" | custom-call | tf_op jit(solution)/shard_map/pack/pallas_call | solution.py:250
  1.8 0.0 copy-start
  1.8 16.2 %all_to_all.5.refs_0_ = f32[16,24,128]{2,1,0:T(8,128)S(1)} all-to-all(f32[16,24,128]{2,1,0:T(8,128)S(1)} %pack.1), channel_id=1, replica_groups=mesh['groups'=2,'tile'=16] {'tile'}, dimensions={0} | all-to-all | bytes 393216 | tf_op jit(solution)/shard_map/all_to_all | solution.py:259
  17.9 0.0 copy-done
  17.9 3.5 %first_iteration.1.refs_2_ = f32[16,256]{1,0:T(8,128)S(1)} custom-call(f32[16,24,128]{2,1,0:T(8,128)S(1)} %all_to_all.5.refs_0_, f32[16,2,256]{2,1,0:T(2,128)S(1)} %copy-done), custom_call_target="tpu_custom_call" | custom-call | tf_op jit(solution)/shard_map/first_iteration/pallas_call | solution.py:267
  21.4 0.1 collective-permute-start
  21.5 1.2 %collective-permute-done.refs_3_ = f32[16,256]{1,0:T(8,128)S(1)} collective-permute-done((f32[16,256]{1,0:T(8,128)S(1)}, f32[16,256]{1,0:T(8,128)S(1)}, u32[]{:S(2)}, u32[]{:S(2)}) %collective-permute-start) | collective-permute-done | bytes 16416 | tf_op jit(solution)/shard_map/ppermute | solution.py:275
  22.7 2.5 %second_iteration.1 = (f32[24,128]{1,0:T(8,128)S(1)}, f32[24,128]{1,0:T(8,128)S(1)}) custom-call(f32[16,24,128]{2,1,0:T(8,128)S(1)} %all_to_all.5.refs_0_, f32[16,2,256]{2,1,0:T(2,128)S(1)} %copy-done, f32[16,256]{1,0:T(8,128)S(1)} %first_iteration.1.refs_2_, f32[16,256]{1,0:T(8,128)S(1)} %collective-permute-done.refs_3_), custom_call_target="tpu_custom_call" | custom-call | tf_op jit(solution)/shard_map/second_iteration/pallas_call | solution.py:276
  25.2 0.2 collective-permute-start.1
  25.4 1.0 %collective-permute-done.1.got_ref = f32[24,128]{1,0:T(8,128)S(1)} collective-permute-done((f32[24,128]{1,0:T(8,128)S(1)}, f32[24,128]{1,0:T(8,128)S(1)}, u32[]{:S(2)}, u32[]{:S(2)}) %collective-permute-start.1) | collective-permute-done | bytes 12320 | tf_op jit(solution)/shard_map/ppermute | solution.py:286
  26.4 0.9 %unpack.1 = (f32[16,256]{1,0:T(8,128)}, f32[1,256]{1,0:T(1,128)}) custom-call(f32[24,128]{1,0:T(8,128)S(1)} %get-tuple-element.4.keep_ref, f32[24,128]{1,0:T(8,128)S(1)} %collective-permute-done.1.got_ref), custom_call_target="tpu_custom_call" | custom-call | tf_op jit(solution)/shard_map/unpack/pallas_call | solution.py:287
Async XLA Ops:
  1.8 16.2 %copy-start = (f32[16,2,256]{2,1,0:T(2,128)S(1)}, f32[16,2,256]{2,1,0:T(2,128)}, u32[]{:S(2)}) copy-start(f32[16,2,256]{2,1,0:T(2,128)} %refs_1_.5) | copy-start | bytes 98308
  21.4 1.2 %collective-permute-start = (f32[16,256]{1,0:T(8,128)S(1)}, f32[16,256]{1,0:T(8,128)S(1)}, u32[]{:S(2)}, u32[]{:S(2)}) collective-permute-start(f32[16,256]{1,0:T(8,128)S(1)} %first_iteration.1.refs_2_), channel_id=1, source_target_pairs={{0,1},{1,0},{2,3},{3,2},{4,5},{5,4},{6,7},{7,6},{8,9},{9,8},{10,11... | collective-permute-start | bytes 49160 | tf_op jit(solution)/shard_map/ppermute | solution.py:275
  25.2 1.2 %collective-permute-start.1 = (f32[24,128]{1,0:T(8,128)S(1)}, f32[24,128]{1,0:T(8,128)S(1)}, u32[]{:S(2)}, u32[]{:S(2)}) collective-permute-start(f32[24,128]{1,0:T(8,128)S(1)} %get-tuple-element.5), channel_id=1, source_target_pairs={{0,1},{1,0},{2,3},{3,2},{4,5},{5,4},{6,7},{7,6},{8,9},{9,8},{10,11... | collective-permute-start | bytes 36872 | tf_op jit(solution)/shard_map/ppermute | solution.py:286

commit v4 on v3

--- a/solution.py
+++ b/solution.py
@@ -19,10 +19,13 @@
 COLS_HALF = TILE_COLS // 2
 SCALE = 1.0 / float(REACH * REACH)
 MIDDLE = 736.0
-ROW_POT = TSIDE
-ROW_CAP = TSIDE + 2
-ROW_MASK = TSIDE + 4
-ROWS = TSIDE + 8
+TAIL = 8
+ROWS = 2 * TSIDE + TAIL
+KEEP_ROWS = TSIDE + TAIL
+ROW_POT = 0
+ROW_CAP = 2
+ROW_MASK = 4
+STEP = 4
 
 
 def dot_nt(a, b):
@@ -39,80 +42,108 @@
     return high, low
 
 
-def center_cost(xy_ref, block, core, rows):
-    fx = xy_ref[block, 0:1, :]
-    fy = xy_ref[block, 1:2, :]
-    x_mid = (core * HALF).astype(jnp.float32) + 0.5 * HALF
-    y_mid = (lax.broadcasted_iota(jnp.int32, (rows, 1), 0) * TSIDE).astype(jnp.float32) + 0.5 * TSIDE
-    dx = x_mid - fx
-    dy = y_mid - fy
-    return (dx * dx + dy * dy) * SCALE
-
-
-def y_factor(xy_ref, block):
-    offset = lax.broadcasted_iota(jnp.int32, (TSIDE, 1), 0).astype(jnp.float32) - 0.5 * (TSIDE - 1)
-    return jnp.exp(offset * ((xy_ref[block, 1:2, :] - MIDDLE) * (2.0 * SCALE)))
-
-
-def x_factor(xy_ref, block):
-    offset = lax.broadcasted_iota(jnp.int32, (HALF, 1), 0).astype(jnp.float32) - 0.5 * (HALF - 1)
-    return jnp.exp(offset * ((xy_ref[block, 0:1, :] - MIDDLE) * (2.0 * SCALE)))
-
-
-def build_mask(recv_ref, mask_ref, rows, blocks):
-    marks = recv_ref[:, ROW_MASK, :]
-    lane_block = lax.broadcasted_iota(jnp.int32, (blocks, rows, HALF), 2) // COLS_HALF
-    own_block = lax.broadcasted_iota(jnp.int32, (blocks, rows, HALF), 0)
+def halves_of(row_pair):
+    return jnp.concatenate([row_pair[0:1, :], row_pair[1:2, :]], axis=1)
+
+
+class Gathered:
+    def __init__(self, refs):
+        self.refs = refs
+        self.slots = range(len(refs) * refs[0].shape[0])
+
+    def block_of(self, slot, first, rows):
+        return self.refs[slot % STEP][slot // STEP, first : first + rows, :]
+
+    def demand(self, slot):
+        return self.block_of(slot, TAIL if slot % 2 else 0, TSIDE)
+
+    def tail(self, slot):
+        return self.block_of(slot, 0 if slot % 2 else TSIDE, TAIL)
+
+    def potential(self, slot):
+        return halves_of(self.tail(slot)[ROW_POT : ROW_POT + 2])
+
+    def capacity(self, slot):
+        return halves_of(self.tail(slot)[ROW_CAP : ROW_CAP + 2])
+
+    def mask(self, slot):
+        row = ROW_MASK + slot % 2
+        return self.tail(slot)[row : row + 1]
+
+
+def setup_kernel(slots, xy_ref, xf_ref, yf_ref, cost_ref):
+    me = lax.axis_index("tile")
+    x_mid = (me % 2 * HALF).astype(jnp.float32) + 0.5 * HALF
+    row_ids = me ^ lax.broadcasted_iota(jnp.int32, (slots, 1), 0)
+    y_mid = (row_ids * TSIDE).astype(jnp.float32) + 0.5 * TSIDE
+    x_off = lax.broadcasted_iota(jnp.int32, (HALF, 1), 0).astype(jnp.float32) - 0.5 * (HALF - 1)
+    y_off = lax.broadcasted_iota(jnp.int32, (TSIDE, 1), 0).astype(jnp.float32) - 0.5 * (TSIDE - 1)
+    for slot in range(slots):
+        block = me ^ slot
+        fx = xy_ref[block, 0:1, :]
+        fy = xy_ref[block, 1:2, :]
+        high, low = split(jnp.exp(x_off * ((fx - MIDDLE) * (2.0 * SCALE))))
+        xf_ref[slot, :HALF, :] = high
+        xf_ref[slot, HALF:, :] = low
+        yf_ref[slot] = jnp.exp(y_off * ((fy - MIDDLE) * (2.0 * SCALE)))
+        dx = x_mid - fx
+        dy = y_mid - fy
+        cost_ref[slot] = (dx * dx + dy * dy) * SCALE
+
+
+def build_mask(gathered, me, mask_ref):
+    slots = len(gathered.slots)
+    marks = jnp.concatenate([gathered.mask(slot) for slot in gathered.slots], axis=0)
+    lane_block = lax.broadcasted_iota(jnp.int32, (slots, slots, HALF), 2) // COLS_HALF
+    own_block = lax.broadcasted_iota(jnp.int32, (slots, slots, HALF), 0) ^ me
     picked = jnp.where(lane_block == own_block, marks[None], 0.0)
-    picked = picked.reshape(blocks * rows, HALF).astype(jnp.bfloat16)
+    picked = picked.reshape(slots * slots, HALF).astype(jnp.bfloat16)
     source = lax.broadcasted_iota(jnp.int32, (HALF, HALF), 0) % COLS_HALF
     target = lax.broadcasted_iota(jnp.int32, (HALF, HALF), 1) // TSIDE
     spread = jnp.where(source == target, 1.0, 0.0).astype(jnp.bfloat16)
-    mask_ref[...] = dot_nn(picked, spread).reshape(blocks, rows, HALF)
-
-
-def row_pass(recv_ref, xy_ref, pot_of, mask_ref, top_ref, xf_ref, acc_ref, core, rows, blocks):
-    def tops(block, best):
-        scores = pot_of(block) - center_cost(xy_ref, block, core, rows)
-        top = jnp.broadcast_to(jnp.max(scores, axis=1, keepdims=True), (rows, HALF))
-        top_ref[block] = top
-        return jnp.maximum(best, jnp.where(mask_ref[block] > 0.0, top, LOWEST))
-
-    best = lax.fori_loop(0, blocks, tops, jnp.full((rows, HALF), LOWEST, jnp.float32), unroll=True)
-    acc_ref[...] = jnp.zeros_like(acc_ref)
-
-    def sums(block, carry):
-        high, low = split(x_factor(xy_ref, block))
-        xf_ref[block, :HALF, :] = high
-        xf_ref[block, HALF:, :] = low
-        top = top_ref[block]
-        scores = pot_of(block) - center_cost(xy_ref, block, core, rows)
-        weight = jnp.exp(scores - top[:, 0:1])
-        lhs = weight[:, None, :] * y_factor(xy_ref, block)[None]
-        a_high, a_low = split(lhs.reshape(rows * TSIDE, lhs.shape[-1]))
-        both = dot_nt(a_high, xf_ref[block])
-        third = dot_nt(a_low, xf_ref[block, :HALF, :])
+    mask_ref[...] = dot_nn(picked, spread).reshape(slots, slots, HALF)
+
+
+def row_pass(gathered, potential, factors, mask_ref, acc_ref):
+    xf_ref, yf_ref, cost_ref = factors
+    slots = len(gathered.slots)
+    best = jnp.full((slots, HALF), LOWEST, jnp.float32)
+    tops = []
+    for slot in gathered.slots:
+        top = jnp.max(potential(slot) - cost_ref[slot], axis=1, keepdims=True)
+        tops.append(top)
+        best = jnp.maximum(best, jnp.where(mask_ref[slot] > 0.0, top, LOWEST))
+    for slot in gathered.slots:
+        top = tops[slot]
+        weight = jnp.exp(potential(slot) - cost_ref[slot] - top)
+        lhs = weight[:, None, :] * yf_ref[slot][None]
+        a_high, a_low = split(lhs.reshape(slots * TSIDE, lhs.shape[-1]))
+        both = dot_nt(a_high, xf_ref[slot])
+        third = dot_nt(a_low, xf_ref[slot, :HALF, :])
         part = both[:, :HALF] + both[:, HALF:] + third
-        scale = jnp.where(mask_ref[block] > 0.0, jnp.exp(jnp.minimum(top - best, 0.0)), 0.0)
-        acc_ref[...] += part.reshape(rows, TSIDE, HALF) * scale[:, None, :]
-        return carry
-
-    lax.fori_loop(0, blocks, sums, 0, unroll=True)
-    demand = recv_ref[:, :TSIDE, :]
+        scale = jnp.where(mask_ref[slot] > 0.0, jnp.exp(jnp.minimum(top - best, 0.0)), 0.0)
+        scaled = part.reshape(slots, TSIDE, HALF) * scale[:, None, :]
+        if slot == 0:
+            acc_ref[...] = scaled
+        else:
+            acc_ref[...] += scaled
+    demand = jnp.concatenate([gathered.demand(slot)[None] for slot in gathered.slots], axis=0)
     return demand - best[:, None, :] - jnp.log(acc_ref[...])
 
 
-def column_part(xy_ref, mask_ref, xf_ref, level, base, block, core, rows):
-    active = mask_ref[block] > 0.0
+def column_part(factors, mask_ref, level, base, slot):
+    xf_ref, yf_ref, cost_ref = factors
+    slots = level.shape[0]
+    active = mask_ref[slot] > 0.0
     top = jnp.max(jnp.where(active, level, LOWEST), axis=1, keepdims=True)
     scale = jnp.where(active, jnp.exp(jnp.minimum(level - top, 0.0)), 0.0)
-    weights = (base * scale[:, None, :]).reshape(rows * TSIDE, HALF)
+    weights = (base * scale[:, None, :]).reshape(slots * TSIDE, HALF)
     w_high, w_low = split(weights)
-    mixed = dot_nn(jnp.concatenate([w_high, w_high], axis=1), xf_ref[block])
-    mixed = mixed + dot_nn(w_low, xf_ref[block, :HALF, :])
+    mixed = dot_nn(jnp.concatenate([w_high, w_high], axis=1), xf_ref[slot])
+    mixed = mixed + dot_nn(w_low, xf_ref[slot, :HALF, :])
     width = mixed.shape[-1]
-    sums = jnp.sum(mixed.reshape(rows, TSIDE, width) * y_factor(xy_ref, block)[None], axis=1)
-    tops = top - center_cost(xy_ref, block, core, rows)
+    sums = jnp.sum(mixed.reshape(slots, TSIDE, width) * yf_ref[slot][None], axis=1)
+    tops = top - cost_ref[slot]
     best = jnp.max(tops, axis=0, keepdims=True)
     total = jnp.sum(sums * jnp.exp(tops - best), axis=0, keepdims=True)
     return best + jnp.log(total)
@@ -140,7 +171,7 @@
     return result
 
 
-def pack_kernel(devices, *refs):
+def pack_kernel(*refs):
     sources, message_ref, targets, sems = refs[:5], refs[5], refs[6:11], refs[11]
     copies = [
         pltpu.make_async_copy(source, target, sems.at[i])
@@ -163,14 +194,15 @@
     own = lax.broadcasted_iota(jnp.int32, (tiles, HALF), 0) % COLS_HALF == lanes % COLS_HALF
     marks = jnp.where(found & own, 1.0, 0.0)
     grid_rows = swap_minor(demand_ref[...])
-    tails = jnp.zeros((ROWS - ROW_MASK - 1, HALF), jnp.float32)
-    for half in (0, 1):
-        mark = jnp.sum(marks[half * COLS_HALF : (half + 1) * COLS_HALF], axis=0, keepdims=True)
-        pieces = [row[half] for row in grid_rows]
-        pieces += [pot_ref[:, :HALF], pot_ref[:, HALF:], cap_ref[:, :HALF], cap_ref[:, HALF:], mark, tails]
-        block = jnp.concatenate(pieces, axis=0)
-        for device in range(half, devices, 2):
-            message_ref[device] = block
+    is_left = lax.axis_index("tile") % 2 == 0
+    tops = [jnp.sum(marks[start : start + COLS_HALF], axis=0, keepdims=True) for start in (0, COLS_HALF)]
+    sides = [jnp.concatenate([row[half] for row in grid_rows], axis=0) for half in (0, 1)]
+    message_ref[:TSIDE, :] = jnp.where(is_left, sides[0], sides[1])
+    message_ref[TSIDE + TAIL :, :] = jnp.where(is_left, sides[1], sides[0])
+    pieces = [pot_ref[:, :HALF], pot_ref[:, HALF:], cap_ref[:, :HALF], cap_ref[:, HALF:]]
+    pieces += [jnp.where(is_left, tops[0], tops[1]), jnp.where(is_left, tops[1], tops[0])]
+    pieces += [jnp.zeros((TAIL - ROW_MASK - 2, HALF), jnp.float32)]
+    message_ref[TSIDE : TSIDE + TAIL, :] = jnp.concatenate(pieces, axis=0)
 
 
 def unpack_kernel(keep_ref, got_ref, cell_ref, fac_ref):
@@ -181,110 +213,120 @@
     for row, halves in enumerate(swap_minor(grid)):
         cell_ref[row : row + 1, :HALF] = halves[0]
         cell_ref[row : row + 1, HALF:] = halves[1]
-    total = log_add(keep_ref[ROW_POT : ROW_POT + 2, :], got_ref[ROW_POT : ROW_POT + 2, :])
-    fac = keep_ref[ROW_CAP : ROW_CAP + 2, :] - total
+    tail = keep_ref[TSIDE:, :]
+    total = log_add(tail[ROW_POT : ROW_POT + 2], got_ref[TSIDE + ROW_POT : TSIDE + ROW_POT + 2, :])
+    fac = tail[ROW_CAP : ROW_CAP + 2] - total
     fac_ref[:, :HALF] = fac[0:1]
     fac_ref[:, HALF:] = fac[1:2]
 
 
-def first_kernel(rows, blocks, recv_ref, xy_ref, part_ref, mask_ref, top_ref, xf_ref, acc_ref):
-    core = lax.axis_index("tile") % 2
-    build_mask(recv_ref, mask_ref, rows, blocks)
-
-    def pot_of(block):
-        return jnp.concatenate(
-            [recv_ref[block, ROW_POT : ROW_POT + 1, :], recv_ref[block, ROW_POT + 1 : ROW_POT + 2, :]], axis=1
-        )
-
-    shifted = row_pass(recv_ref, xy_ref, pot_of, mask_ref, top_ref, xf_ref, acc_ref, core, rows, blocks)
+def first_kernel(*refs):
+    gathered = Gathered(refs[:STEP])
+    factors = refs[STEP : STEP + 3]
+    part_ref, mask_ref, acc_ref = refs[STEP + 3 :]
+    build_mask(gathered, lax.axis_index("tile"), mask_ref)
+    shifted = row_pass(gathered, gathered.potential, factors, mask_ref, acc_ref)
     level = jnp.max(shifted, axis=1)
     acc_ref[...] = jnp.exp(shifted - level[:, None, :])
-
-    def columns(block, carry):
-        part_ref[pl.ds(block, 1), :] = column_part(
-            xy_ref, mask_ref, xf_ref, level, acc_ref[...], block, core, rows
-        )
-        return carry
-
-    lax.fori_loop(0, blocks, columns, 0, unroll=True)
-
-
-def second_kernel(
-    rows, blocks, recv_ref, xy_ref, mine_ref, other_ref, keep_ref, send_ref, pot_ref, mask_ref, top_ref, xf_ref, acc_ref
-):
+    for slot in gathered.slots:
+        part_ref[slot : slot + 1, :] = column_part(factors, mask_ref, level, acc_ref[...], slot)
+
+
+def second_kernel(*refs):
+    gathered = Gathered(refs[:STEP])
+    factors = refs[STEP : STEP + 3]
+    mine_ref, other_ref, keep_ref, send_ref, pot_ref, mask_ref, acc_ref = refs[STEP + 3 :]
     me = lax.axis_index("tile")
     core = me % 2
-    build_mask(recv_ref, mask_ref, rows, blocks)
-    capacity = jnp.concatenate([recv_ref[:, ROW_CAP, :], recv_ref[:, ROW_CAP + 1, :]], axis=1)
-    pot_ref[...] = capacity - log_add(mine_ref[...], other_ref[...])
-
-    def pot_of(block):
-        return pot_ref[pl.ds(block, 1), :]
-
-    shifted = row_pass(recv_ref, xy_ref, pot_of, mask_ref, top_ref, xf_ref, acc_ref, core, rows, blocks)
+    build_mask(gathered, me, mask_ref)
+    slots = len(gathered.slots)
+    other = other_ref[...]
+    even = lax.broadcasted_iota(jnp.int32, other.shape, 0) % 2 == 0
+    swapped = jnp.where(even, pltpu.roll(other, slots - 1, 0), pltpu.roll(other, 1, 0))
+    capacity = jnp.concatenate([gathered.capacity(slot) for slot in gathered.slots], axis=0)
+    pot_ref[...] = capacity - log_add(mine_ref[...], swapped)
+
+    def potential(slot):
+        return pot_ref[slot : slot + 1, :]
+
+    shifted = row_pass(gathered, potential, factors, mask_ref, acc_ref)
     level = jnp.max(shifted, axis=1)
-    acc_ref[...] = shifted
+    base = jnp.exp(shifted - level[:, None, :])
     x_mid = (core * HALF).astype(jnp.float32) + 0.5 * HALF
     dx = lax.broadcasted_iota(jnp.int32, (1, HALF), 1).astype(jnp.float32) - 0.5 * (HALF - 1)
     dy = lax.broadcasted_iota(jnp.int32, (TSIDE, 1), 0).astype(jnp.float32) - 0.5 * (TSIDE - 1)
-    for row, out_ref in ((me, keep_ref), (me + 1 - 2 * core, send_ref)):
-        y_mid = (row * TSIDE).astype(jnp.float32) + 0.5 * TSIDE
+    for slot, out_ref in ((0, keep_ref), (1, send_ref)):
+        y_mid = ((me ^ slot) * TSIDE).astype(jnp.float32) + 0.5 * TSIDE
         lift = (dx * (dx + 2.0 * (x_mid - MIDDLE)) + dy * (dy + 2.0 * (y_mid - MIDDLE))) * SCALE
-        out_ref[:TSIDE, :] = acc_ref[row] + lift
-        part = column_part(
-            xy_ref, mask_ref, xf_ref, level, jnp.exp(shifted - level[:, None, :]), row, core, rows
-        )
-        out_ref[ROW_POT : ROW_POT + 1, :] = part[:, :HALF]
-        out_ref[ROW_POT + 1 : ROW_POT + 2, :] = part[:, HALF:]
-        out_ref[ROW_CAP:, :] = recv_ref[row, ROW_CAP:, :]
+        out_ref[:TSIDE, :] = shifted[slot] + lift
+        part = column_part(factors, mask_ref, level, base, slot)
+        pieces = [part[:, :HALF], part[:, HALF:], gathered.tail(slot)[ROW_CAP:]]
+        out_ref[TSIDE:, :] = jnp.concatenate(pieces, axis=0)
+
+
+def exchange(block, distance):
+    devices = lax.axis_size("tile")
+    return lax.ppermute(block, "tile", [(i, i ^ distance) for i in range(devices)])
 
 
 def on_device_all_rows(log_demand, log_capacity, warm_potential, facility_xy, pair_block, pair_count):
-    devices = lax.axis_size("tile")
-    rows = devices
-    blocks = facility_xy.shape[0]
+    slots = lax.axis_size("tile")
     width = log_capacity.shape[1]
     light = pltpu.CompilerParams(vmem_limit_bytes=4 * 1024 * 1024)
+    heavy = pltpu.CompilerParams(vmem_limit_bytes=16 * 1024 * 1024)
     local = (log_demand, log_capacity, warm_potential, pair_block, pair_count.reshape(1, -1))
     local = [pltpu.with_memory_space_constraint(x, pltpu.HBM) for x in local]
     message = pl.pallas_call(
-        lambda *refs: pack_kernel(devices, *refs),
+        pack_kernel,
         in_specs=[pl.BlockSpec(memory_space=pltpu.HBM)] * len(local),
-        out_shape=jax.ShapeDtypeStruct((devices, ROWS, HALF), jnp.float32),
+        out_shape=jax.ShapeDtypeStruct((ROWS, HALF), jnp.float32),
         scratch_shapes=[pltpu.VMEM(x.shape, x.dtype) for x in local]
         + [pltpu.SemaphoreType.DMA((len(local),))],
         compiler_params=light,
         name="pack",
     )(*local)
-    recv = lax.all_to_all(message, "tile", 0, 0, tiled=True)
+    factors = pl.pallas_call(
+        lambda *refs: setup_kernel(slots, *refs),
+        out_shape=(
+            jax.ShapeDtypeStruct((slots, 2 * HALF, width), jnp.bfloat16),
+            jax.ShapeDtypeStruct((slots, TSIDE, width), jnp.float32),
+            jax.ShapeDtypeStruct((slots, slots, width), jnp.float32),
+        ),
+        compiler_params=light,
+        name="setup",
+    )(facility_xy)
+    lines = message[None]
+    distance = STEP
+    while distance < slots:
+        lines = jnp.concatenate([lines, exchange(lines, distance)], axis=0)
+        distance *= 2
+    same = lines[:, :KEEP_ROWS]
+    across = lines[:, TSIDE:]
+    gathered = (lines, exchange(across, 1), exchange(same, 2), exchange(across, 3))
     scratch = [
-        pltpu.VMEM((blocks, rows, HALF), jnp.float32),
-        pltpu.VMEM((blocks, rows, HALF), jnp.float32),
-        pltpu.VMEM((blocks, 2 * HALF, width), jnp.bfloat16),
-        pltpu.VMEM((rows, TSIDE, HALF), jnp.float32),
+        pltpu.VMEM((slots, slots, HALF), jnp.float32),
+        pltpu.VMEM((slots, TSIDE, HALF), jnp.float32),
     ]
-    params = pltpu.CompilerParams(vmem_limit_bytes=32 * 1024 * 1024)
     part = pl.pallas_call(
-        lambda *refs: first_kernel(rows, blocks, *refs),
-        out_shape=jax.ShapeDtypeStruct((blocks, width), jnp.float32),
+        first_kernel,
+        out_shape=jax.ShapeDtypeStruct((slots, width), jnp.float32),
         scratch_shapes=scratch,
-        compiler_params=params,
+        compiler_params=heavy,
         name="first_iteration",
-    )(recv, facility_xy)
-    swap = [(i, i ^ 1) for i in range(devices)]
-    other = lax.ppermute(part, "tile", swap)
+    )(*gathered, *factors)
+    other = exchange(part, 1)
     keep, send = pl.pallas_call(
-        lambda *refs: second_kernel(rows, blocks, *refs),
+        second_kernel,
         out_shape=(
-            jax.ShapeDtypeStruct((ROWS, HALF), jnp.float32),
-            jax.ShapeDtypeStruct((ROWS, HALF), jnp.float32),
+            jax.ShapeDtypeStruct((KEEP_ROWS, HALF), jnp.float32),
+            jax.ShapeDtypeStruct((KEEP_ROWS, HALF), jnp.float32),
         ),
-        scratch_shapes=[pltpu.VMEM((blocks, width), jnp.float32)] + scratch,
-        compiler_params=params,
+        scratch_shapes=[pltpu.VMEM((slots, width), jnp.float32)] + scratch,
+        compiler_params=heavy,
         name="second_iteration",
-    )(recv, facility_xy, part, other)
-    got = lax.ppermute(send, "tile", swap)
-    cell_pot, facility_pot = pl.pallas_call(
+    )(*gathered, *factors, part, other)
+    got = exchange(send, 1)
+    return pl.pallas_call(
         unpack_kernel,
         out_shape=(
             jax.ShapeDtypeStruct(log_demand.shape, jnp.float32),
@@ -293,7 +335,6 @@
         compiler_params=light,
         name="unpack",
     )(keep, got)
-    return (cell_pot, facility_pot)
 
 
 def from_behind(block, axis, distance):

time: 27.6 us -> 25.5 us (0.924)
  blocking collectives: 16.2 us -> 0 us
  starting transfers between devices: 0.3 us -> 8.63 us
  waiting for transfers between devices: 2.18 us -> 7.74 us
  local copies, waits for them, and re-layouts: 0.01 us -> 0.77 us
  Pallas kernels: 7.99 us -> 7.39 us
    all_to_all x1 -> x0, blocking collectives: 16.2 us -> none  [on_device_all_rows(): recv = lax.all_to_all(message, 'tile', 0, 0, tiled=True)]
    ppermute x2 -> x7, starting transfers between devices: 0.3 us -> 8.63 us  [exchange(): lax.ppermute(block, 'tile', [(i, i ^ distance) for i in range(devices)])]
    ppermute x2 -> x7, waiting for transfers between devices: 2.18 us -> 7.74 us  [exchange(): lax.ppermute(block, 'tile', [(i, i ^ distance) for i in range(devices)])]
    unnamed x2, local copies, waits for them, and re-layouts: 0.01 us -> 0.76 us
    pallas_call x3 -> x4, Pallas kernels: 7.13 us -> 6.52 us  [the longest x1 2.97 us: on_device_all_rows(): pl.pallas_call(first_kernel, out_shape=jax.ShapeDtypeStruct((slots, width...]
  transfers between devices with their start and end apart: 2 -> 7, of which waited for: 2 -> 6; matrix products, arithmetic and copies ran while one was open for 0% -> 0% of each run, Pallas kernels for 0% -> 2%
where the time goes in v4:
time: 25.5 us; the launch traced here: 25.2 us
  starting transfers between devices  8.63 us (34%)
  waiting for transfers between devices  7.74 us (30%)
  Pallas kernels  7.39 us (29%)
  local copies, waits for them, and re-layouts  0.77 us (3%)
  between operations  0.67 us (3%)
    ppermute x7, starting transfers between devices, exchange(): lax.ppermute(block, 'tile', [(i, i ^ distance) for i in range(devices)])  8.63 us
    ppermute x7, waiting for transfers between devices, exchange(): lax.ppermute(block, 'tile', [(i, i ^ distance) for i in range(devices)])  7.74 us
    pallas_call x1, Pallas kernels, on_device_all_rows(): pl.pallas_call(first_kernel, out_shape=jax.ShapeDtypeStruct((slots, width...  2.97 us
    pallas_call x1, Pallas kernels, on_device_all_rows(): pl.pallas_call(second_kernel, out_shape=(jax.ShapeDtypeStruct((KEEP_ROWS,...  1.81 us
    pallas_call x1, Pallas kernels, on_device_all_rows(): pl.pallas_call(pack_kernel, in_specs=[pl.BlockSpec(memory_space=pltpu.HBM...  1.13 us
    pallas_call x1, Pallas kernels, on_device_all_rows(): pl.pallas_call(unpack_kernel, out_shape=(jax.ShapeDtypeStruct(log_demand....  0.86 us
    unnamed x2, local copies, waits for them, and re-layouts  0.76 us
    pallas_call x1, Pallas kernels, on_device_all_rows(): pl.pallas_call(lambda *refs: setup_kernel(slots, *refs), out_shape=(jax.S...  0.62 us
  transfers between devices with their start and end apart: 7, of which 6 were waited for; matrix products, arithmetic and copies ran while one was open for 0% of the time, Pallas kernels for 2%

profile of v4, /device:TPU:0, one launch (start us, length us, event | category | flops | bytes accessed | tf_op | source)
XLA Modules:
  0.0 25.2 jit_solution(11257693508951538817)
XLA Ops:
  0.6 1.1 %pack.1 = f32[40,128]{1,0:T(8,128)S(1)} custom-call(f32[16,256]{1,0:T(8,128)} %refs_0_.2, f32[1,256]{1,0:T(1,128)} %refs_1_.1, f32[1,256]{1,0:T(1,128)} %refs_2_.1, s32[16,16]{1,0:T(8,128)} %refs_3_.1, s32[1,16]{1,0:T(1,128)} %bitcast.5), custom_call_target="tpu_custom_call" | custom-call | tf_op jit(solution)/shard_map/pack/pallas_call | solution.py:279
  1.8 3.1 %collective-permute-start = (f32[1,40,128]{2,1,0:T(8,128)S(1)}, f32[1,40,128]{2,1,0:T(8,128)S(1)}, u32[]{:S(2)}, u32[]{:S(2)}) collective-permute-start(f32[1,40,128]{2,1,0:T(8,128)S(1)} %bitcast.2), channel_id=1, source_target_pairs={{0,4},{1,5},{2,6},{3,7},{4,0},{5,1},{6,2},{7,3},{8,12},{9,13},{10,... | collective-permute-start | bytes 61448 | tf_op jit(solution)/shard_map/ppermute | solution.py:269
  4.9 1.8 %collective-permute-done = f32[1,40,128]{2,1,0:T(8,128)S(1)} collective-permute-done((f32[1,40,128]{2,1,0:T(8,128)S(1)}, f32[1,40,128]{2,1,0:T(8,128)S(1)}, u32[]{:S(2)}, u32[]{:S(2)}) %collective-permute-start) | collective-permute-done | bytes 20512 | tf_op jit(solution)/shard_map/ppermute | solution.py:269
  6.6 3.0 %collective-permute-start.1 = (f32[2,40,128]{2,1,0:T(8,128)S(1)}, f32[2,40,128]{2,1,0:T(8,128)S(1)}, u32[]{:S(2)}, u32[]{:S(2)}) collective-permute-start(f32[2,40,128]{2,1,0:T(8,128)S(1)} %pad_maximum_fusion.1), channel_id=1, source_target_pairs={{0,8},{1,9},{2,10},{3,11},{4,12},{5,13},{6,14},{7,15},{8,0},{9,1},... | collective-permute-start | bytes 122888 | tf_op jit(solution)/shard_map/ppermute | solution.py:269
  9.7 2.0 %collective-permute-done.1 = f32[2,40,128]{2,1,0:T(8,128)S(1)} collective-permute-done((f32[2,40,128]{2,1,0:T(8,128)S(1)}, f32[2,40,128]{2,1,0:T(8,128)S(1)}, u32[]{:S(2)}, u32[]{:S(2)}) %collective-permute-start.1) | collective-permute-done | bytes 40992 | tf_op jit(solution)/shard_map/ppermute | solution.py:269
  11.7 1.9 %collective-permute-start.3 = (f32[4,24,128]{2,1,0:T(8,128)S(1)}, f32[4,24,128]{2,1,0:T(8,128)S(1)}, u32[]{:S(2)}, u32[]{:S(2)}) collective-permute-start(f32[4,24,128]{2,1,0:T(8,128)S(1)} %get-tuple-element.12), channel_id=1, source_target_pairs={{0,2},{1,3},{2,0},{3,1},{4,6},{5,7},{6,4},{7,5},{8,10},{9,11},{10,... | collective-permute-start | bytes 147464 | tf_op jit(solution)/shard_map/ppermute | solution.py:269
  13.5 0.0 collective-permute-start.4
  13.6 0.3 %collective-permute-start.2 = (f32[4,24,128]{2,1,0:T(8,128)S(1)}, f32[4,24,128]{2,1,0:T(8,128)S(1)}, u32[]{:S(2)}, u32[]{:S(2)}) collective-permute-start(f32[4,24,128]{2,1,0:T(8,128)S(1)} %get-tuple-element.13), channel_id=1, source_target_pairs={{0,1},{1,0},{2,3},{3,2},{4,5},{5,4},{6,7},{7,6},{8,9},{9,8},{10,11... | collective-permute-start | bytes 147464 | tf_op jit(solution)/shard_map/ppermute | solution.py:269
  13.9 0.0 copy-start
  13.9 0.8 %copy-done = f32[16,2,256]{2,1,0:T(2,128)S(1)} copy-done((f32[16,2,256]{2,1,0:T(2,128)S(1)}, f32[16,2,256]{2,1,0:T(2,128)}, u32[]{:S(2)}) %copy-start) | copy-done | bytes 32792
  14.6 0.6 %setup.1 = (bf16[16,256,256]{2,1,0:T(8,128)(2,1)S(1)}, f32[16,16,256]{2,1,0:T(8,128)S(1)}, f32[16,16,256]{2,1,0:T(8,128)S(1)}) custom-call(f32[16,2,256]{2,1,0:T(2,128)S(1)} %copy-done), custom_call_target="tpu_custom_call" | custom-call | tf_op jit(solution)/shard_map/setup/pallas_call | solution.py:288
  15.2 0.6 %collective-permute-done.3.refs_2_ = f32[4,24,128]{2,1,0:T(8,128)S(1)} collective-permute-done((f32[4,24,128]{2,1,0:T(8,128)S(1)}, f32[4,24,128]{2,1,0:T(8,128)S(1)}, u32[]{:S(2)}, u32[]{:S(2)}) %collective-permute-start.3) | collective-permute-done | bytes 49184 | tf_op jit(solution)/shard_map/ppermute | solution.py:269
  15.8 1.2 %collective-permute-done.4.refs_3_ = f32[4,24,128]{2,1,0:T(8,128)S(1)} collective-permute-done((f32[4,24,128]{2,1,0:T(8,128)S(1)}, f32[4,24,128]{2,1,0:T(8,128)S(1)}, u32[]{:S(2)}, u32[]{:S(2)}) %collective-permute-start.4) | collective-permute-done | bytes 49184 | tf_op jit(solution)/shard_map/ppermute | solution.py:269
  17.1 0.0 collective-permute-done.2.refs_1_
  17.1 3.0 %first_iteration.1.refs_7_ = f32[16,256]{1,0:T(8,128)S(1)} custom-call(f32[4,40,128]{2,1,0:T(8,128)S(1)} %pad_maximum_fusion.refs_0_, f32[4,24,128]{2,1,0:T(8,128)S(1)} %collective-permute-done.2.refs_1_, f32[4,24,128]{2,1,0:T(8,128)S(1)} %collective-permute-done.3.refs_2_, f32[4,24,128]{2,1,0:T(8,128)S(1)} %collective-permute-done.4.refs_3_, ...), custom_call_target="tpu_custom_call" | custom-call | tf_op jit(solution)/shard_map/first_iteration/pallas_call | solution.py:310
  20.0 0.1 collective-permute-start.5
  20.1 1.2 %collective-permute-done.5.refs_8_ = f32[16,256]{1,0:T(8,128)S(1)} collective-permute-done((f32[16,256]{1,0:T(8,128)S(1)}, f32[16,256]{1,0:T(8,128)S(1)}, u32[]{:S(2)}, u32[]{:S(2)}) %collective-permute-start.5) | collective-permute-done | bytes 16416 | tf_op jit(solution)/shard_map/ppermute | solution.py:269
  21.3 1.8 %second_iteration.1 = (f32[24,128]{1,0:T(8,128)S(1)}, f32[24,128]{1,0:T(8,128)S(1)}) custom-call(f32[4,40,128]{2,1,0:T(8,128)S(1)} %pad_maximum_fusion.refs_0_, f32[4,24,128]{2,1,0:T(8,128)S(1)} %collective-permute-done.2.refs_1_, f32[4,24,128]{2,1,0:T(8,128)S(1)} %collective-permute-done.3.refs_2_, f32[4,24,128]{2,1,0:T(8,128)S(1)} %collective-permute-done.4.refs_3_, ...), custom_call_target="tpu_custom_call" | custom-call | tf_op jit(solution)/shard_map/second_iteration/pallas_call | solution.py:318
  23.1 0.2 collective-permute-start.6
  23.3 1.0 %collective-permute-done.6.got_ref = f32[24,128]{1,0:T(8,128)S(1)} collective-permute-done((f32[24,128]{1,0:T(8,128)S(1)}, f32[24,128]{1,0:T(8,128)S(1)}, u32[]{:S(2)}, u32[]{:S(2)}) %collective-permute-start.6) | collective-permute-done | bytes 12320 | tf_op jit(solution)/shard_map/ppermute | solution.py:269
  24.3 0.9 %unpack.1 = (f32[16,256]{1,0:T(8,128)}, f32[1,256]{1,0:T(1,128)}) custom-call(f32[24,128]{1,0:T(8,128)S(1)} %get-tuple-element.10.keep_ref, f32[24,128]{1,0:T(8,128)S(1)} %collective-permute-done.6.got_ref), custom_call_target="tpu_custom_call" | custom-call | tf_op jit(solution)/shard_map/unpack/pallas_call | solution.py:329
  (3 shorter events, 0.0 us)
Async XLA Ops:
  1.8 4.9 %collective-permute-start = (f32[1,40,128]{2,1,0:T(8,128)S(1)}, f32[1,40,128]{2,1,0:T(8,128)S(1)}, u32[]{:S(2)}, u32[]{:S(2)}) collective-permute-start(f32[1,40,128]{2,1,0:T(8,128)S(1)} %bitcast.2), channel_id=1, source_target_pairs={{0,4},{1,5},{2,6},{3,7},{4,0},{5,1},{6,2},{7,3},{8,12},{9,13},{10,... | collective-permute-start | bytes 61448 | tf_op jit(solution)/shard_map/ppermute | solution.py:269
  6.6 5.0 %collective-permute-start.1 = (f32[2,40,128]{2,1,0:T(8,128)S(1)}, f32[2,40,128]{2,1,0:T(8,128)S(1)}, u32[]{:S(2)}, u32[]{:S(2)}) collective-permute-start(f32[2,40,128]{2,1,0:T(8,128)S(1)} %pad_maximum_fusion.1), channel_id=1, source_target_pairs={{0,8},{1,9},{2,10},{3,11},{4,12},{5,13},{6,14},{7,15},{8,0},{9,1},... | collective-permute-start | bytes 122888 | tf_op jit(solution)/shard_map/ppermute | solution.py:269
  11.7 4.2 %collective-permute-start.3 = (f32[4,24,128]{2,1,0:T(8,128)S(1)}, f32[4,24,128]{2,1,0:T(8,128)S(1)}, u32[]{:S(2)}, u32[]{:S(2)}) collective-permute-start(f32[4,24,128]{2,1,0:T(8,128)S(1)} %get-tuple-element.12), channel_id=1, source_target_pairs={{0,2},{1,3},{2,0},{3,1},{4,6},{5,7},{6,4},{7,5},{8,10},{9,11},{10,... | collective-permute-start | bytes 147464 | tf_op jit(solution)/shard_map/ppermute | solution.py:269
  13.5 3.5 %collective-permute-start.4 = (f32[4,24,128]{2,1,0:T(8,128)S(1)}, f32[4,24,128]{2,1,0:T(8,128)S(1)}, u32[]{:S(2)}, u32[]{:S(2)}) collective-permute-start(f32[4,24,128]{2,1,0:T(8,128)S(1)} %get-tuple-element.13), channel_id=1, source_target_pairs={{0,3},{1,2},{2,1},{3,0},{4,7},{5,6},{6,5},{7,4},{8,11},{9,10},{10,... | collective-permute-start | bytes 147464 | tf_op jit(solution)/shard_map/ppermute | solution.py:269
  13.6 3.5 %collective-permute-start.2 = (f32[4,24,128]{2,1,0:T(8,128)S(1)}, f32[4,24,128]{2,1,0:T(8,128)S(1)}, u32[]{:S(2)}, u32[]{:S(2)}) collective-permute-start(f32[4,24,128]{2,1,0:T(8,128)S(1)} %get-tuple-element.13), channel_id=1, source_target_pairs={{0,1},{1,0},{2,3},{3,2},{4,5},{5,4},{6,7},{7,6},{8,9},{9,8},{10,11... | collective-permute-start | bytes 147464 | tf_op jit(solution)/shard_map/ppermute | solution.py:269
  13.9 0.8 %copy-start = (f32[16,2,256]{2,1,0:T(2,128)S(1)}, f32[16,2,256]{2,1,0:T(2,128)}, u32[]{:S(2)}) copy-start(f32[16,2,256]{2,1,0:T(2,128)} %refs_0_.3) | copy-start | bytes 98308
  20.0 1.2 %collective-permute-start.5 = (f32[16,256]{1,0:T(8,128)S(1)}, f32[16,256]{1,0:T(8,128)S(1)}, u32[]{:S(2)}, u32[]{:S(2)}) collective-permute-start(f32[16,256]{1,0:T(8,128)S(1)} %first_iteration.1.refs_7_), channel_id=1, source_target_pairs={{0,1},{1,0},{2,3},{3,2},{4,5},{5,4},{6,7},{7,6},{8,9},{9,8},{10,11... | collective-permute-start | bytes 49160 | tf_op jit(solution)/shard_map/ppermute | solution.py:269
  23.1 1.2 %collective-permute-start.6 = (f32[24,128]{1,0:T(8,128)S(1)}, f32[24,128]{1,0:T(8,128)S(1)}, u32[]{:S(2)}, u32[]{:S(2)}) collective-permute-start(f32[24,128]{1,0:T(8,128)S(1)} %get-tuple-element.11), channel_id=1, source_target_pairs={{0,1},{1,0},{2,3},{3,2},{4,5},{5,4},{6,7},{7,6},{8,9},{9,8},{10,11... | collective-permute-start | bytes 36872 | tf_op jit(solution)/shard_map/ppermute | solution.py:269

commit v5 on v4

--- a/solution.py
+++ b/solution.py
@@ -26,6 +26,9 @@
 ROW_CAP = 2
 ROW_MASK = 4
 STEP = 4
+SUBLANES = 8
+LOG2E = 1.4426950408889634
+LN2 = 0.6931471805599453
 
 
 def dot_nt(a, b):
@@ -85,7 +88,8 @@
         high, low = split(jnp.exp(x_off * ((fx - MIDDLE) * (2.0 * SCALE))))
         xf_ref[slot, :HALF, :] = high
         xf_ref[slot, HALF:, :] = low
-        yf_ref[slot] = jnp.exp(y_off * ((fy - MIDDLE) * (2.0 * SCALE)))
+        y_factor = jnp.exp(y_off * ((fy - MIDDLE) * (2.0 * SCALE)))
+        yf_ref[slot] = jnp.broadcast_to(y_factor[:, None, :], yf_ref.shape[1:])
         dx = x_mid - fx
         dy = y_mid - fy
         cost_ref[slot] = (dx * dx + dy * dy) * SCALE
@@ -104,46 +108,77 @@
     mask_ref[...] = dot_nn(picked, spread).reshape(slots, slots, HALF)
 
 
-def row_pass(gathered, potential, factors, mask_ref, acc_ref):
+def block_top(potential, factors, slot):
+    return jnp.max(potential(slot) - factors[2][slot], axis=1, keepdims=True)
+
+
+def block_sums(potential, factors, top, slot):
     xf_ref, yf_ref, cost_ref = factors
-    slots = len(gathered.slots)
+    slots = top.shape[0]
+    weight = jnp.exp(potential(slot) - cost_ref[slot] - top)
+    parts = [weight[i : i + SUBLANES][None] * yf_ref[slot] for i in range(0, slots, SUBLANES)]
+    lhs = jnp.concatenate(parts, axis=1)
+    a_high, a_low = split(lhs.reshape(TSIDE * slots, lhs.shape[-1]))
+    return row_product(a_high, a_low, xf_ref, slot).reshape(TSIDE, slots, HALF)
+
+
+def row_pass(potential, factors, mask_ref, demand_ref, acc_ref, early_ref=None):
+    slots = mask_ref.shape[0]
     best = jnp.full((slots, HALF), LOWEST, jnp.float32)
     tops = []
-    for slot in gathered.slots:
-        top = jnp.max(potential(slot) - cost_ref[slot], axis=1, keepdims=True)
+    for slot in range(slots):
+        top = block_top(potential, factors, slot)
         tops.append(top)
         best = jnp.maximum(best, jnp.where(mask_ref[slot] > 0.0, top, LOWEST))
-    for slot in gathered.slots:
+    for slot in range(slots):
         top = tops[slot]
-        weight = jnp.exp(potential(slot) - cost_ref[slot] - top)
-        lhs = weight[:, None, :] * yf_ref[slot][None]
-        a_high, a_low = split(lhs.reshape(slots * TSIDE, lhs.shape[-1]))
-        both = dot_nt(a_high, xf_ref[slot])
-        third = dot_nt(a_low, xf_ref[slot, :HALF, :])
-        part = both[:, :HALF] + both[:, HALF:] + third
+        if early_ref is not None and slot % STEP == 0:
+            part = early_ref[slot // STEP]
+        else:
+            part = block_sums(potential, factors, top, slot)
         scale = jnp.where(mask_ref[slot] > 0.0, jnp.exp(jnp.minimum(top - best, 0.0)), 0.0)
-        scaled = part.reshape(slots, TSIDE, HALF) * scale[:, None, :]
+        scaled = part * scale[None]
         if slot == 0:
             acc_ref[...] = scaled
         else:
             acc_ref[...] += scaled
-    demand = jnp.concatenate([gathered.demand(slot)[None] for slot in gathered.slots], axis=0)
-    return demand - best[:, None, :] - jnp.log(acc_ref[...])
-
-
-def column_part(factors, mask_ref, level, base, slot):
+    return demand_ref[...] - best[None] - jnp.log(acc_ref[...])
+
+
+def row_product(a_high, a_low, xf_ref, slot):
+    both = dot_nt(a_high, xf_ref[slot])
+    third = dot_nt(a_low, xf_ref[slot, :HALF, :])
+    return both[:, :HALF] + both[:, HALF:] + third
+
+
+def column_product(w_high, w_low, xf_ref, slot):
+    mixed = dot_nn(jnp.concatenate([w_high, w_high], axis=1), xf_ref[slot])
+    return mixed + dot_nn(w_low, xf_ref[slot, :HALF, :])
+
+
+def column_base(shifted):
+    scaled = shifted * LOG2E
+    level = jnp.ceil(jnp.max(scaled, axis=0))
+    high, low = split(jnp.exp2(scaled - level[None]))
+    return level, high, low
+
+
+def column_part(factors, mask_ref, base, slot):
     xf_ref, yf_ref, cost_ref = factors
+    level, high, low = base
     slots = level.shape[0]
     active = mask_ref[slot] > 0.0
     top = jnp.max(jnp.where(active, level, LOWEST), axis=1, keepdims=True)
-    scale = jnp.where(active, jnp.exp(jnp.minimum(level - top, 0.0)), 0.0)
-    weights = (base * scale[:, None, :]).reshape(slots * TSIDE, HALF)
-    w_high, w_low = split(weights)
-    mixed = dot_nn(jnp.concatenate([w_high, w_high], axis=1), xf_ref[slot])
-    mixed = mixed + dot_nn(w_low, xf_ref[slot, :HALF, :])
-    width = mixed.shape[-1]
-    sums = jnp.sum(mixed.reshape(slots, TSIDE, width) * yf_ref[slot][None], axis=1)
-    tops = top - cost_ref[slot]
+    scale = jnp.where(active, jnp.exp2(jnp.minimum(level - top, 0.0)), 0.0).astype(jnp.bfloat16)
+    w_high = (high * scale[None]).reshape(TSIDE * slots, HALF)
+    w_low = (low * scale[None]).reshape(TSIDE * slots, HALF)
+    mixed = column_product(w_high, w_low, xf_ref, slot)
+    mixed = mixed.reshape(TSIDE, slots, mixed.shape[-1])
+    sums = [
+        jnp.sum(mixed[:, i : i + SUBLANES] * yf_ref[slot], axis=0) for i in range(0, slots, SUBLANES)
+    ]
+    sums = jnp.concatenate(sums, axis=0)
+    tops = top * LN2 - cost_ref[slot]
     best = jnp.max(tops, axis=0, keepdims=True)
     total = jnp.sum(sums * jnp.exp(tops - best), axis=0, keepdims=True)
     return best + jnp.log(total)
@@ -169,6 +204,20 @@
         ]
         result.append(halves)
     return result
+
+
+def swap_half(values):
+    lane_group = lax.broadcasted_iota(jnp.int32, (TSIDE, HALF), 1) // TSIDE
+    diagonal = lane_group[:COLS_HALF] == lax.broadcasted_iota(jnp.int32, (COLS_HALF, HALF), 0)
+    result = ([], [])
+    for tile in range(COLS_HALF):
+        piece = jnp.where(lane_group == tile, values, 0.0)
+        for shift in (TSIDE, 2 * TSIDE, 4 * TSIDE):
+            piece = piece + pltpu.roll(piece, shift, 1)
+        for half in (0, 1):
+            part = piece[half * COLS_HALF : (half + 1) * COLS_HALF]
+            result[half].append(jnp.sum(jnp.where(diagonal, part, 0.0), axis=0, keepdims=True))
+    return jnp.concatenate(result[0] + result[1], axis=0)
 
 
 def pack_kernel(*refs):
@@ -206,13 +255,11 @@
 
 
 def unpack_kernel(keep_ref, got_ref, cell_ref, fac_ref):
-    is_left = lax.axis_index("tile") % 2 == 0
-    keep = keep_ref[:TSIDE, :]
-    got = got_ref[:TSIDE, :]
-    grid = jnp.concatenate([jnp.where(is_left, keep, got), jnp.where(is_left, got, keep)], axis=1)
-    for row, halves in enumerate(swap_minor(grid)):
-        cell_ref[row : row + 1, :HALF] = halves[0]
-        cell_ref[row : row + 1, HALF:] = halves[1]
+    core = lax.axis_index("tile") % 2
+    for side, ref in ((core, keep_ref), (1 - core, got_ref)):
+        rows = pl.ds(pl.multiple_of(side * COLS_HALF, COLS_HALF), COLS_HALF)
+        cell_ref[rows, :HALF] = ref[:COLS_HALF, :]
+        cell_ref[rows, HALF:] = ref[COLS_HALF:TSIDE, :]
     tail = keep_ref[TSIDE:, :]
     total = log_add(tail[ROW_POT : ROW_POT + 2], got_ref[TSIDE + ROW_POT : TSIDE + ROW_POT + 2, :])
     fac = tail[ROW_CAP : ROW_CAP + 2] - total
@@ -220,47 +267,56 @@
     fac_ref[:, HALF:] = fac[1:2]
 
 
+def early_kernel(*refs):
+    gathered = Gathered(refs[:1])
+    factors = refs[1:4]
+    for line in range(refs[0].shape[0]):
+        slot = line * STEP
+        top = block_top(gathered.potential, factors, slot)
+        refs[4][line] = block_sums(gathered.potential, factors, top, slot)
+
+
 def first_kernel(*refs):
     gathered = Gathered(refs[:STEP])
     factors = refs[STEP : STEP + 3]
-    part_ref, mask_ref, acc_ref = refs[STEP + 3 :]
+    early_ref, part_ref, mask_ref, demand_ref, cap_ref, acc_ref = refs[STEP + 3 :]
     build_mask(gathered, lax.axis_index("tile"), mask_ref)
-    shifted = row_pass(gathered, gathered.potential, factors, mask_ref, acc_ref)
-    level = jnp.max(shifted, axis=1)
-    acc_ref[...] = jnp.exp(shifted - level[:, None, :])
     for slot in gathered.slots:
-        part_ref[slot : slot + 1, :] = column_part(factors, mask_ref, level, acc_ref[...], slot)
+        demand_ref[:, slot, :] = gathered.demand(slot)
+        cap_ref[slot : slot + 1, :] = gathered.capacity(slot)
+    base = column_base(row_pass(gathered.potential, factors, mask_ref, demand_ref, acc_ref, early_ref))
+    for slot in gathered.slots:
+        part_ref[slot : slot + 1, :] = column_part(factors, mask_ref, base, slot)
 
 
 def second_kernel(*refs):
-    gathered = Gathered(refs[:STEP])
-    factors = refs[STEP : STEP + 3]
-    mine_ref, other_ref, keep_ref, send_ref, pot_ref, mask_ref, acc_ref = refs[STEP + 3 :]
+    factors = refs[:3]
+    mask_ref, demand_ref, cap_ref, mine_ref, other_ref, keep_ref, send_ref, pot_ref, acc_ref = refs[3:]
     me = lax.axis_index("tile")
     core = me % 2
-    build_mask(gathered, me, mask_ref)
-    slots = len(gathered.slots)
+    slots = mask_ref.shape[0]
     other = other_ref[...]
     even = lax.broadcasted_iota(jnp.int32, other.shape, 0) % 2 == 0
     swapped = jnp.where(even, pltpu.roll(other, slots - 1, 0), pltpu.roll(other, 1, 0))
-    capacity = jnp.concatenate([gathered.capacity(slot) for slot in gathered.slots], axis=0)
-    pot_ref[...] = capacity - log_add(mine_ref[...], swapped)
+    pot_ref[...] = cap_ref[...] - log_add(mine_ref[...], swapped)
 
     def potential(slot):
         return pot_ref[slot : slot + 1, :]
 
-    shifted = row_pass(gathered, potential, factors, mask_ref, acc_ref)
-    level = jnp.max(shifted, axis=1)
-    base = jnp.exp(shifted - level[:, None, :])
+    shifted = row_pass(potential, factors, mask_ref, demand_ref, acc_ref)
+    acc_ref[...] = shifted
+    base = column_base(shifted)
     x_mid = (core * HALF).astype(jnp.float32) + 0.5 * HALF
     dx = lax.broadcasted_iota(jnp.int32, (1, HALF), 1).astype(jnp.float32) - 0.5 * (HALF - 1)
     dy = lax.broadcasted_iota(jnp.int32, (TSIDE, 1), 0).astype(jnp.float32) - 0.5 * (TSIDE - 1)
     for slot, out_ref in ((0, keep_ref), (1, send_ref)):
         y_mid = ((me ^ slot) * TSIDE).astype(jnp.float32) + 0.5 * TSIDE
         lift = (dx * (dx + 2.0 * (x_mid - MIDDLE)) + dy * (dy + 2.0 * (y_mid - MIDDLE))) * SCALE
-        out_ref[:TSIDE, :] = shifted[slot] + lift
-        part = column_part(factors, mask_ref, level, base, slot)
-        pieces = [part[:, :HALF], part[:, HALF:], gathered.tail(slot)[ROW_CAP:]]
+        out_ref[:TSIDE, :] = swap_half(acc_ref[:, slot, :] + lift)
+        part = column_part(factors, mask_ref, base, slot)
+        cap = cap_ref[slot : slot + 1, :]
+        pieces = [part[:, :HALF], part[:, HALF:], cap[:, :HALF], cap[:, HALF:]]
+        pieces += [jnp.zeros((TAIL - ROW_MASK, HALF), jnp.float32)]
         out_ref[TSIDE:, :] = jnp.concatenate(pieces, axis=0)
 
 
@@ -289,7 +345,7 @@
         lambda *refs: setup_kernel(slots, *refs),
         out_shape=(
             jax.ShapeDtypeStruct((slots, 2 * HALF, width), jnp.bfloat16),
-            jax.ShapeDtypeStruct((slots, TSIDE, width), jnp.float32),
+            jax.ShapeDtypeStruct((slots, TSIDE, SUBLANES, width), jnp.float32),
             jax.ShapeDtypeStruct((slots, slots, width), jnp.float32),
         ),
         compiler_params=light,
@@ -303,17 +359,24 @@
     same = lines[:, :KEEP_ROWS]
     across = lines[:, TSIDE:]
     gathered = (lines, exchange(across, 1), exchange(same, 2), exchange(across, 3))
-    scratch = [
-        pltpu.VMEM((slots, slots, HALF), jnp.float32),
-        pltpu.VMEM((slots, TSIDE, HALF), jnp.float32),
-    ]
-    part = pl.pallas_call(
+    early = pl.pallas_call(
+        early_kernel,
+        out_shape=jax.ShapeDtypeStruct((slots // STEP, TSIDE, slots, HALF), jnp.float32),
+        compiler_params=heavy,
+        name="early",
+    )(lines, *factors)
+    part, mask, demand, cap = pl.pallas_call(
         first_kernel,
-        out_shape=jax.ShapeDtypeStruct((slots, width), jnp.float32),
-        scratch_shapes=scratch,
+        out_shape=(
+            jax.ShapeDtypeStruct((slots, width), jnp.float32),
+            jax.ShapeDtypeStruct((slots, slots, HALF), jnp.float32),
+            jax.ShapeDtypeStruct((TSIDE, slots, HALF), jnp.float32),
+            jax.ShapeDtypeStruct((slots, width), jnp.float32),
+        ),
+        scratch_shapes=[pltpu.VMEM((TSIDE, slots, HALF), jnp.float32)],
         compiler_params=heavy,
         name="first_iteration",
-    )(*gathered, *factors)
+    )(*gathered, *factors, early)
     other = exchange(part, 1)
     keep, send = pl.pallas_call(
         second_kernel,
@@ -321,10 +384,13 @@
             jax.ShapeDtypeStruct((KEEP_ROWS, HALF), jnp.float32),
             jax.ShapeDtypeStruct((KEEP_ROWS, HALF), jnp.float32),
         ),
-        scratch_shapes=[pltpu.VMEM((slots, width), jnp.float32)] + scratch,
+        scratch_shapes=[
+            pltpu.VMEM((slots, width), jnp.float32),
+            pltpu.VMEM((TSIDE, slots, HALF), jnp.float32),
+        ],
         compiler_params=heavy,
         name="second_iteration",
-    )(*gathered, *factors, part, other)
+    )(*factors, mask, demand, cap, part, other)
     got = exchange(send, 1)
     return pl.pallas_call(
         unpack_kernel,

time: 25.5 us -> 24.7 us (0.969)
  waiting for transfers between devices: 7.74 us -> 7.07 us
    ppermute x7, waiting for transfers between devices: 7.74 us -> 7.07 us  [exchange(): lax.ppermute(block, 'tile', [(i, i ^ distance) for i in range(devices)])]
    pallas_call x1 -> x2, Pallas kernels: 2.97 us -> 2.98 us  [the longest x1 2.46 us: on_device_all_rows(): pl.pallas_call(first_kernel, out_shape=(jax.ShapeDtypeStruct((slots, widt...]
  transfers between devices with their start and end apart: 7 -> 7, of which waited for: 6 -> 5; matrix products, arithmetic and copies ran while one was open for 0% -> 0% of each run, Pallas kernels for 2% -> 5%
where the time goes in v5:
time: 24.7 us; the launch traced here: 24.4 us
  starting transfers between devices  8.63 us (35%)
  Pallas kernels  7.27 us (29%)
  waiting for transfers between devices  7.07 us (29%)
  local copies, waits for them, and re-layouts  0.77 us (3%)
  between operations  0.69 us (3%)
    ppermute x7, starting transfers between devices, exchange(): lax.ppermute(block, 'tile', [(i, i ^ distance) for i in range(devices)])  8.63 us
    ppermute x7, waiting for transfers between devices, exchange(): lax.ppermute(block, 'tile', [(i, i ^ distance) for i in range(devices)])  7.07 us
    pallas_call x1, Pallas kernels, on_device_all_rows(): pl.pallas_call(first_kernel, out_shape=(jax.ShapeDtypeStruct((slots, widt...  2.46 us
    pallas_call x1, Pallas kernels, on_device_all_rows(): pl.pallas_call(second_kernel, out_shape=(jax.ShapeDtypeStruct((KEEP_ROWS,...  1.78 us
    pallas_call x1, Pallas kernels, on_device_all_rows(): pl.pallas_call(pack_kernel, in_specs=[pl.BlockSpec(memory_space=pltpu.HBM...  1.13 us
    pallas_call x1, Pallas kernels, on_device_all_rows(): pl.pallas_call(lambda *refs: setup_kernel(slots, *refs), out_shape=(jax.S...  0.76 us
    unnamed x2, local copies, waits for them, and re-layouts  0.76 us
    pallas_call x1, Pallas kernels, on_device_all_rows(): pl.pallas_call(unpack_kernel, out_shape=(jax.ShapeDtypeStruct(log_demand....  0.62 us
  transfers between devices with their start and end apart: 7, of which 5 were waited for; matrix products, arithmetic and copies ran while one was open for 0% of the time, Pallas kernels for 5%

profile of v5, /device:TPU:0, one launch (start us, length us, event | category | flops | bytes accessed | tf_op | source)
XLA Modules:
  0.0 24.4 jit_solution(4266569821132456300)
XLA Ops:
  0.6 1.1 %pack.1 = f32[40,128]{1,0:T(8,128)S(1)} custom-call(f32[16,256]{1,0:T(8,128)} %refs_0_.3, f32[1,256]{1,0:T(1,128)} %refs_1_.1, f32[1,256]{1,0:T(1,128)} %refs_2_.1, s32[16,16]{1,0:T(8,128)} %refs_3_.1, s32[1,16]{1,0:T(1,128)} %bitcast.5), custom_call_target="tpu_custom_call" | custom-call | tf_op jit(solution)/shard_map/pack/pallas_call | solution.py:335
  1.8 3.1 %collective-permute-start = (f32[1,40,128]{2,1,0:T(8,128)S(1)}, f32[1,40,128]{2,1,0:T(8,128)S(1)}, u32[]{:S(2)}, u32[]{:S(2)}) collective-permute-start(f32[1,40,128]{2,1,0:T(8,128)S(1)} %bitcast.2), channel_id=1, source_target_pairs={{0,4},{1,5},{2,6},{3,7},{4,0},{5,1},{6,2},{7,3},{8,12},{9,13},{10,... | collective-permute-start | bytes 61448 | tf_op jit(solution)/shard_map/ppermute | solution.py:325
  4.9 1.8 %collective-permute-done = f32[1,40,128]{2,1,0:T(8,128)S(1)} collective-permute-done((f32[1,40,128]{2,1,0:T(8,128)S(1)}, f32[1,40,128]{2,1,0:T(8,128)S(1)}, u32[]{:S(2)}, u32[]{:S(2)}) %collective-permute-start) | collective-permute-done | bytes 20512 | tf_op jit(solution)/shard_map/ppermute | solution.py:325
  6.6 3.0 %collective-permute-start.1 = (f32[2,40,128]{2,1,0:T(8,128)S(1)}, f32[2,40,128]{2,1,0:T(8,128)S(1)}, u32[]{:S(2)}, u32[]{:S(2)}) collective-permute-start(f32[2,40,128]{2,1,0:T(8,128)S(1)} %pad_maximum_fusion.1), channel_id=1, source_target_pairs={{0,8},{1,9},{2,10},{3,11},{4,12},{5,13},{6,14},{7,15},{8,0},{9,1},... | collective-permute-start | bytes 122888 | tf_op jit(solution)/shard_map/ppermute | solution.py:325
  9.7 2.0 %collective-permute-done.1 = f32[2,40,128]{2,1,0:T(8,128)S(1)} collective-permute-done((f32[2,40,128]{2,1,0:T(8,128)S(1)}, f32[2,40,128]{2,1,0:T(8,128)S(1)}, u32[]{:S(2)}, u32[]{:S(2)}) %collective-permute-start.1) | collective-permute-done | bytes 40992 | tf_op jit(solution)/shard_map/ppermute | solution.py:325
  11.7 1.9 %collective-permute-start.3 = (f32[4,24,128]{2,1,0:T(8,128)S(1)}, f32[4,24,128]{2,1,0:T(8,128)S(1)}, u32[]{:S(2)}, u32[]{:S(2)}) collective-permute-start(f32[4,24,128]{2,1,0:T(8,128)S(1)} %get-tuple-element.20), channel_id=1, source_target_pairs={{0,2},{1,3},{2,0},{3,1},{4,6},{5,7},{6,4},{7,5},{8,10},{9,11},{10,... | collective-permute-start | bytes 147464 | tf_op jit(solution)/shard_map/ppermute | solution.py:325
  13.5 0.0 collective-permute-start.4
  13.6 0.3 %collective-permute-start.2 = (f32[4,24,128]{2,1,0:T(8,128)S(1)}, f32[4,24,128]{2,1,0:T(8,128)S(1)}, u32[]{:S(2)}, u32[]{:S(2)}) collective-permute-start(f32[4,24,128]{2,1,0:T(8,128)S(1)} %get-tuple-element.21), channel_id=1, source_target_pairs={{0,1},{1,0},{2,3},{3,2},{4,5},{5,4},{6,7},{7,6},{8,9},{9,8},{10,11... | collective-permute-start | bytes 147464 | tf_op jit(solution)/shard_map/ppermute | solution.py:325
  13.9 0.0 copy-start
  13.9 0.8 %copy-done = f32[16,2,256]{2,1,0:T(2,128)S(1)} copy-done((f32[16,2,256]{2,1,0:T(2,128)S(1)}, f32[16,2,256]{2,1,0:T(2,128)}, u32[]{:S(2)}) %copy-start) | copy-done | bytes 32792
  14.6 0.8 %setup.1 = (bf16[16,256,256]{2,1,0:T(8,128)(2,1)S(1)}, f32[16,16,8,256]{3,2,1,0:T(8,128)S(1)}, f32[16,16,256]{2,1,0:T(8,128)S(1)}) custom-call(f32[16,2,256]{2,1,0:T(2,128)S(1)} %copy-done), custom_call_target="tpu_custom_call" | custom-call | tf_op jit(solution)/shard_map/setup/pallas_call | solution.py:344
  15.4 0.5 %early.1.refs_7_ = f32[4,16,16,128]{3,2,1,0:T(8,128)S(1)} custom-call(f32[4,40,128]{2,1,0:T(8,128)S(1)} %pad_maximum_fusion.refs_0_, bf16[16,256,256]{2,1,0:T(8,128)(2,1)S(1)} %get-tuple-element.11.refs_1_.refs_4_.refs_0_, f32[16,16,8,256]{3,2,1,0:T(8,128)S(1)} %get-tuple-element.12.refs_2_.refs_5_.refs_1_, ...), custom_call_target="tpu_custom_call" | custom-call | tf_op jit(solution)/shard_map/early/pallas_call | solution.py:362
  15.9 0.0 collective-permute-done.3.refs_2_
  15.9 1.1 %collective-permute-done.4.refs_3_ = f32[4,24,128]{2,1,0:T(8,128)S(1)} collective-permute-done((f32[4,24,128]{2,1,0:T(8,128)S(1)}, f32[4,24,128]{2,1,0:T(8,128)S(1)}, u32[]{:S(2)}, u32[]{:S(2)}) %collective-permute-start.4) | collective-permute-done | bytes 49184 | tf_op jit(solution)/shard_map/ppermute | solution.py:325
  17.1 0.0 collective-permute-done.2.refs_1_
  17.1 2.5 %first_iteration.1 = (f32[16,256]{1,0:T(8,128)S(1)}, f32[16,16,128]{2,1,0:T(8,128)S(1)}, f32[16,16,128]{2,1,0:T(8,128)S(1)}, f32[16,256]{1,0:T(8,128)S(1)}) custom-call(f32[4,40,128]{2,1,0:T(8,128)S(1)} %pad_maximum_fusion.refs_0_, f32[4,24,128]{2,1,0:T(8,128)S(1)} %collective-permute-done.2.refs_1_, f32[4,24,128]{2,1,0:T(8,128)S(1)} %collective-permute-done.3.refs_2_, ...), custom_call_target="tpu_custom_call" | custom-call | tf_op jit(solution)/shard_map/first_iteration/pallas_call | solution.py:368
  19.5 0.1 collective-permute-start.5
  19.6 1.2 %collective-permute-done.5.refs_7_ = f32[16,256]{1,0:T(8,128)S(1)} collective-permute-done((f32[16,256]{1,0:T(8,128)S(1)}, f32[16,256]{1,0:T(8,128)S(1)}, u32[]{:S(2)}, u32[]{:S(2)}) %collective-permute-start.5) | collective-permute-done | bytes 16416 | tf_op jit(solution)/shard_map/ppermute | solution.py:325
  20.8 1.8 %second_iteration.1 = (f32[24,128]{1,0:T(8,128)S(1)}, f32[24,128]{1,0:T(8,128)S(1)}) custom-call(bf16[16,256,256]{2,1,0:T(8,128)(2,1)S(1)} %get-tuple-element.11.refs_1_.refs_4_.refs_0_, f32[16,16,8,256]{3,2,1,0:T(8,128)S(1)} %get-tuple-element.12.refs_2_.refs_5_.refs_1_, f32[16,16,256]{2,1,0:T(8,128)S(1)} %get-tuple-element.13.refs_3_.refs_6_.refs_2_, ...), custom_call_target="tpu_custom_call" | custom-call | tf_op jit(solution)/shard_map/second_iteration/pallas_call | solution.py:381
  22.6 0.2 collective-permute-start.6
  22.8 1.0 %collective-permute-done.6.got_ref = f32[24,128]{1,0:T(8,128)S(1)} collective-permute-done((f32[24,128]{1,0:T(8,128)S(1)}, f32[24,128]{1,0:T(8,128)S(1)}, u32[]{:S(2)}, u32[]{:S(2)}) %collective-permute-start.6) | collective-permute-done | bytes 12320 | tf_op jit(solution)/shard_map/ppermute | solution.py:325
  23.8 0.6 %unpack.1 = (f32[16,256]{1,0:T(8,128)}, f32[1,256]{1,0:T(1,128)}) custom-call(f32[24,128]{1,0:T(8,128)S(1)} %get-tuple-element.18.keep_ref, f32[24,128]{1,0:T(8,128)S(1)} %collective-permute-done.6.got_ref), custom_call_target="tpu_custom_call" | custom-call | tf_op jit(solution)/shard_map/unpack/pallas_call | solution.py:395
  (3 shorter events, 0.0 us)
Async XLA Ops:
  1.8 4.9 %collective-permute-start = (f32[1,40,128]{2,1,0:T(8,128)S(1)}, f32[1,40,128]{2,1,0:T(8,128)S(1)}, u32[]{:S(2)}, u32[]{:S(2)}) collective-permute-start(f32[1,40,128]{2,1,0:T(8,128)S(1)} %bitcast.2), channel_id=1, source_target_pairs={{0,4},{1,5},{2,6},{3,7},{4,0},{5,1},{6,2},{7,3},{8,12},{9,13},{10,... | collective-permute-start | bytes 61448 | tf_op jit(solution)/shard_map/ppermute | solution.py:325
  6.6 5.0 %collective-permute-start.1 = (f32[2,40,128]{2,1,0:T(8,128)S(1)}, f32[2,40,128]{2,1,0:T(8,128)S(1)}, u32[]{:S(2)}, u32[]{:S(2)}) collective-permute-start(f32[2,40,128]{2,1,0:T(8,128)S(1)} %pad_maximum_fusion.1), channel_id=1, source_target_pairs={{0,8},{1,9},{2,10},{3,11},{4,12},{5,13},{6,14},{7,15},{8,0},{9,1},... | collective-permute-start | bytes 122888 | tf_op jit(solution)/shard_map/ppermute | solution.py:325
  11.7 4.3 %collective-permute-start.3 = (f32[4,24,128]{2,1,0:T(8,128)S(1)}, f32[4,24,128]{2,1,0:T(8,128)S(1)}, u32[]{:S(2)}, u32[]{:S(2)}) collective-permute-start(f32[4,24,128]{2,1,0:T(8,128)S(1)} %get-tuple-element.20), channel_id=1, source_target_pairs={{0,2},{1,3},{2,0},{3,1},{4,6},{5,7},{6,4},{7,5},{8,10},{9,11},{10,... | collective-permute-start | bytes 147464 | tf_op jit(solution)/shard_map/ppermute | solution.py:325
  13.5 3.5 %collective-permute-start.4 = (f32[4,24,128]{2,1,0:T(8,128)S(1)}, f32[4,24,128]{2,1,0:T(8,128)S(1)}, u32[]{:S(2)}, u32[]{:S(2)}) collective-permute-start(f32[4,24,128]{2,1,0:T(8,128)S(1)} %get-tuple-element.21), channel_id=1, source_target_pairs={{0,3},{1,2},{2,1},{3,0},{4,7},{5,6},{6,5},{7,4},{8,11},{9,10},{10,... | collective-permute-start | bytes 147464 | tf_op jit(solution)/shard_map/ppermute | solution.py:325
  13.6 3.5 %collective-permute-start.2 = (f32[4,24,128]{2,1,0:T(8,128)S(1)}, f32[4,24,128]{2,1,0:T(8,128)S(1)}, u32[]{:S(2)}, u32[]{:S(2)}) collective-permute-start(f32[4,24,128]{2,1,0:T(8,128)S(1)} %get-tuple-element.21), channel_id=1, source_target_pairs={{0,1},{1,0},{2,3},{3,2},{4,5},{5,4},{6,7},{7,6},{8,9},{9,8},{10,11... | collective-permute-start | bytes 147464 | tf_op jit(solution)/shard_map/ppermute | solution.py:325
  13.9 0.8 %copy-start = (f32[16,2,256]{2,1,0:T(2,128)S(1)}, f32[16,2,256]{2,1,0:T(2,128)}, u32[]{:S(2)}) copy-start(f32[16,2,256]{2,1,0:T(2,128)} %refs_0_.2) | copy-start | bytes 98308
  19.5 1.2 %collective-permute-start.5 = (f32[16,256]{1,0:T(8,128)S(1)}, f32[16,256]{1,0:T(8,128)S(1)}, u32[]{:S(2)}, u32[]{:S(2)}) collective-permute-start(f32[16,256]{1,0:T(8,128)S(1)} %get-tuple-element.17.refs_6_), channel_id=1, source_target_pairs={{0,1},{1,0},{2,3},{3,2},{4,5},{5,4},{6,7},{7,6},{8,9},{9,8},{10,11... | collective-permute-start | bytes 49160 | tf_op jit(solution)/shard_map/ppermute | solution.py:325
  22.6 1.2 %collective-permute-start.6 = (f32[24,128]{1,0:T(8,128)S(1)}, f32[24,128]{1,0:T(8,128)S(1)}, u32[]{:S(2)}, u32[]{:S(2)}) collective-permute-start(f32[24,128]{1,0:T(8,128)S(1)} %get-tuple-element.19), channel_id=1, source_target_pairs={{0,1},{1,0},{2,3},{3,2},{4,5},{5,4},{6,7},{7,6},{8,9},{9,8},{10,11... | collective-permute-start | bytes 36872 | tf_op jit(solution)/shard_map/ppermute | solution.py:325

commit v6 on v5

--- a/solution.py
+++ b/solution.py
@@ -352,10 +352,7 @@
         name="setup",
     )(facility_xy)
     lines = message[None]
-    distance = STEP
-    while distance < slots:
-        lines = jnp.concatenate([lines, exchange(lines, distance)], axis=0)
-        distance *= 2
+    lines = jnp.concatenate([lines] + [exchange(lines, STEP * i) for i in range(1, slots // STEP)], axis=0)
     same = lines[:, :KEEP_ROWS]
     across = lines[:, TSIDE:]
     gathered = (lines, exchange(across, 1), exchange(same, 2), exchange(across, 3))

time: 24.7 us -> 24.4 us (0.988)
  starting transfers between devices: 8.63 us -> 8.26 us
    ppermute x7 -> x8, starting transfers between devices: 8.63 us -> 8.26 us  [exchange(): lax.ppermute(block, 'tile', [(i, i ^ distance) for i in range(devices)])]
    ppermute x7 -> x8, waiting for transfers between devices: 7.07 us -> 7.18 us  [exchange(): lax.ppermute(block, 'tile', [(i, i ^ distance) for i in range(devices)])]
  transfers between devices with their start and end apart: 7 -> 8, of which waited for: 5 -> 5; matrix products, arithmetic and copies ran while one was open for 0% -> 0% of each run, Pallas kernels for 5% -> 5%
where the time goes in v6:
time: 24.4 us; the launch traced here: 24.2 us
  starting transfers between devices  8.26 us (34%)
  Pallas kernels  7.27 us (30%)
  waiting for transfers between devices  7.18 us (29%)
  local copies, waits for them, and re-layouts  0.77 us (3%)
  between operations  0.69 us (3%)
    ppermute x8, starting transfers between devices, exchange(): lax.ppermute(block, 'tile', [(i, i ^ distance) for i in range(devices)])  8.26 us
    ppermute x8, waiting for transfers between devices, exchange(): lax.ppermute(block, 'tile', [(i, i ^ distance) for i in range(devices)])  7.18 us
    pallas_call x1, Pallas kernels, on_device_all_rows(): pl.pallas_call(first_kernel, out_shape=(jax.ShapeDtypeStruct((slots, widt...  2.45 us
    pallas_call x1, Pallas kernels, on_device_all_rows(): pl.pallas_call(second_kernel, out_shape=(jax.ShapeDtypeStruct((KEEP_ROWS,...  1.79 us
    pallas_call x1, Pallas kernels, on_device_all_rows(): pl.pallas_call(pack_kernel, in_specs=[pl.BlockSpec(memory_space=pltpu.HBM...  1.13 us
    pallas_call x1, Pallas kernels, on_device_all_rows(): pl.pallas_call(lambda *refs: setup_kernel(slots, *refs), out_shape=(jax.S...  0.76 us
    unnamed x2, local copies, waits for them, and re-layouts  0.76 us
    pallas_call x1, Pallas kernels, on_device_all_rows(): pl.pallas_call(unpack_kernel, out_shape=(jax.ShapeDtypeStruct(log_demand....  0.62 us
  transfers between devices with their start and end apart: 8, of which 5 were waited for; matrix products, arithmetic and copies ran while one was open for 0% of the time, Pallas kernels for 5%

profile of v6, /device:TPU:0, one launch (start us, length us, event | category | flops | bytes accessed | tf_op | source)
XLA Modules:
  0.0 24.2 jit_solution(705729848081818858)
XLA Ops:
  0.6 1.1 %pack.1 = f32[40,128]{1,0:T(8,128)S(1)} custom-call(f32[16,256]{1,0:T(8,128)} %refs_0_.3, f32[1,256]{1,0:T(1,128)} %refs_1_.1, f32[1,256]{1,0:T(1,128)} %refs_2_.1, s32[16,16]{1,0:T(8,128)} %refs_3_.1, s32[1,16]{1,0:T(1,128)} %bitcast.6), custom_call_target="tpu_custom_call" | custom-call | tf_op jit(solution)/shard_map/pack/pallas_call | solution.py:335
  1.8 5.1 %collective-permute-start.2 = (f32[1,40,128]{2,1,0:T(8,128)S(1)}, f32[1,40,128]{2,1,0:T(8,128)S(1)}, u32[]{:S(2)}, u32[]{:S(2)}) collective-permute-start(f32[1,40,128]{2,1,0:T(8,128)S(1)} %bitcast.2), channel_id=1, source_target_pairs={{0,12},{1,13},{2,14},{3,15},{4,8},{5,9},{6,10},{7,11},{8,4},{9,5},... | collective-permute-start | bytes 61448 | tf_op jit(solution)/shard_map/ppermute | solution.py:325
  6.9 0.0 collective-permute-start.1
  6.9 0.6 %collective-permute-start = (f32[1,40,128]{2,1,0:T(8,128)S(1)}, f32[1,40,128]{2,1,0:T(8,128)S(1)}, u32[]{:S(2)}, u32[]{:S(2)}) collective-permute-start(f32[1,40,128]{2,1,0:T(8,128)S(1)} %bitcast.4), channel_id=1, source_target_pairs={{0,4},{1,5},{2,6},{3,7},{4,0},{5,1},{6,2},{7,3},{8,12},{9,13},{10,... | collective-permute-start | bytes 61448 | tf_op jit(solution)/shard_map/ppermute | solution.py:325
  7.5 1.1 %collective-permute-done.2 = f32[1,40,128]{2,1,0:T(8,128)S(1)} collective-permute-done((f32[1,40,128]{2,1,0:T(8,128)S(1)}, f32[1,40,128]{2,1,0:T(8,128)S(1)}, u32[]{:S(2)}, u32[]{:S(2)}) %collective-permute-start.2) | collective-permute-done | bytes 20512 | tf_op jit(solution)/shard_map/ppermute | solution.py:325
  8.6 2.9 %collective-permute-done.1 = f32[1,40,128]{2,1,0:T(8,128)S(1)} collective-permute-done((f32[1,40,128]{2,1,0:T(8,128)S(1)}, f32[1,40,128]{2,1,0:T(8,128)S(1)}, u32[]{:S(2)}, u32[]{:S(2)}) %collective-permute-start.1) | collective-permute-done | bytes 20512 | tf_op jit(solution)/shard_map/ppermute | solution.py:325
  11.6 0.0 collective-permute-done
  11.6 1.6 %collective-permute-start.4 = (f32[4,24,128]{2,1,0:T(8,128)S(1)}, f32[4,24,128]{2,1,0:T(8,128)S(1)}, u32[]{:S(2)}, u32[]{:S(2)}) collective-permute-start(f32[4,24,128]{2,1,0:T(8,128)S(1)} %get-tuple-element.20), channel_id=1, source_target_pairs={{0,2},{1,3},{2,0},{3,1},{4,6},{5,7},{6,4},{7,5},{8,10},{9,11},{10,... | collective-permute-start | bytes 147464 | tf_op jit(solution)/shard_map/ppermute | solution.py:325
  13.2 0.0 collective-permute-start.5
  13.2 0.6 %collective-permute-start.3 = (f32[4,24,128]{2,1,0:T(8,128)S(1)}, f32[4,24,128]{2,1,0:T(8,128)S(1)}, u32[]{:S(2)}, u32[]{:S(2)}) collective-permute-start(f32[4,24,128]{2,1,0:T(8,128)S(1)} %get-tuple-element.21), channel_id=1, source_target_pairs={{0,1},{1,0},{2,3},{3,2},{4,5},{5,4},{6,7},{7,6},{8,9},{9,8},{10,11... | collective-permute-start | bytes 147464 | tf_op jit(solution)/shard_map/ppermute | solution.py:325
  13.8 0.0 copy-start
  13.8 0.8 %copy-done = f32[16,2,256]{2,1,0:T(2,128)S(1)} copy-done((f32[16,2,256]{2,1,0:T(2,128)S(1)}, f32[16,2,256]{2,1,0:T(2,128)}, u32[]{:S(2)}) %copy-start) | copy-done | bytes 32792
  14.6 0.8 %setup.1 = (bf16[16,256,256]{2,1,0:T(8,128)(2,1)S(1)}, f32[16,16,8,256]{3,2,1,0:T(8,128)S(1)}, f32[16,16,256]{2,1,0:T(8,128)S(1)}) custom-call(f32[16,2,256]{2,1,0:T(2,128)S(1)} %copy-done), custom_call_target="tpu_custom_call" | custom-call | tf_op jit(solution)/shard_map/setup/pallas_call | solution.py:344
  15.3 0.5 %early.1.refs_7_ = f32[4,16,16,128]{3,2,1,0:T(8,128)S(1)} custom-call(f32[4,40,128]{2,1,0:T(8,128)S(1)} %pad_maximum_fusion.refs_0_, bf16[16,256,256]{2,1,0:T(8,128)(2,1)S(1)} %get-tuple-element.11.refs_1_.refs_4_.refs_0_, f32[16,16,8,256]{3,2,1,0:T(8,128)S(1)} %get-tuple-element.12.refs_2_.refs_5_.refs_1_, ...), custom_call_target="tpu_custom_call" | custom-call | tf_op jit(solution)/shard_map/early/pallas_call | solution.py:359
  15.8 0.0 collective-permute-done.4.refs_2_
  15.9 0.9 %collective-permute-done.5.refs_3_ = f32[4,24,128]{2,1,0:T(8,128)S(1)} collective-permute-done((f32[4,24,128]{2,1,0:T(8,128)S(1)}, f32[4,24,128]{2,1,0:T(8,128)S(1)}, u32[]{:S(2)}, u32[]{:S(2)}) %collective-permute-start.5) | collective-permute-done | bytes 49184 | tf_op jit(solution)/shard_map/ppermute | solution.py:325
  16.8 0.0 collective-permute-done.3.refs_1_
  16.8 2.5 %first_iteration.1 = (f32[16,256]{1,0:T(8,128)S(1)}, f32[16,16,128]{2,1,0:T(8,128)S(1)}, f32[16,16,128]{2,1,0:T(8,128)S(1)}, f32[16,256]{1,0:T(8,128)S(1)}) custom-call(f32[4,40,128]{2,1,0:T(8,128)S(1)} %pad_maximum_fusion.refs_0_, f32[4,24,128]{2,1,0:T(8,128)S(1)} %collective-permute-done.3.refs_1_, f32[4,24,128]{2,1,0:T(8,128)S(1)} %collective-permute-done.4.refs_2_, ...), custom_call_target="tpu_custom_call" | custom-call | tf_op jit(solution)/shard_map/first_iteration/pallas_call | solution.py:365
  19.3 0.1 collective-permute-start.6
  19.3 1.2 %collective-permute-done.6.refs_7_ = f32[16,256]{1,0:T(8,128)S(1)} collective-permute-done((f32[16,256]{1,0:T(8,128)S(1)}, f32[16,256]{1,0:T(8,128)S(1)}, u32[]{:S(2)}, u32[]{:S(2)}) %collective-permute-start.6) | collective-permute-done | bytes 16416 | tf_op jit(solution)/shard_map/ppermute | solution.py:325
  20.5 1.8 %second_iteration.1 = (f32[24,128]{1,0:T(8,128)S(1)}, f32[24,128]{1,0:T(8,128)S(1)}) custom-call(bf16[16,256,256]{2,1,0:T(8,128)(2,1)S(1)} %get-tuple-element.11.refs_1_.refs_4_.refs_0_, f32[16,16,8,256]{3,2,1,0:T(8,128)S(1)} %get-tuple-element.12.refs_2_.refs_5_.refs_1_, f32[16,16,256]{2,1,0:T(8,128)S(1)} %get-tuple-element.13.refs_3_.refs_6_.refs_2_, ...), custom_call_target="tpu_custom_call" | custom-call | tf_op jit(solution)/shard_map/second_iteration/pallas_call | solution.py:378
  22.3 0.2 collective-permute-start.7
  22.5 1.0 %collective-permute-done.7.got_ref = f32[24,128]{1,0:T(8,128)S(1)} collective-permute-done((f32[24,128]{1,0:T(8,128)S(1)}, f32[24,128]{1,0:T(8,128)S(1)}, u32[]{:S(2)}, u32[]{:S(2)}) %collective-permute-start.7) | collective-permute-done | bytes 12320 | tf_op jit(solution)/shard_map/ppermute | solution.py:325
  23.6 0.6 %unpack.1 = (f32[16,256]{1,0:T(8,128)}, f32[1,256]{1,0:T(1,128)}) custom-call(f32[24,128]{1,0:T(8,128)S(1)} %get-tuple-element.18.keep_ref, f32[24,128]{1,0:T(8,128)S(1)} %collective-permute-done.7.got_ref), custom_call_target="tpu_custom_call" | custom-call | tf_op jit(solution)/shard_map/unpack/pallas_call | solution.py:392
  (2 shorter events, 0.0 us)
Async XLA Ops:
  1.8 6.9 %collective-permute-start.2 = (f32[1,40,128]{2,1,0:T(8,128)S(1)}, f32[1,40,128]{2,1,0:T(8,128)S(1)}, u32[]{:S(2)}, u32[]{:S(2)}) collective-permute-start(f32[1,40,128]{2,1,0:T(8,128)S(1)} %bitcast.2), channel_id=1, source_target_pairs={{0,12},{1,13},{2,14},{3,15},{4,8},{5,9},{6,10},{7,11},{8,4},{9,5},... | collective-permute-start | bytes 61448 | tf_op jit(solution)/shard_map/ppermute | solution.py:325
  6.9 4.7 %collective-permute-start.1 = (f32[1,40,128]{2,1,0:T(8,128)S(1)}, f32[1,40,128]{2,1,0:T(8,128)S(1)}, u32[]{:S(2)}, u32[]{:S(2)}) collective-permute-start(f32[1,40,128]{2,1,0:T(8,128)S(1)} %bitcast.3), channel_id=1, source_target_pairs={{0,8},{1,9},{2,10},{3,11},{4,12},{5,13},{6,14},{7,15},{8,0},{9,1},... | collective-permute-start | bytes 61448 | tf_op jit(solution)/shard_map/ppermute | solution.py:325
  6.9 4.7 %collective-permute-start = (f32[1,40,128]{2,1,0:T(8,128)S(1)}, f32[1,40,128]{2,1,0:T(8,128)S(1)}, u32[]{:S(2)}, u32[]{:S(2)}) collective-permute-start(f32[1,40,128]{2,1,0:T(8,128)S(1)} %bitcast.4), channel_id=1, source_target_pairs={{0,4},{1,5},{2,6},{3,7},{4,0},{5,1},{6,2},{7,3},{8,12},{9,13},{10,... | collective-permute-start | bytes 61448 | tf_op jit(solution)/shard_map/ppermute | solution.py:325
  11.6 4.3 %collective-permute-start.4 = (f32[4,24,128]{2,1,0:T(8,128)S(1)}, f32[4,24,128]{2,1,0:T(8,128)S(1)}, u32[]{:S(2)}, u32[]{:S(2)}) collective-permute-start(f32[4,24,128]{2,1,0:T(8,128)S(1)} %get-tuple-element.20), channel_id=1, source_target_pairs={{0,2},{1,3},{2,0},{3,1},{4,6},{5,7},{6,4},{7,5},{8,10},{9,11},{10,... | collective-permute-start | bytes 147464 | tf_op jit(solution)/shard_map/ppermute | solution.py:325
  13.2 3.7 %collective-permute-start.5 = (f32[4,24,128]{2,1,0:T(8,128)S(1)}, f32[4,24,128]{2,1,0:T(8,128)S(1)}, u32[]{:S(2)}, u32[]{:S(2)}) collective-permute-start(f32[4,24,128]{2,1,0:T(8,128)S(1)} %get-tuple-element.21), channel_id=1, source_target_pairs={{0,3},{1,2},{2,1},{3,0},{4,7},{5,6},{6,5},{7,4},{8,11},{9,10},{10,... | collective-permute-start | bytes 147464 | tf_op jit(solution)/shard_map/ppermute | solution.py:325
  13.2 3.7 %collective-permute-start.3 = (f32[4,24,128]{2,1,0:T(8,128)S(1)}, f32[4,24,128]{2,1,0:T(8,128)S(1)}, u32[]{:S(2)}, u32[]{:S(2)}) collective-permute-start(f32[4,24,128]{2,1,0:T(8,128)S(1)} %get-tuple-element.21), channel_id=1, source_target_pairs={{0,1},{1,0},{2,3},{3,2},{4,5},{5,4},{6,7},{7,6},{8,9},{9,8},{10,11... | collective-permute-start | bytes 147464 | tf_op jit(solution)/shard_map/ppermute | solution.py:325
  13.8 0.8 %copy-start = (f32[16,2,256]{2,1,0:T(2,128)S(1)}, f32[16,2,256]{2,1,0:T(2,128)}, u32[]{:S(2)}) copy-start(f32[16,2,256]{2,1,0:T(2,128)} %refs_0_.2) | copy-start | bytes 98308
  19.3 1.2 %collective-permute-start.6 = (f32[16,256]{1,0:T(8,128)S(1)}, f32[16,256]{1,0:T(8,128)S(1)}, u32[]{:S(2)}, u32[]{:S(2)}) collective-permute-start(f32[16,256]{1,0:T(8,128)S(1)} %get-tuple-element.17.refs_6_), channel_id=1, source_target_pairs={{0,1},{1,0},{2,3},{3,2},{4,5},{5,4},{6,7},{7,6},{8,9},{9,8},{10,11... | collective-permute-start | bytes 49160 | tf_op jit(solution)/shard_map/ppermute | solution.py:325
  22.3 1.2 %collective-permute-start.7 = (f32[24,128]{1,0:T(8,128)S(1)}, f32[24,128]{1,0:T(8,128)S(1)}, u32[]{:S(2)}, u32[]{:S(2)}) collective-permute-start(f32[24,128]{1,0:T(8,128)S(1)} %get-tuple-element.19), channel_id=1, source_target_pairs={{0,1},{1,0},{2,3},{3,2},{4,5},{5,4},{6,7},{7,6},{8,9},{9,8},{10,11... | collective-permute-start | bytes 36872 | tf_op jit(solution)/shard_map/ppermute | solution.py:325

commit v7 on v6

--- a/solution.py
+++ b/solution.py
@@ -26,6 +26,7 @@
 ROW_CAP = 2
 ROW_MASK = 4
 STEP = 4
+EARLY = 3
 SUBLANES = 8
 LOG2E = 1.4426950408889634
 LN2 = 0.6931471805599453
@@ -122,7 +123,7 @@
     return row_product(a_high, a_low, xf_ref, slot).reshape(TSIDE, slots, HALF)
 
 
-def row_pass(potential, factors, mask_ref, demand_ref, acc_ref, early_ref=None):
+def row_pass(potential, factors, mask_ref, demand_ref, acc_ref, early_refs=()):
     slots = mask_ref.shape[0]
     best = jnp.full((slots, HALF), LOWEST, jnp.float32)
     tops = []
@@ -132,8 +133,8 @@
         best = jnp.maximum(best, jnp.where(mask_ref[slot] > 0.0, top, LOWEST))
     for slot in range(slots):
         top = tops[slot]
-        if early_ref is not None and slot % STEP == 0:
-            part = early_ref[slot // STEP]
+        if slot % STEP < len(early_refs):
+            part = early_refs[slot % STEP][slot // STEP]
         else:
             part = block_sums(potential, factors, top, slot)
         scale = jnp.where(mask_ref[slot] > 0.0, jnp.exp(jnp.minimum(top - best, 0.0)), 0.0)
@@ -189,35 +190,17 @@
     return top + jnp.log(jnp.exp(a - top) + jnp.exp(b - top))
 
 
-def swap_minor(values):
-    lane_group = lax.broadcasted_iota(jnp.int32, (TSIDE, HALF), 1) // TSIDE
-    diagonal = lane_group[:COLS_HALF] == lax.broadcasted_iota(jnp.int32, (COLS_HALF, HALF), 0)
-    result = []
-    for b in range(TSIDE):
-        start = b // COLS_HALF * HALF
-        piece = jnp.where(lane_group == b % COLS_HALF, values[:, start : start + HALF], 0.0)
-        for shift in (TSIDE, 2 * TSIDE, 4 * TSIDE):
-            piece = piece + pltpu.roll(piece, shift, 1)
-        halves = [
-            jnp.sum(jnp.where(diagonal, piece[start : start + COLS_HALF], 0.0), axis=0, keepdims=True)
-            for start in (0, COLS_HALF)
-        ]
-        result.append(halves)
-    return result
-
-
-def swap_half(values):
-    lane_group = lax.broadcasted_iota(jnp.int32, (TSIDE, HALF), 1) // TSIDE
-    diagonal = lane_group[:COLS_HALF] == lax.broadcasted_iota(jnp.int32, (COLS_HALF, HALF), 0)
-    result = ([], [])
-    for tile in range(COLS_HALF):
-        piece = jnp.where(lane_group == tile, values, 0.0)
-        for shift in (TSIDE, 2 * TSIDE, 4 * TSIDE):
-            piece = piece + pltpu.roll(piece, shift, 1)
-        for half in (0, 1):
-            part = piece[half * COLS_HALF : (half + 1) * COLS_HALF]
-            result[half].append(jnp.sum(jnp.where(diagonal, part, 0.0), axis=0, keepdims=True))
-    return jnp.concatenate(result[0] + result[1], axis=0)
+def swap_tile(values):
+    row = lax.broadcasted_iota(jnp.int32, (COLS_HALF, HALF), 0)
+    group = lax.broadcasted_iota(jnp.int32, (COLS_HALF, HALF), 1) // TSIDE
+    step = 1
+    while step < COLS_HALF:
+        from_below = pltpu.roll(pltpu.roll(values, COLS_HALF - step, 0), TSIDE * step, 1)
+        from_above = pltpu.roll(pltpu.roll(values, step, 0), HALF - TSIDE * step, 1)
+        moved = jnp.where((group & step) != 0, from_below, from_above)
+        values = jnp.where((row & step) == (group & step), values, moved)
+        step *= 2
+    return values
 
 
 def pack_kernel(*refs):
@@ -242,12 +225,14 @@
         found = found | (pairs[:, slot : slot + 1] == lanes // COLS_HALF)
     own = lax.broadcasted_iota(jnp.int32, (tiles, HALF), 0) % COLS_HALF == lanes % COLS_HALF
     marks = jnp.where(found & own, 1.0, 0.0)
-    grid_rows = swap_minor(demand_ref[...])
     is_left = lax.axis_index("tile") % 2 == 0
     tops = [jnp.sum(marks[start : start + COLS_HALF], axis=0, keepdims=True) for start in (0, COLS_HALF)]
-    sides = [jnp.concatenate([row[half] for row in grid_rows], axis=0) for half in (0, 1)]
-    message_ref[:TSIDE, :] = jnp.where(is_left, sides[0], sides[1])
-    message_ref[TSIDE + TAIL :, :] = jnp.where(is_left, sides[1], sides[0])
+    for start in (0, COLS_HALF):
+        lanes_of = slice(start // COLS_HALF * HALF, (start // COLS_HALF + 1) * HALF)
+        sides = [swap_tile(demand_ref[i : i + COLS_HALF, lanes_of]) for i in (0, COLS_HALF)]
+        message_ref[start : start + COLS_HALF, :] = jnp.where(is_left, sides[0], sides[1])
+        below = KEEP_ROWS + start
+        message_ref[below : below + COLS_HALF, :] = jnp.where(is_left, sides[1], sides[0])
     pieces = [pot_ref[:, :HALF], pot_ref[:, HALF:], cap_ref[:, :HALF], cap_ref[:, HALF:]]
     pieces += [jnp.where(is_left, tops[0], tops[1]), jnp.where(is_left, tops[1], tops[0])]
     pieces += [jnp.zeros((TAIL - ROW_MASK - 2, HALF), jnp.float32)]
@@ -267,24 +252,25 @@
     fac_ref[:, HALF:] = fac[1:2]
 
 
-def early_kernel(*refs):
-    gathered = Gathered(refs[:1])
-    factors = refs[1:4]
-    for line in range(refs[0].shape[0]):
-        slot = line * STEP
+def early_kernel(neighbor, *refs):
+    message_ref, factors, sums_ref = refs[0], refs[1:4], refs[4]
+    gathered = Gathered([message_ref] * STEP)
+    for line in range(message_ref.shape[0]):
+        slot = line * STEP + neighbor
         top = block_top(gathered.potential, factors, slot)
-        refs[4][line] = block_sums(gathered.potential, factors, top, slot)
+        sums_ref[line] = block_sums(gathered.potential, factors, top, slot)
 
 
 def first_kernel(*refs):
     gathered = Gathered(refs[:STEP])
     factors = refs[STEP : STEP + 3]
-    early_ref, part_ref, mask_ref, demand_ref, cap_ref, acc_ref = refs[STEP + 3 :]
+    early_refs = refs[STEP + 3 : STEP + 3 + EARLY]
+    part_ref, mask_ref, demand_ref, cap_ref, acc_ref = refs[STEP + 3 + EARLY :]
     build_mask(gathered, lax.axis_index("tile"), mask_ref)
     for slot in gathered.slots:
         demand_ref[:, slot, :] = gathered.demand(slot)
         cap_ref[slot : slot + 1, :] = gathered.capacity(slot)
-    base = column_base(row_pass(gathered.potential, factors, mask_ref, demand_ref, acc_ref, early_ref))
+    base = column_base(row_pass(gathered.potential, factors, mask_ref, demand_ref, acc_ref, early_refs))
     for slot in gathered.slots:
         part_ref[slot : slot + 1, :] = column_part(factors, mask_ref, base, slot)
 
@@ -312,7 +298,9 @@
     for slot, out_ref in ((0, keep_ref), (1, send_ref)):
         y_mid = ((me ^ slot) * TSIDE).astype(jnp.float32) + 0.5 * TSIDE
         lift = (dx * (dx + 2.0 * (x_mid - MIDDLE)) + dy * (dy + 2.0 * (y_mid - MIDDLE))) * SCALE
-        out_ref[:TSIDE, :] = swap_half(acc_ref[:, slot, :] + lift)
+        for start in (0, COLS_HALF):
+            rows = slice(start, start + COLS_HALF)
+            out_ref[rows, :] = swap_tile(acc_ref[rows, slot, :] + lift[rows])
         part = column_part(factors, mask_ref, base, slot)
         cap = cap_ref[slot : slot + 1, :]
         pieces = [part[:, :HALF], part[:, HALF:], cap[:, :HALF], cap[:, HALF:]]
@@ -356,12 +344,15 @@
     same = lines[:, :KEEP_ROWS]
     across = lines[:, TSIDE:]
     gathered = (lines, exchange(across, 1), exchange(same, 2), exchange(across, 3))
-    early = pl.pallas_call(
-        early_kernel,
-        out_shape=jax.ShapeDtypeStruct((slots // STEP, TSIDE, slots, HALF), jnp.float32),
-        compiler_params=heavy,
-        name="early",
-    )(lines, *factors)
+    early = [
+        pl.pallas_call(
+            lambda *refs, neighbor=neighbor: early_kernel(neighbor, *refs),
+            out_shape=jax.ShapeDtypeStruct((slots // STEP, TSIDE, slots, HALF), jnp.float32),
+            compiler_params=heavy,
+            name="early",
+        )(gathered[neighbor], *factors)
+        for neighbor in range(EARLY)
+    ]
     part, mask, demand, cap = pl.pallas_call(
         first_kernel,
         out_shape=(
@@ -373,7 +364,7 @@
         scratch_shapes=[pltpu.VMEM((TSIDE, slots, HALF), jnp.float32)],
         compiler_params=heavy,
         name="first_iteration",
-    )(*gathered, *factors, early)
+    )(*gathered, *factors, *early)
     other = exchange(part, 1)
     keep, send = pl.pallas_call(
         second_kernel,

time: 24.4 us -> 24 us (0.984)
  waiting for transfers between devices: 7.18 us -> 5.92 us
  Pallas kernels: 7.27 us -> 7.75 us
  starting transfers between devices: 8.26 us -> 8.58 us
    ppermute x8, waiting for transfers between devices: 7.18 us -> 5.92 us  [exchange(): lax.ppermute(block, 'tile', [(i, i ^ distance) for i in range(devices)])]
    pallas_call x1 -> x3, Pallas kernels: 0.52 us -> 1.56 us  [on_device_all_rows(): pl.pallas_call(lambda *refs, neighbor=neighbor: early_kernel(neighbor, *r...]
    pallas_call x1, Pallas kernels: 2.45 us -> 2 us  [on_device_all_rows(): pl.pallas_call(first_kernel, out_shape=(jax.ShapeDtypeStruct((slots, widt...]
    ppermute x8, starting transfers between devices: 8.26 us -> 8.58 us  [exchange(): lax.ppermute(block, 'tile', [(i, i ^ distance) for i in range(devices)])]
  transfers between devices with their start and end apart: 8 -> 8, of which waited for: 5 -> 4; matrix products, arithmetic and copies ran while one was open for 0% -> 0% of each run, Pallas kernels for 5% -> 10%
where the time goes in v7:
time: 24 us; the launch traced here: 23.7 us
  starting transfers between devices  8.58 us (36%)
  Pallas kernels  7.75 us (32%)
  waiting for transfers between devices  5.92 us (25%)
  local copies, waits for them, and re-layouts  0.77 us (3%)
  between operations  0.71 us (3%)
    ppermute x8, starting transfers between devices, exchange(): lax.ppermute(block, 'tile', [(i, i ^ distance) for i in range(devices)])  8.58 us
    ppermute x8, waiting for transfers between devices, exchange(): lax.ppermute(block, 'tile', [(i, i ^ distance) for i in range(devices)])  5.92 us
    pallas_call x1, Pallas kernels, on_device_all_rows(): pl.pallas_call(first_kernel, out_shape=(jax.ShapeDtypeStruct((slots, widt...  2 us
    pallas_call x1, Pallas kernels, on_device_all_rows(): pl.pallas_call(second_kernel, out_shape=(jax.ShapeDtypeStruct((KEEP_ROWS,...  1.79 us
    pallas_call x3, Pallas kernels, on_device_all_rows(): pl.pallas_call(lambda *refs, neighbor=neighbor: early_kernel(neighbor, *r...  1.56 us
    pallas_call x1, Pallas kernels, on_device_all_rows(): pl.pallas_call(pack_kernel, in_specs=[pl.BlockSpec(memory_space=pltpu.HBM...  1.03 us
    pallas_call x1, Pallas kernels, on_device_all_rows(): pl.pallas_call(lambda *refs: setup_kernel(slots, *refs), out_shape=(jax.S...  0.76 us
    unnamed x2, local copies, waits for them, and re-layouts  0.76 us
  transfers between devices with their start and end apart: 8, of which 4 were waited for; matrix products, arithmetic and copies ran while one was open for 0% of the time, Pallas kernels for 10%

profile of v7, /device:TPU:0, one launch (start us, length us, event | category | flops | bytes accessed | tf_op | source)
XLA Modules:
  0.0 23.7 jit_solution(11108527101948666234)
XLA Ops:
  0.6 1.0 %pack.1 = f32[40,128]{1,0:T(8,128)S(1)} custom-call(f32[16,256]{1,0:T(8,128)} %refs_0_.3, f32[1,256]{1,0:T(1,128)} %refs_1_.1, f32[1,256]{1,0:T(1,128)} %refs_2_.1, s32[16,16]{1,0:T(8,128)} %refs_3_.1, s32[1,16]{1,0:T(1,128)} %bitcast.6), custom_call_target="tpu_custom_call" | custom-call | tf_op jit(solution)/shard_map/pack/pallas_call | solution.py:323
  1.7 5.1 %collective-permute-start.2 = (f32[1,40,128]{2,1,0:T(8,128)S(1)}, f32[1,40,128]{2,1,0:T(8,128)S(1)}, u32[]{:S(2)}, u32[]{:S(2)}) collective-permute-start(f32[1,40,128]{2,1,0:T(8,128)S(1)} %bitcast.2), channel_id=1, source_target_pairs={{0,12},{1,13},{2,14},{3,15},{4,8},{5,9},{6,10},{7,11},{8,4},{9,5},... | collective-permute-start | bytes 61448 | tf_op jit(solution)/shard_map/ppermute | solution.py:313
  6.8 0.0 collective-permute-start.1
  6.8 0.6 %collective-permute-start = (f32[1,40,128]{2,1,0:T(8,128)S(1)}, f32[1,40,128]{2,1,0:T(8,128)S(1)}, u32[]{:S(2)}, u32[]{:S(2)}) collective-permute-start(f32[1,40,128]{2,1,0:T(8,128)S(1)} %bitcast.4), channel_id=1, source_target_pairs={{0,4},{1,5},{2,6},{3,7},{4,0},{5,1},{6,2},{7,3},{8,12},{9,13},{10,... | collective-permute-start | bytes 61448 | tf_op jit(solution)/shard_map/ppermute | solution.py:313
  7.4 1.1 %collective-permute-done.2 = f32[1,40,128]{2,1,0:T(8,128)S(1)} collective-permute-done((f32[1,40,128]{2,1,0:T(8,128)S(1)}, f32[1,40,128]{2,1,0:T(8,128)S(1)}, u32[]{:S(2)}, u32[]{:S(2)}) %collective-permute-start.2) | collective-permute-done | bytes 20512 | tf_op jit(solution)/shard_map/ppermute | solution.py:313
  8.5 2.9 %collective-permute-done.1 = f32[1,40,128]{2,1,0:T(8,128)S(1)} collective-permute-done((f32[1,40,128]{2,1,0:T(8,128)S(1)}, f32[1,40,128]{2,1,0:T(8,128)S(1)}, u32[]{:S(2)}, u32[]{:S(2)}) %collective-permute-start.1) | collective-permute-done | bytes 20512 | tf_op jit(solution)/shard_map/ppermute | solution.py:313
  11.5 0.0 collective-permute-done
  11.5 1.6 %collective-permute-start.4 = (f32[4,24,128]{2,1,0:T(8,128)S(1)}, f32[4,24,128]{2,1,0:T(8,128)S(1)}, u32[]{:S(2)}, u32[]{:S(2)}) collective-permute-start(f32[4,24,128]{2,1,0:T(8,128)S(1)} %get-tuple-element.20), channel_id=1, source_target_pairs={{0,2},{1,3},{2,0},{3,1},{4,6},{5,7},{6,4},{7,5},{8,10},{9,11},{10,... | collective-permute-start | bytes 147464 | tf_op jit(solution)/shard_map/ppermute | solution.py:313
  13.1 0.0 collective-permute-start.3
  13.1 0.6 %collective-permute-start.5 = (f32[4,24,128]{2,1,0:T(8,128)S(1)}, f32[4,24,128]{2,1,0:T(8,128)S(1)}, u32[]{:S(2)}, u32[]{:S(2)}) collective-permute-start(f32[4,24,128]{2,1,0:T(8,128)S(1)} %get-tuple-element.21), channel_id=1, source_target_pairs={{0,3},{1,2},{2,1},{3,0},{4,7},{5,6},{6,5},{7,4},{8,11},{9,10},{10,... | collective-permute-start | bytes 147464 | tf_op jit(solution)/shard_map/ppermute | solution.py:313
  13.7 0.8 %copy-done = f32[16,2,256]{2,1,0:T(2,128)S(1)} copy-done((f32[16,2,256]{2,1,0:T(2,128)S(1)}, f32[16,2,256]{2,1,0:T(2,128)}, u32[]{:S(2)}) %copy-start) | copy-done | bytes 32792
  14.5 0.8 %setup.1 = (bf16[16,256,256]{2,1,0:T(8,128)(2,1)S(1)}, f32[16,16,8,256]{3,2,1,0:T(8,128)S(1)}, f32[16,16,256]{2,1,0:T(8,128)S(1)}) custom-call(f32[16,2,256]{2,1,0:T(2,128)S(1)} %copy-done), custom_call_target="tpu_custom_call" | custom-call | tf_op jit(solution)/shard_map/setup/pallas_call | solution.py:332
  15.2 0.5 %early.3.refs_7_ = f32[4,16,16,128]{3,2,1,0:T(8,128)S(1)} custom-call(f32[4,40,128]{2,1,0:T(8,128)S(1)} %pad_maximum_fusion.refs_0_, bf16[16,256,256]{2,1,0:T(8,128)(2,1)S(1)} %get-tuple-element.11.refs_1_.refs_4_.refs_0_, f32[16,16,8,256]{3,2,1,0:T(8,128)S(1)} %get-tuple-element.12.refs_2_.refs_5_.refs_1_, ...), custom_call_target="tpu_custom_call" | custom-call | tf_op jit(solution)/shard_map/early/pallas_call | solution.py:348
  15.7 0.0 collective-permute-done.4.refs_0_.refs_2_
  15.8 0.5 %early.5.refs_9_ = f32[4,16,16,128]{3,2,1,0:T(8,128)S(1)} custom-call(f32[4,24,128]{2,1,0:T(8,128)S(1)} %collective-permute-done.4.refs_0_.refs_2_, bf16[16,256,256]{2,1,0:T(8,128)(2,1)S(1)} %get-tuple-element.11.refs_1_.refs_4_.refs_0_, f32[16,16,8,256]{3,2,1,0:T(8,128)S(1)} %get-tuple-element.12.refs_2_.refs_5_.refs_1_, ...), custom_call_target="tpu_custom_call" | custom-call | tf_op jit(solution)/shard_map/early/pallas_call | solution.py:348
  16.3 0.0 collective-permute-done.3.refs_0_.refs_1_
  16.3 0.5 %early.4.refs_8_ = f32[4,16,16,128]{3,2,1,0:T(8,128)S(1)} custom-call(f32[4,24,128]{2,1,0:T(8,128)S(1)} %collective-permute-done.3.refs_0_.refs_1_, bf16[16,256,256]{2,1,0:T(8,128)(2,1)S(1)} %get-tuple-element.11.refs_1_.refs_4_.refs_0_, f32[16,16,8,256]{3,2,1,0:T(8,128)S(1)} %get-tuple-element.12.refs_2_.refs_5_.refs_1_, ...), custom_call_target="tpu_custom_call" | custom-call | tf_op jit(solution)/shard_map/early/pallas_call | solution.py:348
  16.8 2.0 %first_iteration.1 = (f32[16,256]{1,0:T(8,128)S(1)}, f32[16,16,128]{2,1,0:T(8,128)S(1)}, f32[16,16,128]{2,1,0:T(8,128)S(1)}, f32[16,256]{1,0:T(8,128)S(1)}) custom-call(f32[4,40,128]{2,1,0:T(8,128)S(1)} %pad_maximum_fusion.refs_0_, f32[4,24,128]{2,1,0:T(8,128)S(1)} %collective-permute-done.3.refs_0_.refs_1_, ...), custom_call_target="tpu_custom_call" | custom-call | tf_op jit(solution)/shard_map/first_iteration/pallas_call | solution.py:356
  18.8 0.3 %collective-permute-start.6 = (f32[16,256]{1,0:T(8,128)S(1)}, f32[16,256]{1,0:T(8,128)S(1)}, u32[]{:S(2)}, u32[]{:S(2)}) collective-permute-start(f32[16,256]{1,0:T(8,128)S(1)} %get-tuple-element.17.refs_6_), channel_id=1, source_target_pairs={{0,1},{1,0},{2,3},{3,2},{4,5},{5,4},{6,7},{7,6},{8,9},{9,8},{10,11... | collective-permute-start | bytes 49160 | tf_op jit(solution)/shard_map/ppermute | solution.py:313
  19.1 0.9 %collective-permute-done.6.refs_7_ = f32[16,256]{1,0:T(8,128)S(1)} collective-permute-done((f32[16,256]{1,0:T(8,128)S(1)}, f32[16,256]{1,0:T(8,128)S(1)}, u32[]{:S(2)}, u32[]{:S(2)}) %collective-permute-start.6) | collective-permute-done | bytes 16416 | tf_op jit(solution)/shard_map/ppermute | solution.py:313
  20.1 1.8 %second_iteration.1 = (f32[24,128]{1,0:T(8,128)S(1)}, f32[24,128]{1,0:T(8,128)S(1)}) custom-call(bf16[16,256,256]{2,1,0:T(8,128)(2,1)S(1)} %get-tuple-element.11.refs_1_.refs_4_.refs_0_, f32[16,16,8,256]{3,2,1,0:T(8,128)S(1)} %get-tuple-element.12.refs_2_.refs_5_.refs_1_, f32[16,16,256]{2,1,0:T(8,128)S(1)} %get-tuple-element.13.refs_3_.refs_6_.refs_2_, ...), custom_call_target="tpu_custom_call" | custom-call | tf_op jit(solution)/shard_map/second_iteration/pallas_call | solution.py:369
  21.9 0.3 %collective-permute-start.7 = (f32[24,128]{1,0:T(8,128)S(1)}, f32[24,128]{1,0:T(8,128)S(1)}, u32[]{:S(2)}, u32[]{:S(2)}) collective-permute-start(f32[24,128]{1,0:T(8,128)S(1)} %get-tuple-element.19), channel_id=1, source_target_pairs={{0,1},{1,0},{2,3},{3,2},{4,5},{5,4},{6,7},{7,6},{8,9},{9,8},{10,11... | collective-permute-start | bytes 36872 | tf_op jit(solution)/shard_map/ppermute | solution.py:313
  22.2 0.9 %collective-permute-done.7.got_ref = f32[24,128]{1,0:T(8,128)S(1)} collective-permute-done((f32[24,128]{1,0:T(8,128)S(1)}, f32[24,128]{1,0:T(8,128)S(1)}, u32[]{:S(2)}, u32[]{:S(2)}) %collective-permute-start.7) | collective-permute-done | bytes 12320 | tf_op jit(solution)/shard_map/ppermute | solution.py:313
  23.1 0.6 %unpack.1 = (f32[16,256]{1,0:T(8,128)}, f32[1,256]{1,0:T(1,128)}) custom-call(f32[24,128]{1,0:T(8,128)S(1)} %get-tuple-element.18.keep_ref, f32[24,128]{1,0:T(8,128)S(1)} %collective-permute-done.7.got_ref), custom_call_target="tpu_custom_call" | custom-call | tf_op jit(solution)/shard_map/unpack/pallas_call | solution.py:383
  (4 shorter events, 0.0 us)
Async XLA Ops:
  1.7 6.9 %collective-permute-start.2 = (f32[1,40,128]{2,1,0:T(8,128)S(1)}, f32[1,40,128]{2,1,0:T(8,128)S(1)}, u32[]{:S(2)}, u32[]{:S(2)}) collective-permute-start(f32[1,40,128]{2,1,0:T(8,128)S(1)} %bitcast.2), channel_id=1, source_target_pairs={{0,12},{1,13},{2,14},{3,15},{4,8},{5,9},{6,10},{7,11},{8,4},{9,5},... | collective-permute-start | bytes 61448 | tf_op jit(solution)/shard_map/ppermute | solution.py:313
  6.8 4.7 %collective-permute-start.1 = (f32[1,40,128]{2,1,0:T(8,128)S(1)}, f32[1,40,128]{2,1,0:T(8,128)S(1)}, u32[]{:S(2)}, u32[]{:S(2)}) collective-permute-start(f32[1,40,128]{2,1,0:T(8,128)S(1)} %bitcast.3), channel_id=1, source_target_pairs={{0,8},{1,9},{2,10},{3,11},{4,12},{5,13},{6,14},{7,15},{8,0},{9,1},... | collective-permute-start | bytes 61448 | tf_op jit(solution)/shard_map/ppermute | solution.py:313
  6.8 4.7 %collective-permute-start = (f32[1,40,128]{2,1,0:T(8,128)S(1)}, f32[1,40,128]{2,1,0:T(8,128)S(1)}, u32[]{:S(2)}, u32[]{:S(2)}) collective-permute-start(f32[1,40,128]{2,1,0:T(8,128)S(1)} %bitcast.4), channel_id=1, source_target_pairs={{0,4},{1,5},{2,6},{3,7},{4,0},{5,1},{6,2},{7,3},{8,12},{9,13},{10,... | collective-permute-start | bytes 61448 | tf_op jit(solution)/shard_map/ppermute | solution.py:313
  11.5 4.3 %collective-permute-start.4 = (f32[4,24,128]{2,1,0:T(8,128)S(1)}, f32[4,24,128]{2,1,0:T(8,128)S(1)}, u32[]{:S(2)}, u32[]{:S(2)}) collective-permute-start(f32[4,24,128]{2,1,0:T(8,128)S(1)} %get-tuple-element.20), channel_id=1, source_target_pairs={{0,2},{1,3},{2,0},{3,1},{4,6},{5,7},{6,4},{7,5},{8,10},{9,11},{10,... | collective-permute-start | bytes 147464 | tf_op jit(solution)/shard_map/ppermute | solution.py:313
  13.1 3.2 %collective-permute-start.3 = (f32[4,24,128]{2,1,0:T(8,128)S(1)}, f32[4,24,128]{2,1,0:T(8,128)S(1)}, u32[]{:S(2)}, u32[]{:S(2)}) collective-permute-start(f32[4,24,128]{2,1,0:T(8,128)S(1)} %get-tuple-element.21), channel_id=1, source_target_pairs={{0,1},{1,0},{2,3},{3,2},{4,5},{5,4},{6,7},{7,6},{8,9},{9,8},{10,11... | collective-permute-start | bytes 147464 | tf_op jit(solution)/shard_map/ppermute | solution.py:313
  13.1 3.8 %collective-permute-start.5 = (f32[4,24,128]{2,1,0:T(8,128)S(1)}, f32[4,24,128]{2,1,0:T(8,128)S(1)}, u32[]{:S(2)}, u32[]{:S(2)}) collective-permute-start(f32[4,24,128]{2,1,0:T(8,128)S(1)} %get-tuple-element.21), channel_id=1, source_target_pairs={{0,3},{1,2},{2,1},{3,0},{4,7},{5,6},{6,5},{7,4},{8,11},{9,10},{10,... | collective-permute-start | bytes 147464 | tf_op jit(solution)/shard_map/ppermute | solution.py:313
  13.7 0.8 %copy-start = (f32[16,2,256]{2,1,0:T(2,128)S(1)}, f32[16,2,256]{2,1,0:T(2,128)}, u32[]{:S(2)}) copy-start(f32[16,2,256]{2,1,0:T(2,128)} %refs_0_.2) | copy-start | bytes 98308
  18.8 1.2 %collective-permute-start.6 = (f32[16,256]{1,0:T(8,128)S(1)}, f32[16,256]{1,0:T(8,128)S(1)}, u32[]{:S(2)}, u32[]{:S(2)}) collective-permute-start(f32[16,256]{1,0:T(8,128)S(1)} %get-tuple-element.17.refs_6_), channel_id=1, source_target_pairs={{0,1},{1,0},{2,3},{3,2},{4,5},{5,4},{6,7},{7,6},{8,9},{9,8},{10,11... | collective-permute-start | bytes 49160 | tf_op jit(solution)/shard_map/ppermute | solution.py:313
  21.9 1.2 %collective-permute-start.7 = (f32[24,128]{1,0:T(8,128)S(1)}, f32[24,128]{1,0:T(8,128)S(1)}, u32[]{:S(2)}, u32[]{:S(2)}) collective-permute-start(f32[24,128]{1,0:T(8,128)S(1)} %get-tuple-element.19), channel_id=1, source_target_pairs={{0,1},{1,0},{2,3},{3,2},{4,5},{5,4},{6,7},{7,6},{8,9},{9,8},{10,11... | collective-permute-start | bytes 36872 | tf_op jit(solution)/shard_map/ppermute | solution.py:313

commit v8 on v7

--- a/solution.py
+++ b/solution.py
@@ -26,6 +26,7 @@
 ROW_CAP = 2
 ROW_MASK = 4
 STEP = 4
+PLACES = (0, 1, 3, 2)
 EARLY = 3
 SUBLANES = 8
 LOG2E = 1.4426950408889634
@@ -56,7 +57,7 @@
         self.slots = range(len(refs) * refs[0].shape[0])
 
     def block_of(self, slot, first, rows):
-        return self.refs[slot % STEP][slot // STEP, first : first + rows, :]
+        return self.refs[slot % STEP][PLACES.index(slot // STEP), first : first + rows, :]
 
     def demand(self, slot):
         return self.block_of(slot, TAIL if slot % 2 else 0, TSIDE)
@@ -340,7 +341,7 @@
         name="setup",
     )(facility_xy)
     lines = message[None]
-    lines = jnp.concatenate([lines] + [exchange(lines, STEP * i) for i in range(1, slots // STEP)], axis=0)
+    lines = jnp.concatenate([lines] + [exchange(lines, STEP * i) for i in PLACES[1:]], axis=0)
     same = lines[:, :KEEP_ROWS]
     across = lines[:, TSIDE:]
     gathered = (lines, exchange(across, 1), exchange(same, 2), exchange(across, 3))

time: 24 us -> 23.9 us (level)
  no operation moved by 1% of the time
where the time goes in v8:
time: 23.9 us; the launch traced here: 23.6 us
  starting transfers between devices  8.53 us (36%)
  Pallas kernels  7.74 us (32%)
  waiting for transfers between devices  5.86 us (25%)
  local copies, waits for them, and re-layouts  0.77 us (3%)
  between operations  0.71 us (3%)
    ppermute x8, starting transfers between devices, exchange(): lax.ppermute(block, 'tile', [(i, i ^ distance) for i in range(devices)])  8.53 us
    ppermute x8, waiting for transfers between devices, exchange(): lax.ppermute(block, 'tile', [(i, i ^ distance) for i in range(devices)])  5.86 us
    pallas_call x1, Pallas kernels, on_device_all_rows(): pl.pallas_call(first_kernel, out_shape=(jax.ShapeDtypeStruct((slots, widt...  2 us
    pallas_call x1, Pallas kernels, on_device_all_rows(): pl.pallas_call(second_kernel, out_shape=(jax.ShapeDtypeStruct((KEEP_ROWS,...  1.79 us
    pallas_call x3, Pallas kernels, on_device_all_rows(): pl.pallas_call(lambda *refs, neighbor=neighbor: early_kernel(neighbor, *r...  1.55 us
    pallas_call x1, Pallas kernels, on_device_all_rows(): pl.pallas_call(pack_kernel, in_specs=[pl.BlockSpec(memory_space=pltpu.HBM...  1.03 us
    pallas_call x1, Pallas kernels, on_device_all_rows(): pl.pallas_call(lambda *refs: setup_kernel(slots, *refs), out_shape=(jax.S...  0.76 us
    unnamed x2, local copies, waits for them, and re-layouts  0.76 us
  transfers between devices with their start and end apart: 8, of which 4 were waited for; matrix products, arithmetic and copies ran while one was open for 0% of the time, Pallas kernels for 10%

profile of v8, /device:TPU:0, one launch (start us, length us, event | category | flops | bytes accessed | tf_op | source)
XLA Modules:
  0.0 23.6 jit_solution(8596269867185323671)
XLA Ops:
  0.6 1.0 %pack.1 = f32[40,128]{1,0:T(8,128)S(1)} custom-call(f32[16,256]{1,0:T(8,128)} %refs_0_.3, f32[1,256]{1,0:T(1,128)} %refs_1_.1, f32[1,256]{1,0:T(1,128)} %refs_2_.1, s32[16,16]{1,0:T(8,128)} %refs_3_.1, s32[1,16]{1,0:T(1,128)} %bitcast.6), custom_call_target="tpu_custom_call" | custom-call | tf_op jit(solution)/shard_map/pack/pallas_call | solution.py:324
  1.7 4.1 %collective-permute-start.2 = (f32[1,40,128]{2,1,0:T(8,128)S(1)}, f32[1,40,128]{2,1,0:T(8,128)S(1)}, u32[]{:S(2)}, u32[]{:S(2)}) collective-permute-start(f32[1,40,128]{2,1,0:T(8,128)S(1)} %bitcast.2), channel_id=1, source_target_pairs={{0,8},{1,9},{2,10},{3,11},{4,12},{5,13},{6,14},{7,15},{8,0},{9,1},... | collective-permute-start | bytes 61448 | tf_op jit(solution)/shard_map/ppermute | solution.py:314
  5.8 1.3 %collective-permute-start.1 = (f32[1,40,128]{2,1,0:T(8,128)S(1)}, f32[1,40,128]{2,1,0:T(8,128)S(1)}, u32[]{:S(2)}, u32[]{:S(2)}) collective-permute-start(f32[1,40,128]{2,1,0:T(8,128)S(1)} %bitcast.3), channel_id=1, source_target_pairs={{0,12},{1,13},{2,14},{3,15},{4,8},{5,9},{6,10},{7,11},{8,4},{9,5},... | collective-permute-start | bytes 61448 | tf_op jit(solution)/shard_map/ppermute | solution.py:314
  7.1 0.2 collective-permute-start
  7.3 0.2 collective-permute-done.2
  7.5 3.8 %collective-permute-done.1 = f32[1,40,128]{2,1,0:T(8,128)S(1)} collective-permute-done((f32[1,40,128]{2,1,0:T(8,128)S(1)}, f32[1,40,128]{2,1,0:T(8,128)S(1)}, u32[]{:S(2)}, u32[]{:S(2)}) %collective-permute-start.1) | collective-permute-done | bytes 20512 | tf_op jit(solution)/shard_map/ppermute | solution.py:314
  11.3 0.0 collective-permute-done
  11.4 1.6 %collective-permute-start.4 = (f32[4,24,128]{2,1,0:T(8,128)S(1)}, f32[4,24,128]{2,1,0:T(8,128)S(1)}, u32[]{:S(2)}, u32[]{:S(2)}) collective-permute-start(f32[4,24,128]{2,1,0:T(8,128)S(1)} %get-tuple-element.20), channel_id=1, source_target_pairs={{0,2},{1,3},{2,0},{3,1},{4,6},{5,7},{6,4},{7,5},{8,10},{9,11},{10,... | collective-permute-start | bytes 147464 | tf_op jit(solution)/shard_map/ppermute | solution.py:314
  12.9 0.0 collective-permute-start.3
  12.9 0.6 %collective-permute-start.5 = (f32[4,24,128]{2,1,0:T(8,128)S(1)}, f32[4,24,128]{2,1,0:T(8,128)S(1)}, u32[]{:S(2)}, u32[]{:S(2)}) collective-permute-start(f32[4,24,128]{2,1,0:T(8,128)S(1)} %get-tuple-element.21), channel_id=1, source_target_pairs={{0,3},{1,2},{2,1},{3,0},{4,7},{5,6},{6,5},{7,4},{8,11},{9,10},{10,... | collective-permute-start | bytes 147464 | tf_op jit(solution)/shard_map/ppermute | solution.py:314
  13.6 0.8 %copy-done = f32[16,2,256]{2,1,0:T(2,128)S(1)} copy-done((f32[16,2,256]{2,1,0:T(2,128)S(1)}, f32[16,2,256]{2,1,0:T(2,128)}, u32[]{:S(2)}) %copy-start) | copy-done | bytes 32792
  14.3 0.8 %setup.1 = (bf16[16,256,256]{2,1,0:T(8,128)(2,1)S(1)}, f32[16,16,8,256]{3,2,1,0:T(8,128)S(1)}, f32[16,16,256]{2,1,0:T(8,128)S(1)}) custom-call(f32[16,2,256]{2,1,0:T(2,128)S(1)} %copy-done), custom_call_target="tpu_custom_call" | custom-call | tf_op jit(solution)/shard_map/setup/pallas_call | solution.py:333
  15.1 0.5 %early.3.refs_7_ = f32[4,16,16,128]{3,2,1,0:T(8,128)S(1)} custom-call(f32[4,40,128]{2,1,0:T(8,128)S(1)} %pad_maximum_fusion.refs_0_, bf16[16,256,256]{2,1,0:T(8,128)(2,1)S(1)} %get-tuple-element.11.refs_1_.refs_4_.refs_0_, f32[16,16,8,256]{3,2,1,0:T(8,128)S(1)} %get-tuple-element.12.refs_2_.refs_5_.refs_1_, ...), custom_call_target="tpu_custom_call" | custom-call | tf_op jit(solution)/shard_map/early/pallas_call | solution.py:349
  15.6 0.5 %early.5.refs_9_ = f32[4,16,16,128]{3,2,1,0:T(8,128)S(1)} custom-call(f32[4,24,128]{2,1,0:T(8,128)S(1)} %collective-permute-done.4.refs_0_.refs_2_, bf16[16,256,256]{2,1,0:T(8,128)(2,1)S(1)} %get-tuple-element.11.refs_1_.refs_4_.refs_0_, f32[16,16,8,256]{3,2,1,0:T(8,128)S(1)} %get-tuple-element.12.refs_2_.refs_5_.refs_1_, ...), custom_call_target="tpu_custom_call" | custom-call | tf_op jit(solution)/shard_map/early/pallas_call | solution.py:349
  16.2 0.0 collective-permute-done.3.refs_0_.refs_1_
  16.2 0.5 %early.4.refs_8_ = f32[4,16,16,128]{3,2,1,0:T(8,128)S(1)} custom-call(f32[4,24,128]{2,1,0:T(8,128)S(1)} %collective-permute-done.3.refs_0_.refs_1_, bf16[16,256,256]{2,1,0:T(8,128)(2,1)S(1)} %get-tuple-element.11.refs_1_.refs_4_.refs_0_, f32[16,16,8,256]{3,2,1,0:T(8,128)S(1)} %get-tuple-element.12.refs_2_.refs_5_.refs_1_, ...), custom_call_target="tpu_custom_call" | custom-call | tf_op jit(solution)/shard_map/early/pallas_call | solution.py:349
  16.7 0.0 collective-permute-done.5.refs_3_
  16.7 2.0 %first_iteration.1 = (f32[16,256]{1,0:T(8,128)S(1)}, f32[16,16,128]{2,1,0:T(8,128)S(1)}, f32[16,16,128]{2,1,0:T(8,128)S(1)}, f32[16,256]{1,0:T(8,128)S(1)}) custom-call(f32[4,40,128]{2,1,0:T(8,128)S(1)} %pad_maximum_fusion.refs_0_, f32[4,24,128]{2,1,0:T(8,128)S(1)} %collective-permute-done.3.refs_0_.refs_1_, ...), custom_call_target="tpu_custom_call" | custom-call | tf_op jit(solution)/shard_map/first_iteration/pallas_call | solution.py:357
  18.7 0.3 %collective-permute-start.6 = (f32[16,256]{1,0:T(8,128)S(1)}, f32[16,256]{1,0:T(8,128)S(1)}, u32[]{:S(2)}, u32[]{:S(2)}) collective-permute-start(f32[16,256]{1,0:T(8,128)S(1)} %get-tuple-element.17.refs_6_), channel_id=1, source_target_pairs={{0,1},{1,0},{2,3},{3,2},{4,5},{5,4},{6,7},{7,6},{8,9},{9,8},{10,11... | collective-permute-start | bytes 49160 | tf_op jit(solution)/shard_map/ppermute | solution.py:314
  19.0 0.9 %collective-permute-done.6.refs_7_ = f32[16,256]{1,0:T(8,128)S(1)} collective-permute-done((f32[16,256]{1,0:T(8,128)S(1)}, f32[16,256]{1,0:T(8,128)S(1)}, u32[]{:S(2)}, u32[]{:S(2)}) %collective-permute-start.6) | collective-permute-done | bytes 16416 | tf_op jit(solution)/shard_map/ppermute | solution.py:314
  20.0 1.8 %second_iteration.1 = (f32[24,128]{1,0:T(8,128)S(1)}, f32[24,128]{1,0:T(8,128)S(1)}) custom-call(bf16[16,256,256]{2,1,0:T(8,128)(2,1)S(1)} %get-tuple-element.11.refs_1_.refs_4_.refs_0_, f32[16,16,8,256]{3,2,1,0:T(8,128)S(1)} %get-tuple-element.12.refs_2_.refs_5_.refs_1_, f32[16,16,256]{2,1,0:T(8,128)S(1)} %get-tuple-element.13.refs_3_.refs_6_.refs_2_, ...), custom_call_target="tpu_custom_call" | custom-call | tf_op jit(solution)/shard_map/second_iteration/pallas_call | solution.py:370
  21.7 0.3 %collective-permute-start.7 = (f32[24,128]{1,0:T(8,128)S(1)}, f32[24,128]{1,0:T(8,128)S(1)}, u32[]{:S(2)}, u32[]{:S(2)}) collective-permute-start(f32[24,128]{1,0:T(8,128)S(1)} %get-tuple-element.19), channel_id=1, source_target_pairs={{0,1},{1,0},{2,3},{3,2},{4,5},{5,4},{6,7},{7,6},{8,9},{9,8},{10,11... | collective-permute-start | bytes 36872 | tf_op jit(solution)/shard_map/ppermute | solution.py:314
  22.1 0.9 %collective-permute-done.7.got_ref = f32[24,128]{1,0:T(8,128)S(1)} collective-permute-done((f32[24,128]{1,0:T(8,128)S(1)}, f32[24,128]{1,0:T(8,128)S(1)}, u32[]{:S(2)}, u32[]{:S(2)}) %collective-permute-start.7) | collective-permute-done | bytes 12320 | tf_op jit(solution)/shard_map/ppermute | solution.py:314
  23.0 0.6 %unpack.1 = (f32[16,256]{1,0:T(8,128)}, f32[1,256]{1,0:T(1,128)}) custom-call(f32[24,128]{1,0:T(8,128)S(1)} %get-tuple-element.18.keep_ref, f32[24,128]{1,0:T(8,128)S(1)} %collective-permute-done.7.got_ref), custom_call_target="tpu_custom_call" | custom-call | tf_op jit(solution)/shard_map/unpack/pallas_call | solution.py:384
  (4 shorter events, 0.0 us)
Async XLA Ops:
  1.7 5.9 %collective-permute-start.2 = (f32[1,40,128]{2,1,0:T(8,128)S(1)}, f32[1,40,128]{2,1,0:T(8,128)S(1)}, u32[]{:S(2)}, u32[]{:S(2)}) collective-permute-start(f32[1,40,128]{2,1,0:T(8,128)S(1)} %bitcast.2), channel_id=1, source_target_pairs={{0,8},{1,9},{2,10},{3,11},{4,12},{5,13},{6,14},{7,15},{8,0},{9,1},... | collective-permute-start | bytes 61448 | tf_op jit(solution)/shard_map/ppermute | solution.py:314
  5.8 5.6 %collective-permute-start.1 = (f32[1,40,128]{2,1,0:T(8,128)S(1)}, f32[1,40,128]{2,1,0:T(8,128)S(1)}, u32[]{:S(2)}, u32[]{:S(2)}) collective-permute-start(f32[1,40,128]{2,1,0:T(8,128)S(1)} %bitcast.3), channel_id=1, source_target_pairs={{0,12},{1,13},{2,14},{3,15},{4,8},{5,9},{6,10},{7,11},{8,4},{9,5},... | collective-permute-start | bytes 61448 | tf_op jit(solution)/shard_map/ppermute | solution.py:314
  7.1 4.2 %collective-permute-start = (f32[1,40,128]{2,1,0:T(8,128)S(1)}, f32[1,40,128]{2,1,0:T(8,128)S(1)}, u32[]{:S(2)}, u32[]{:S(2)}) collective-permute-start(f32[1,40,128]{2,1,0:T(8,128)S(1)} %bitcast.4), channel_id=1, source_target_pairs={{0,4},{1,5},{2,6},{3,7},{4,0},{5,1},{6,2},{7,3},{8,12},{9,13},{10,... | collective-permute-start | bytes 61448 | tf_op jit(solution)/shard_map/ppermute | solution.py:314
  11.4 4.3 %collective-permute-start.4 = (f32[4,24,128]{2,1,0:T(8,128)S(1)}, f32[4,24,128]{2,1,0:T(8,128)S(1)}, u32[]{:S(2)}, u32[]{:S(2)}) collective-permute-start(f32[4,24,128]{2,1,0:T(8,128)S(1)} %get-tuple-element.20), channel_id=1, source_target_pairs={{0,2},{1,3},{2,0},{3,1},{4,6},{5,7},{6,4},{7,5},{8,10},{9,11},{10,... | collective-permute-start | bytes 147464 | tf_op jit(solution)/shard_map/ppermute | solution.py:314
  12.9 3.2 %collective-permute-start.3 = (f32[4,24,128]{2,1,0:T(8,128)S(1)}, f32[4,24,128]{2,1,0:T(8,128)S(1)}, u32[]{:S(2)}, u32[]{:S(2)}) collective-permute-start(f32[4,24,128]{2,1,0:T(8,128)S(1)} %get-tuple-element.21), channel_id=1, source_target_pairs={{0,1},{1,0},{2,3},{3,2},{4,5},{5,4},{6,7},{7,6},{8,9},{9,8},{10,11... | collective-permute-start | bytes 147464 | tf_op jit(solution)/shard_map/ppermute | solution.py:314
  12.9 3.8 %collective-permute-start.5 = (f32[4,24,128]{2,1,0:T(8,128)S(1)}, f32[4,24,128]{2,1,0:T(8,128)S(1)}, u32[]{:S(2)}, u32[]{:S(2)}) collective-permute-start(f32[4,24,128]{2,1,0:T(8,128)S(1)} %get-tuple-element.21), channel_id=1, source_target_pairs={{0,3},{1,2},{2,1},{3,0},{4,7},{5,6},{6,5},{7,4},{8,11},{9,10},{10,... | collective-permute-start | bytes 147464 | tf_op jit(solution)/shard_map/ppermute | solution.py:314
  13.6 0.8 %copy-start = (f32[16,2,256]{2,1,0:T(2,128)S(1)}, f32[16,2,256]{2,1,0:T(2,128)}, u32[]{:S(2)}) copy-start(f32[16,2,256]{2,1,0:T(2,128)} %refs_0_.2) | copy-start | bytes 98308
  18.7 1.2 %collective-permute-start.6 = (f32[16,256]{1,0:T(8,128)S(1)}, f32[16,256]{1,0:T(8,128)S(1)}, u32[]{:S(2)}, u32[]{:S(2)}) collective-permute-start(f32[16,256]{1,0:T(8,128)S(1)} %get-tuple-element.17.refs_6_), channel_id=1, source_target_pairs={{0,1},{1,0},{2,3},{3,2},{4,5},{5,4},{6,7},{7,6},{8,9},{9,8},{10,11... | collective-permute-start | bytes 49160 | tf_op jit(solution)/shard_map/ppermute | solution.py:314
  21.7 1.2 %collective-permute-start.7 = (f32[24,128]{1,0:T(8,128)S(1)}, f32[24,128]{1,0:T(8,128)S(1)}, u32[]{:S(2)}, u32[]{:S(2)}) collective-permute-start(f32[24,128]{1,0:T(8,128)S(1)} %get-tuple-element.19), channel_id=1, source_target_pairs={{0,1},{1,0},{2,3},{3,2},{4,5},{5,4},{6,7},{7,6},{8,9},{9,8},{10,11... | collective-permute-start | bytes 36872 | tf_op jit(solution)/shard_map/ppermute | solution.py:314
